TPU v7x, 512 devices: a whole 4x8x8 slice. The times are simulated.
512 devices in a mesh: snap: 8 (over y_hi, x), lat: 64 (over y_lo, z, core).
Axes of the slice: x: 4, y: 8 (y_hi: 2, y_lo: 4; y = y_hi * 4 + y_lo), z: 8, core: 2. Of those that a mesh axis runs over, the one named last changes fastest.
Arguments:
- activations: bfloat16 [8, 640, 1536], P('snap', 'lat'), may hold values from -6 to 6
- enc_weight: bfloat16 [8, 1536, 8192], P('snap', None, 'lat'), may hold values from -0.0546875 to 0.0546875
- enc_bias: float32 [8192], P('lat'), may hold values from -3 to 3
- dec_weight: bfloat16 [8192, 8, 1536], P('lat', 'snap'), may hold values from -0.125 to 0.125
- dec_bias: float32 [8, 1536], P('snap'), may hold values from -3 to 3
- dec_first: float32 [8192, 8, 1536], P('lat', 'snap'), may hold values from -0.3 to 0.3
- dec_second: float32 [8192, 8, 1536], P('lat', 'snap'), may hold values from 0.05 to 2
Outputs:
- enc_grad: bfloat16 [8, 1536, 8192], P('snap', None, 'lat')
- new_decoder: float32 [8192, 8, 1536], P('lat', 'snap')
- new_first: float32 [8192, 8, 1536], P('lat', 'snap')
- new_second: float32 [8192, 8, 1536], P('lat', 'snap')
All inputs are finite; a program needn't handle non-finite values.
Results may differ from a plain program's by a relative error of at most 0.01.
Values may be sent and summed in bfloat16 or wider, within the bound.
No kernel may reach another device: no remote copies, remote signals or barrier semaphores. Data moves between devices by JAX's collectives and lax.ppermute only.
A program may use at most 64 MiB of HBM per device.

v0:
```python
import jax
import jax.numpy as jnp
from jax import lax
from jax.sharding import PartitionSpec as P

sparsity_weight = 1.0
learn_rate = 0.001
beta_first = 0.9
beta_second = 0.999
corr_first = 0.6513215599
corr_second = 0.0099551198
adam_epsilon = 1e-08
norm_epsilon = 1e-06


def contract_lead(left, right):
    return lax.dot_general(
        left, right, (((0,), (0,)), ((), ())), preferred_element_type=jnp.float32
    )


def contract_last(left, right):
    return lax.dot_general(
        left, right, (((1,), (1,)), ((), ())), preferred_element_type=jnp.float32
    )


def body(activations, enc_weight, enc_bias, dec_weight, dec_bias, dec_first, dec_second):
    local_rows = activations[0]
    enc_local = enc_weight[0]
    dec_local = dec_weight[:, 0, :]
    lat_count = lax.axis_size("lat")
    rows_dev = local_rows.shape[0]
    batch_rows = rows_dev * lat_count
    scale_rec = 2.0 / batch_rows
    scale_sparse = sparsity_weight / batch_rows
    gathered = lax.all_gather(local_rows, "lat", axis=0, tiled=True)
    partial_pre = jnp.dot(gathered, enc_local, preferred_element_type=jnp.float32)
    dec_float = dec_local.astype(jnp.float32)
    own_norm = jnp.sqrt(jnp.sum(dec_float * dec_float, axis=1) + norm_epsilon)
    pre_sum, norm_total = lax.psum((partial_pre, own_norm), "snap")
    preact = pre_sum + enc_bias[None, :]
    active = jnp.maximum(preact, 0.0)
    codes = active.astype(jnp.bfloat16)
    code_total = jnp.sum(active, axis=0)
    part_codes = codes
    decoded = lax.psum_scatter(
        jnp.dot(part_codes, dec_local, preferred_element_type=jnp.float32),
        "lat",
        scatter_dimension=0,
        tiled=True,
    )
    errors = (decoded + dec_bias[0][None, :] - local_rows.astype(jnp.float32)).astype(jnp.bfloat16)
    incoming = lax.all_gather(errors, "lat", axis=0, tiled=True)
    product = contract_last(incoming, dec_local)
    part_codes = codes
    dec_acc = contract_lead(part_codes, incoming)
    grad_sum = lax.psum(product, "snap")
    grad_code = scale_rec * grad_sum + scale_sparse * norm_total[None, :]
    grad_pre = jnp.where(preact > 0.0, grad_code, 0.0).astype(jnp.bfloat16)
    enc_term = contract_lead(gathered, grad_pre)
    enc_grad = enc_term.astype(jnp.bfloat16)[None]
    dec_grad = (
        scale_rec * dec_acc + scale_sparse * code_total[:, None] * dec_float / own_norm[:, None]
    )
    dec_grad = dec_grad[:, None, :]
    new_first = beta_first * dec_first + (1.0 - beta_first) * dec_grad
    new_second = beta_second * dec_second + (1.0 - beta_second) * dec_grad * dec_grad
    new_decoder = dec_float[:, None, :] - learn_rate * (new_first / corr_first) / (
        jnp.sqrt(new_second / corr_second) + adam_epsilon
    )
    return (enc_grad, new_decoder, new_first, new_second)


def solution(mesh):
    in_specs = (
        P("snap", "lat", None),
        P("snap", None, "lat"),
        P("lat"),
        P("lat", "snap", None),
        P("snap", None),
        P("lat", "snap", None),
        P("lat", "snap", None),
    )
    out_specs = (
        P("snap", None, "lat"),
        P("lat", "snap", None),
        P("lat", "snap", None),
        P("lat", "snap", None),
    )
    return jax.shard_map(body, mesh=mesh, in_specs=in_specs, out_specs=out_specs, check_vma=False)
```

profile of v0, /device:TPU:64, one launch (start us, length us, event | category | flops | bytes accessed | tf_op | source)
XLA Modules:
  0.0 1039.3 jit_solution(4481834609784938482)
XLA Ops:
  7.2 0.0 copy-start
  7.2 0.0 copy-start.1
  7.2 0.0 copy-start.5
  7.2 0.0 all-gather.5.cloned.1.call-start
  7.2 1.5 copy.30
  8.8 0.0 all-gather.5.cloned.1.call-update
  8.8 0.0 all-reduce.5.cloned.1.call-start
  8.9 124.2 %all-gather.5.cloned.1.call-done = bf16[1,640,1536]{2,0,1:T(2,128)(2,1)} async-done(((bf16[1,10,1536]{2,0,1:T(2,128)(2,1)}), bf16[1,640,1536]{2,0,1:T(2,128)(2,1)}) %all-gather.5.cloned.1.call-update) | async-done | bytes 1966096 | tf_op jit(solution)/shard_map/all_gather | solution.py:37
  133.1 0.0 copy-done
  133.1 3.5 fusion.3
  136.6 0.0 all-reduce.5.cloned.1.call-update
  136.6 0.0 all-reduce.9.cloned.1.call-start
  136.7 112.3 %all-reduce.5.cloned.1.call-done = f32[640,128]{1,0:T(8,128)} async-done(((f32[640,128]{1,0:T(8,128)}), f32[640,128]{1,0:T(8,128)}) %all-reduce.5.cloned.1.call-update) | async-done | bytes 327696 | tf_op jit(solution)/shard_map/psum | solution.py:41
  249.0 0.0 copy-done.1
  249.0 0.0 copy-done.5
  249.0 3.6 fusion.13
  252.6 0.0 copy-start.4
  252.6 0.0 copy-start.3
  252.6 0.0 copy-start.2
  252.6 0.0 all-reduce.9.cloned.1.call-update
  252.6 0.0 all-gather.7.cloned.1.call-start
  252.7 1.3 dynamic-slice
  254.7 0.0 copy-done.4
  254.7 540.1 %all-reduce.9.cloned.1.call-done = f32[640,1536]{1,0:T(8,128)} async-done(((f32[640,1536]{1,0:T(8,128)}), f32[640,1536]{1,0:T(8,128)}) %all-reduce.9.cloned.1.call-update) | async-done | bytes 3932176
  794.8 0.0 copy-done.3
  794.8 1.6 fusion.21
  796.3 0.0 all-gather.7.cloned.1.call-update
  796.4 0.0 all-reduce.7.cloned.1.call-start
  796.4 0.2 fusion.5
  796.6 28.8 %psum.23 = f32[128]{0:T(128)S(1)} all-reduce(f32[128]{0:T(128)S(1)} %add_sqrt_fusion), channel_id=1, replica_groups=mesh['snap'=8,'lat'=64] {'snap'}, use_global_device_ids=true, to_apply=%region_4.0 | all-reduce | flops 128 | bytes 1024 | tf_op jit(solution)/shard_map/psum | solution.py:41
  825.3 0.0 copy-done.2
  825.3 0.1 maximum_reduce_fusion
  825.5 87.0 %all-gather.7.cloned.1.call-done = bf16[64,10,1536]{2,1,0:T(8,128)(2,1)} async-done(((bf16[1,10,1536]{2,1,0:T(8,128)(2,1)}), bf16[64,10,1536]{2,1,0:T(8,128)(2,1)}) %all-gather.7.cloned.1.call-update) | async-done | bytes 1966096 | tf_op jit(solution)/shard_map/all_gather | solution.py:54
  912.4 2.9 reshape.25
  915.3 1.4 fusion.11
  916.7 0.0 all-reduce.7.cloned.1.call-update
  916.7 2.5 divide_subtract_fusion
  919.2 1.7 copy.34
  920.9 1.7 copy.35
  922.6 1.7 copy.36
  924.3 104.8 %all-reduce.7.cloned.1.call-done = f32[640,128]{1,0:T(8,128)} async-done(((f32[640,128]{1,0:T(8,128)}), f32[640,128]{1,0:T(8,128)}) %all-reduce.7.cloned.1.call-update) | async-done | bytes 327696 | tf_op jit(solution)/shard_map/psum | solution.py:58
  1029.1 2.7 fusion.1
  1031.8 0.9 copy.33
  (4 shorter events, 0.0 us)
Async XLA Ops:
  7.2 125.9 %copy-start = (bf16[1,1536,128]{2,1,0:T(8,128)(2,1)S(1)}, bf16[1,1536,128]{2,1,0:T(8,128)(2,1)}, u32[]{:S(2)}) copy-start(bf16[1,1536,128]{2,1,0:T(8,128)(2,1)} %param.8) | copy-start | bytes 1179652
  7.2 241.8 %copy-start.1 = (bf16[128,1,1536]{2,0,1:T(8,128)(2,1)S(1)}, bf16[128,1,1536]{2,0,1:T(8,128)(2,1)}, u32[]{:S(2)}) copy-start(bf16[128,1,1536]{2,0,1:T(8,128)(2,1)} %param.10) | copy-start | bytes 1179652
  7.2 241.8 %copy-start.5 = (f32[128]{0:T(128)S(1)}, f32[128]{0:T(128)}, u32[]{:S(2)}) copy-start(f32[128]{0:T(128)} %param.9) | copy-start | bytes 1540
  7.2 125.9 %all-gather.5.cloned.1.call-start = ((), (), s32[]{:S(2)}) async-start(), calls=%async_computation.2 | async-start | bytes 3993600 | tf_op jit(solution)/shard_map/all_gather | solution.py:37
  8.8 240.2 %all-reduce.5.cloned.1.call-start = ((), (), s32[]{:S(2)}) async-start(), calls=%async_computation | async-start | bytes 655360 | tf_op jit(solution)/shard_map/psum | solution.py:41
  136.6 658.1 %all-reduce.9.cloned.1.call-start = ((), (), s32[]{:S(2)}) async-start(), calls=%async_computation.4 | async-start | bytes 7864320
  252.6 2.1 copy-start.4
  252.6 542.2 %copy-start.3 = (bf16[1,10,1536]{2,1,0:T(8,128)(2,1)S(1)}, bf16[1,10,1536]{2,1,0:T(8,128)(2,1)}, u32[]{:S(2)}) copy-start(bf16[1,10,1536]{2,1,0:T(8,128)(2,1)} %param.7) | copy-start | bytes 92164
  252.6 572.7 %copy-start.2 = (f32[640,128]{1,0:T(8,128)S(1)}, f32[640,128]{1,0:T(8,128)}, u32[]{:S(2)}) copy-start(f32[640,128]{1,0:T(8,128)} %all-reduce.5.cloned.1.call-done) | copy-start | bytes 983044
  252.6 659.8 %all-gather.7.cloned.1.call-start = ((), (), s32[]{:S(2)}) async-start(), calls=%async_computation.3 | async-start | bytes 3194880 | tf_op jit(solution)/shard_map/all_gather | solution.py:54
  796.4 232.7 %all-reduce.7.cloned.1.call-start = ((), (), s32[]{:S(2)}) async-start(), calls=%async_computation.1 | async-start | bytes 655360 | tf_op jit(solution)/shard_map/psum | solution.py:58
Sparse Core Ops, SparseCore 0:
  10.7 122.3 all-gather.4
  136.8 112.1 all-reduce.4
  252.8 541.9 all-reduce.8
  797.4 114.9 all-gather.6
  916.9 112.1 all-reduce.6
where the time goes:
time: 1040 us
  waiting for transfers between devices  968 us (93%)
  blocking collectives  28.8 us (3%)
  between operations  14.5 us (1%)
  matrix products  13.7 us (1%)
  local copies, waits for them, and re-layouts  11.8 us (1%)
    unnamed x6, waiting for transfers between devices  540 us
    all_gather x1, waiting for transfers between devices, body(): gathered = lax.all_gather(local_rows, 'lat', axis=0, tiled=True)  124 us
    psum x1, waiting for transfers between devices, body(): pre_sum, norm_total = lax.psum((partial_pre, own_norm), 'snap')  112 us
    psum x1, waiting for transfers between devices, body(): grad_sum = lax.psum(product, 'snap')  105 us
    all_gather x1, waiting for transfers between devices, body(): incoming = lax.all_gather(errors, 'lat', axis=0, tiled=True)  87 us
    psum x1, blocking collectives, body(): pre_sum, norm_total = lax.psum((partial_pre, own_norm), 'snap')  28.8 us
  transfers between devices with their start and end apart: 5, of which 5 were waited for; matrix products, arithmetic and copies ran while one was open for 1% of the time, Pallas kernels for 0%

commit v1 on v0

v1 whole, which is shorter than its diff:
```python
import jax
import jax.numpy as jnp
from jax import lax
from jax.sharding import PartitionSpec as P

sparsity_weight = 1.0
learn_rate = 0.001
beta_first = 0.9
beta_second = 0.999
corr_first = 0.6513215599
corr_second = 0.0099551198
adam_epsilon = 1e-08
norm_epsilon = 1e-06

CHUNKS = (4, 6)
BOTH = ("snap", "lat")
LANES = 128


def mm(left, right, dims):
    return lax.dot_general(left, right, (dims, ((), ())), preferred_element_type=jnp.float32)


def swap(x, core, own, other):
    low = jnp.where(core == 0, own, other)
    high = jnp.where(core == 0, other, own)
    return jnp.concatenate([low, high], axis=x)


def body(activations, enc_weight, enc_bias, dec_weight, dec_bias, dec_first, dec_second):
    snaps = lax.axis_size("snap")
    lats = lax.axis_size("lat")
    rows_dev, width = activations.shape[1:]
    lat_dev = enc_weight.shape[2]
    half = width // 2
    quarter = half // 2
    batch_rows = rows_dev * lats
    scale_rec = 2.0 / batch_rows
    scale_sparse = sparsity_weight / batch_rows
    snap = lax.axis_index("snap")
    lat = lax.axis_index("lat")
    core = lat % 2
    chip = lat // 2
    pair_groups = [[c * lats + 2 * j + k for c in range(snaps) for k in range(2)] for j in range(lats // 2)]
    chip_groups = [[2 * j + k for j in range(lats // 2)] for k in range(2)]
    partner = [(i, i ^ 1) for i in range(lats)]
    pairs = 2 * snaps
    chips = lats // 2

    def over_pairs(x):
        return lax.all_to_all(x, BOTH, 0, 0, tiled=True, axis_index_groups=pair_groups)

    def over_chips(x):
        return lax.all_to_all(x, "lat", 0, 0, tiled=True, axis_index_groups=chip_groups)

    def exchange(x):
        return lax.ppermute(x, "lat", partner)

    rows = activations[0]
    enc_local = enc_weight[0]
    dec_local = dec_weight[:, 0, :]

    gathered = []
    first = 0
    for size in CHUNKS:
        part = rows[first : first + size].reshape(size, 2, half).transpose(1, 0, 2)
        part = part.reshape(1, 2, size * half // LANES, LANES)
        sent = jnp.broadcast_to(part, (chips,) + part.shape[1:]).reshape((lats,) + part.shape[2:])
        got = lax.all_to_all(sent, "lat", 0, 0, tiled=True)
        gathered.append(got.reshape(lats * size, half))
        first += size

    enc_split = enc_local.reshape(2, half, lat_dev)
    enc_own = lax.dynamic_index_in_dim(enc_split, core, 0, keepdims=False)
    enc_other = exchange(lax.dynamic_index_in_dim(enc_split, 1 - core, 0, keepdims=False))
    enc_pair = swap(1, core, enc_own, enc_other)
    dec_own = lax.dynamic_slice_in_dim(dec_local, core * half, half, 1)
    dec_other = exchange(lax.dynamic_slice_in_dim(dec_local, (1 - core) * half, half, 1))
    dec_pair = swap(0, core, dec_own, dec_other)
    dec_float = dec_local.astype(jnp.float32)
    own_norm = jnp.sqrt(jnp.sum(dec_float * dec_float, axis=1) + norm_epsilon)
    nothing = jnp.zeros_like(own_norm)
    norm_part = scale_sparse * swap(0, core, own_norm, nothing)
    bias_part = jnp.where(snap == 0, swap(0, core, enc_bias, nothing), 0.0)

    place_col = chip // (chips // 2)
    place_row = chip % (chips // 2)
    bias_block = lax.dynamic_slice_in_dim(dec_bias[0], core * half + place_col * quarter, quarter, 0)

    pres = []
    for a in gathered:
        partial = mm(a, enc_pair, ((1,), (0,))) + bias_part[None, :]
        count = a.shape[0] // pairs
        pres.append(jnp.sum(over_pairs(partial.reshape(pairs, count, 2 * lat_dev)), axis=0))

    codes_all = []
    for pre in pres:
        codes_block = jnp.maximum(pre, 0.0).astype(jnp.bfloat16)
        sent = jnp.broadcast_to(codes_block[None], (pairs,) + codes_block.shape)
        codes_all.append(over_pairs(sent).reshape(-1, 2 * lat_dev))

    errors_all = []
    for a, codes in zip(gathered, codes_all):
        count = a.shape[0] // (chips // 2)
        sent = jnp.concatenate(
            [
                mm(codes, dec_pair[:, i * quarter : (i + 1) * quarter], ((1,), (0,)))
                .astype(jnp.bfloat16)
                .reshape(chips // 2, count, quarter)
                for i in range(2)
            ],
            axis=0,
        )
        decoded = jnp.sum(over_chips(sent).astype(jnp.float32), axis=0)
        target = lax.dynamic_slice(a, (place_row * count, place_col * quarter), (count, quarter))
        errors = (decoded + bias_block[None, :] - target.astype(jnp.float32)).astype(jnp.bfloat16)
        got = over_chips(jnp.broadcast_to(errors[None], (chips,) + errors.shape))
        got = got.reshape(2, a.shape[0], quarter)
        errors_all.append(jnp.concatenate([got[0], got[1]], axis=1))

    grads = []
    for errors, pre in zip(errors_all, pres):
        partial = scale_rec * mm(errors, dec_pair, ((1,), (1,))) + norm_part[None, :]
        partial = partial.astype(jnp.bfloat16).reshape((pairs,) + pre.shape)
        grad = jnp.sum(over_pairs(partial).astype(jnp.float32), axis=0)
        grad_block = jnp.where(pre > 0.0, grad, 0.0).astype(jnp.bfloat16)
        sent = grad_block.reshape(pre.shape[0], 2, lat_dev).transpose(1, 0, 2)
        sent = jnp.broadcast_to(sent[None], (snaps,) + sent.shape).reshape((pairs,) + sent.shape[1:])
        grads.append(over_pairs(sent).reshape(-1, lat_dev))

    dec_acc = sum(mm(c, e, ((0,), (0,))) for c, e in zip(codes_all, errors_all))
    dec_acc = dec_acc.reshape(2, lat_dev, half)
    acc_own = lax.dynamic_index_in_dim(dec_acc, core, 0, keepdims=False)
    acc_other = exchange(lax.dynamic_index_in_dim(dec_acc, 1 - core, 0, keepdims=False))
    dec_term = swap(1, core, acc_own, acc_other)
    code_pair = sum(jnp.sum(c.astype(jnp.float32), axis=0) for c in codes_all)
    code_total = lax.dynamic_slice_in_dim(code_pair, core * lat_dev, lat_dev, 0)
    dec_grad = scale_rec * dec_term + scale_sparse * code_total[:, None] * dec_float / own_norm[:, None]
    dec_grad = dec_grad[:, None, :]
    new_first = beta_first * dec_first + (1.0 - beta_first) * dec_grad
    new_second = beta_second * dec_second + (1.0 - beta_second) * dec_grad * dec_grad
    new_decoder = dec_float[:, None, :] - learn_rate * (new_first / corr_first) / (
        jnp.sqrt(new_second / corr_second) + adam_epsilon
    )

    enc_half_own = sum(mm(a, g, ((0,), (0,))) for a, g in zip(gathered, grads))
    enc_half_other = sum(mm(exchange(a), g, ((0,), (0,))) for a, g in zip(gathered, grads))
    enc_grad = swap(0, core, enc_half_own.astype(jnp.bfloat16), enc_half_other.astype(jnp.bfloat16))[None]
    return (enc_grad, new_decoder, new_first, new_second)


def solution(mesh):
    in_specs = (
        P("snap", "lat", None),
        P("snap", None, "lat"),
        P("lat"),
        P("lat", "snap", None),
        P("snap", None),
        P("lat", "snap", None),
        P("lat", "snap", None),
    )
    out_specs = (
        P("snap", None, "lat"),
        P("lat", "snap", None),
        P("lat", "snap", None),
        P("lat", "snap", None),
    )
    return jax.shard_map(body, mesh=mesh, in_specs=in_specs, out_specs=out_specs, check_vma=False)
```

time: 1040 us -> 290 us (0.28)
  the two profiles are of different devices: /device:TPU:64 before, /device:TPU:9 now
where the time goes in v1:
time: 290 us; the launch traced here: 289 us
  waiting for transfers between devices  153 us (53%)
  starting transfers between devices  101 us (35%)
  local copies, waits for them, and re-layouts  18.1 us (6%)
  matrix products  11.2 us (4%)
  other arithmetic  4.1 us (1%)
    all_to_all x8, waiting for transfers between devices, over_pairs(): lax.all_to_all(x, BOTH, 0, 0, tiled=True, axis_index_groups=pair_groups)  77.2 us
    all_to_all x4, waiting for transfers between devices, over_chips(): lax.all_to_all(x, 'lat', 0, 0, tiled=True, axis_index_groups=chip_groups)  47.5 us
    all_to_all x8, starting transfers between devices, over_pairs(): lax.all_to_all(x, BOTH, 0, 0, tiled=True, axis_index_groups=pair_groups)  47.4 us
    all_to_all x2, waiting for transfers between devices, body(): got = lax.all_to_all(sent, 'lat', 0, 0, tiled=True)  27.7 us
    all_to_all x4, starting transfers between devices, over_chips(): lax.all_to_all(x, 'lat', 0, 0, tiled=True, axis_index_groups=chip_groups)  21.2 us
    all_to_all x2, starting transfers between devices, body(): got = lax.all_to_all(sent, 'lat', 0, 0, tiled=True)  20.5 us
    ppermute x5, starting transfers between devices, exchange(): return lax.ppermute(x, 'lat', partner)  11.5 us
    dot_general x14, matrix products, mm(): lax.dot_general(left, right, (dims, ((), ())), preferred_element_type=jnp...  11.2 us
  transfers between devices with their start and end apart: 19, of which 15 were waited for; matrix products, arithmetic and copies ran while one was open for 8% of the time, Pallas kernels for 0%

profile of v1, /device:TPU:9, one launch (start us, length us, event | category | flops | bytes accessed | tf_op | source)
XLA Modules:
  0.0 288.5 jit_solution(13263024239789184393)
XLA Ops:
  2.3 14.6 %all-to-all-start = ((bf16[64,24,128]{2,1,0:T(8,128)(2,1)}), bf16[64,24,128]{2,1,0:T(8,128)(2,1)S(1)}, u32[]{:S(2)}, u32[]{:S(2)}) async-start(bf16[64,24,128]{2,1,0:T(8,128)(2,1)} %bitcast.5), calls=%async_computation | async-start | bytes 786432 | tf_op jit(solution)/shard_map/all_to_all | solution.py:69
  17.0 14.7 %all-to-all-done = bf16[64,24,128]{2,1,0:T(8,128)(2,1)S(1)} async-done(((bf16[64,24,128]{2,1,0:T(8,128)(2,1)}), bf16[64,24,128]{2,1,0:T(8,128)(2,1)S(1)}, u32[]{:S(2)}, u32[]{:S(2)}) %all-to-all-start) | async-done | bytes 393248 | tf_op jit(solution)/shard_map/all_to_all | solution.py:69
  31.7 0.9 broadcast_in_dim.40
  32.6 5.8 %all-to-all-start.7 = ((bf16[64,36,128]{2,1,0:T(8,128)(2,1)}), bf16[64,36,128]{2,1,0:T(8,128)(2,1)S(1)}, u32[]{:S(2)}, u32[]{:S(2)}) async-start(bf16[64,36,128]{2,1,0:T(8,128)(2,1)} %bitcast.21), calls=%async_computation.7 | async-start | bytes 1310720 | tf_op jit(solution)/shard_map/all_to_all | solution.py:69
  38.5 2.3 collective-permute-start
  40.8 1.0 collective-permute-done
  41.9 1.1 reshape.214
  43.0 2.0 convolution_add_fusion.4
  45.0 13.0 %all-to-all-done.7 = bf16[64,36,128]{2,1,0:T(8,128)(2,1)S(1)} async-done(((bf16[64,36,128]{2,1,0:T(8,128)(2,1)}), bf16[64,36,128]{2,1,0:T(8,128)(2,1)S(1)}, u32[]{:S(2)}, u32[]{:S(2)}) %all-to-all-start.7) | async-done | bytes 589856 | tf_op jit(solution)/shard_map/all_to_all | solution.py:69
  58.0 7.0 %all-to-all-start.1 = ((f32[16,16,256]{2,1,0:T(8,128)}), f32[16,16,256]{2,1,0:T(8,128)S(1)}, u32[]{:S(2)}, u32[]{:S(2)}) async-start(f32[16,16,256]{2,1,0:T(8,128)} %bitcast.7), calls=%async_computation.1 | async-start | bytes 524288 | tf_op jit(solution)/shard_map/all_to_all | solution.py:51
  65.0 2.0 collective-permute-start.1
  67.6 8.6 %all-to-all-done.1 = f32[16,16,256]{2,1,0:T(8,128)S(1)} async-done(((f32[16,16,256]{2,1,0:T(8,128)}), f32[16,16,256]{2,1,0:T(8,128)S(1)}, u32[]{:S(2)}, u32[]{:S(2)}) %all-to-all-start.1) | async-done | bytes 262176 | tf_op jit(solution)/shard_map/all_to_all | solution.py:51
  76.9 6.8 %all-to-all-start.2 = ((bf16[16,16,256]{2,1,0:T(8,128)(2,1)}), bf16[16,16,256]{2,1,0:T(8,128)(2,1)S(1)}, u32[]{:S(2)}, u32[]{:S(2)}) async-start(bf16[16,16,256]{2,1,0:T(8,128)(2,1)} %broadcast_in_dim.35), calls=%async_computation.2 | async-start | bytes 262144 | tf_op jit(solution)/shard_map/all_to_all | solution.py:51
  85.1 10.2 %all-to-all-done.2 = bf16[16,16,256]{2,1,0:T(8,128)(2,1)S(1)} async-done(((bf16[16,16,256]{2,1,0:T(8,128)(2,1)}), bf16[16,16,256]{2,1,0:T(8,128)(2,1)S(1)}, u32[]{:S(2)}, u32[]{:S(2)}) %all-to-all-start.2) | async-done | bytes 131104 | tf_op jit(solution)/shard_map/all_to_all | solution.py:51
  95.3 4.0 %all-to-all-start.8 = ((f32[16,24,256]{2,1,0:T(8,128)}), f32[16,24,256]{2,1,0:T(8,128)S(1)}, u32[]{:S(2)}, u32[]{:S(2)}) async-start(f32[16,24,256]{2,1,0:T(8,128)} %bitcast.23), calls=%async_computation.8 | async-start | bytes 786432 | tf_op jit(solution)/shard_map/all_to_all | solution.py:51
  100.6 15.3 %all-to-all-done.8 = f32[16,24,256]{2,1,0:T(8,128)S(1)} async-done(((f32[16,24,256]{2,1,0:T(8,128)}), f32[16,24,256]{2,1,0:T(8,128)S(1)}, u32[]{:S(2)}, u32[]{:S(2)}) %all-to-all-start.8) | async-done | bytes 393248 | tf_op jit(solution)/shard_map/all_to_all | solution.py:51
  116.0 3.7 %all-to-all-start.3 = ((bf16[32,16,384]{2,1,0:T(8,128)(2,1)}), bf16[32,16,384]{2,1,0:T(8,128)(2,1)S(1)}, u32[]{:S(2)}, u32[]{:S(2)}) async-start(bf16[32,16,384]{2,1,0:T(8,128)(2,1)} %pad_maximum_fusion.4), calls=%async_computation.3 | async-start | bytes 786432 | tf_op jit(solution)/shard_map/all_to_all | solution.py:54
  119.7 11.6 %all-to-all-done.3 = bf16[32,16,384]{2,1,0:T(8,128)(2,1)S(1)} async-done(((bf16[32,16,384]{2,1,0:T(8,128)(2,1)}), bf16[32,16,384]{2,1,0:T(8,128)(2,1)S(1)}, u32[]{:S(2)}, u32[]{:S(2)}) %all-to-all-start.3) | async-done | bytes 393248 | tf_op jit(solution)/shard_map/all_to_all | solution.py:54
  132.0 6.5 %all-to-all-start.9 = ((bf16[16,24,256]{2,1,0:T(8,128)(2,1)}), bf16[16,24,256]{2,1,0:T(8,128)(2,1)S(1)}, u32[]{:S(2)}, u32[]{:S(2)}) async-start(bf16[16,24,256]{2,1,0:T(8,128)(2,1)} %broadcast_in_dim.41), calls=%async_computation.9 | async-start | bytes 393216 | tf_op jit(solution)/shard_map/all_to_all | solution.py:51
  139.3 11.9 %all-to-all-done.9 = bf16[16,24,256]{2,1,0:T(8,128)(2,1)S(1)} async-done(((bf16[16,24,256]{2,1,0:T(8,128)(2,1)}), bf16[16,24,256]{2,1,0:T(8,128)(2,1)S(1)}, u32[]{:S(2)}, u32[]{:S(2)}) %all-to-all-start.9) | async-done | bytes 196640 | tf_op jit(solution)/shard_map/all_to_all | solution.py:51
  152.0 4.0 %all-to-all-start.4 = ((bf16[32,16,384]{2,1,0:T(8,128)(2,1)}), bf16[32,16,384]{2,1,0:T(8,128)(2,1)S(1)}, u32[]{:S(2)}, u32[]{:S(2)}) async-start(bf16[32,16,384]{2,1,0:T(8,128)(2,1)} %broadcast_in_dim.36), calls=%async_computation.4 | async-start | bytes 786432 | tf_op jit(solution)/shard_map/all_to_all | solution.py:54
  157.4 10.6 %all-to-all-done.4 = bf16[32,16,384]{2,1,0:T(8,128)(2,1)S(1)} async-done(((bf16[32,16,384]{2,1,0:T(8,128)(2,1)}), bf16[32,16,384]{2,1,0:T(8,128)(2,1)S(1)}, u32[]{:S(2)}, u32[]{:S(2)}) %all-to-all-start.4) | async-done | bytes 393248 | tf_op jit(solution)/shard_map/all_to_all | solution.py:54
  168.0 7.4 %all-to-all-start.10 = ((bf16[32,24,384]{2,1,0:T(8,128)(2,1)}), bf16[32,24,384]{2,1,0:T(8,128)(2,1)S(1)}, u32[]{:S(2)}, u32[]{:S(2)}) async-start(bf16[32,24,384]{2,1,0:T(8,128)(2,1)} %pad_maximum_fusion), calls=%async_computation.10 | async-start | bytes 1179648 | tf_op jit(solution)/shard_map/all_to_all | solution.py:54
  175.7 1.0 fusion.6
  176.7 15.1 %all-to-all-done.10 = bf16[32,24,384]{2,1,0:T(8,128)(2,1)S(1)} async-done(((bf16[32,24,384]{2,1,0:T(8,128)(2,1)}), bf16[32,24,384]{2,1,0:T(8,128)(2,1)S(1)}, u32[]{:S(2)}, u32[]{:S(2)}) %all-to-all-start.10) | async-done | bytes 589856 | tf_op jit(solution)/shard_map/all_to_all | solution.py:54
  191.7 6.0 %all-to-all-start.5 = ((bf16[16,16,256]{2,1,0:T(8,128)(2,1)}), bf16[16,16,256]{2,1,0:T(8,128)(2,1)S(1)}, u32[]{:S(2)}, u32[]{:S(2)}) async-start(bf16[16,16,256]{2,1,0:T(8,128)(2,1)} %bitcast.15), calls=%async_computation.5 | async-start | bytes 262144 | tf_op jit(solution)/shard_map/all_to_all | solution.py:51
  197.9 9.9 %all-to-all-done.5 = bf16[16,16,256]{2,1,0:T(8,128)(2,1)S(1)} async-done(((bf16[16,16,256]{2,1,0:T(8,128)(2,1)}), bf16[16,16,256]{2,1,0:T(8,128)(2,1)S(1)}, u32[]{:S(2)}, u32[]{:S(2)}) %all-to-all-start.5) | async-done | bytes 131104 | tf_op jit(solution)/shard_map/all_to_all | solution.py:51
  209.3 6.1 %all-to-all-start.11 = ((bf16[32,24,384]{2,1,0:T(8,128)(2,1)}), bf16[32,24,384]{2,1,0:T(8,128)(2,1)S(1)}, u32[]{:S(2)}, u32[]{:S(2)}) async-start(bf16[32,24,384]{2,1,0:T(8,128)(2,1)} %broadcast_in_dim.42), calls=%async_computation.11 | async-start | bytes 1179648 | tf_op jit(solution)/shard_map/all_to_all | solution.py:54
  215.4 3.1 %collective-permute-start.2 = (bf16[256,768]{1,0:T(8,128)(2,1)}, bf16[256,768]{1,0:T(8,128)(2,1)}, u32[]{:S(2)}, u32[]{:S(2)}) collective-permute-start(bf16[256,768]{1,0:T(8,128)(2,1)} %reshape.214), channel_id=1, source_target_pairs={{0,1},{1,0},{2,3},{3,2},{4,5},{5,4},{6,7},{7,6},{8,9},{9,8},{10,11... | collective-permute-start | bytes 1179656 | tf_op jit(solution)/shard_map/ppermute | solution.py:57
  218.6 1.9 collective-permute-start.3
  221.5 10.2 %all-to-all-done.11 = bf16[32,24,384]{2,1,0:T(8,128)(2,1)S(1)} async-done(((bf16[32,24,384]{2,1,0:T(8,128)(2,1)}), bf16[32,24,384]{2,1,0:T(8,128)(2,1)S(1)}, u32[]{:S(2)}, u32[]{:S(2)}) %all-to-all-start.11) | async-done | bytes 589856 | tf_op jit(solution)/shard_map/all_to_all | solution.py:54
  231.8 1.0 fusion.2
  232.8 6.0 %all-to-all-start.12 = ((bf16[16,24,256]{2,1,0:T(8,128)(2,1)}), bf16[16,24,256]{2,1,0:T(8,128)(2,1)S(1)}, u32[]{:S(2)}, u32[]{:S(2)}) async-start(bf16[16,24,256]{2,1,0:T(8,128)(2,1)} %bitcast.29), calls=%async_computation.12 | async-start | bytes 393216 | tf_op jit(solution)/shard_map/all_to_all | solution.py:51
  238.8 1.4 convolution_add_fusion
  240.3 2.1 collective-permute-start.4
  242.5 9.1 %all-to-all-done.12 = bf16[16,24,256]{2,1,0:T(8,128)(2,1)S(1)} async-done(((bf16[16,24,256]{2,1,0:T(8,128)(2,1)}), bf16[16,24,256]{2,1,0:T(8,128)(2,1)S(1)}, u32[]{:S(2)}, u32[]{:S(2)}) %all-to-all-start.12) | async-done | bytes 196640 | tf_op jit(solution)/shard_map/all_to_all | solution.py:51
  252.3 4.1 %all-to-all-start.13 = ((bf16[16,24,128]{2,1,0:T(8,128)(2,1)}), bf16[16,24,128]{2,1,0:T(8,128)(2,1)S(1)}, u32[]{:S(2)}, u32[]{:S(2)}) async-start(bf16[16,24,128]{2,1,0:T(8,128)(2,1)} %bitcast.31), calls=%async_computation.13 | async-start | bytes 196608 | tf_op jit(solution)/shard_map/all_to_all | solution.py:51
  256.5 1.0 copy-done.6
  258.6 1.7 copy.38
  260.3 1.7 copy.39
  261.9 1.7 copy.40
  263.6 2.7 all-to-all-done.13
  267.0 7.0 %all-to-all-start.6 = ((bf16[16,16,128]{2,1,0:T(8,128)(2,1)}), bf16[16,16,128]{2,1,0:T(8,128)(2,1)S(1)}, u32[]{:S(2)}, u32[]{:S(2)}) async-start(bf16[16,16,128]{2,1,0:T(8,128)(2,1)} %bitcast.17), calls=%async_computation.6 | async-start | bytes 131072 | tf_op jit(solution)/shard_map/all_to_all | solution.py:51
  274.3 9.4 %all-to-all-done.6 = bf16[16,16,128]{2,1,0:T(8,128)(2,1)S(1)} async-done(((bf16[16,16,128]{2,1,0:T(8,128)(2,1)}), bf16[16,16,128]{2,1,0:T(8,128)(2,1)S(1)}, u32[]{:S(2)}, u32[]{:S(2)}) %all-to-all-start.6) | async-done | bytes 65568 | tf_op jit(solution)/shard_map/all_to_all | solution.py:51
  283.7 1.2 fusion.3
  285.0 1.4 fusion.33
  286.3 1.2 select_bitcast_fusion.1
  287.6 0.9 copy.37
  (87 shorter events, 15.1 us)
Async XLA Ops:
  0.6 137.9 %copy-start = (f32[1,1536]{1,0:T(1,128)S(1)}, f32[1,1536]{1,0:T(1,128)}, u32[]{:S(2)}) copy-start(f32[1,1536]{1,0:T(1,128)} %param.11) | copy-start | bytes 18436
  0.6 16.3 %copy-start.11 = (bf16[1,10,1536]{2,1,0:T(8,128)(2,1)S(1)}, bf16[1,10,1536]{2,1,0:T(8,128)(2,1)}, u32[]{:S(2)}) copy-start(bf16[1,10,1536]{2,1,0:T(8,128)(2,1)} %param.7) | copy-start | bytes 92164
  2.3 29.4 %all-to-all-start = ((bf16[64,24,128]{2,1,0:T(8,128)(2,1)}), bf16[64,24,128]{2,1,0:T(8,128)(2,1)S(1)}, u32[]{:S(2)}, u32[]{:S(2)}) async-start(bf16[64,24,128]{2,1,0:T(8,128)(2,1)} %bitcast.5), calls=%async_computation | async-start | bytes 786432 | tf_op jit(solution)/shard_map/all_to_all | solution.py:69
  32.6 5.8 %copy-start.10 = (bf16[1,1536,128]{2,1,0:T(8,128)(2,1)S(1)}, bf16[1,1536,128]{2,1,0:T(8,128)(2,1)}, u32[]{:S(2)}) copy-start(bf16[1,1536,128]{2,1,0:T(8,128)(2,1)} %param.8) | copy-start | bytes 1179652
  32.6 8.2 %copy-start.12 = (f32[128]{0:T(128)S(1)}, f32[128]{0:T(128)}, u32[]{:S(2)}) copy-start(f32[128]{0:T(128)} %param.9) | copy-start | bytes 1540
  32.6 25.4 %all-to-all-start.7 = ((bf16[64,36,128]{2,1,0:T(8,128)(2,1)}), bf16[64,36,128]{2,1,0:T(8,128)(2,1)S(1)}, u32[]{:S(2)}, u32[]{:S(2)}) async-start(bf16[64,36,128]{2,1,0:T(8,128)(2,1)} %bitcast.21), calls=%async_computation.7 | async-start | bytes 1310720 | tf_op jit(solution)/shard_map/all_to_all | solution.py:69
  38.5 3.4 %collective-permute-start = (bf16[768,128]{1,0:T(8,128)(2,1)S(1)}, bf16[768,128]{1,0:T(8,128)(2,1)S(1)}, u32[]{:S(2)}, u32[]{:S(2)}) collective-permute-start(bf16[768,128]{1,0:T(8,128)(2,1)S(1)} %dynamic-slice_bitcast_fusion.2), channel_id=1, source_target_pairs={{0,1},{1,0},{2,3},{3,2},{4,5},{5,4},{6,7},{7,6},{8,9},{9,8},{10,11... | collective-permute-start | bytes 589832 | tf_op jit(solution)/shard_map/ppermute | solution.py:57
  43.0 22.0 %copy-start.1 = (bf16[128,1,1536]{2,0,1:T(8,128)(2,1)S(1)}, bf16[128,1,1536]{2,0,1:T(8,128)(2,1)}, u32[]{:S(2)}) copy-start(bf16[128,1,1536]{2,0,1:T(8,128)(2,1)} %param.10) | copy-start | bytes 1179652
  58.0 18.2 %all-to-all-start.1 = ((f32[16,16,256]{2,1,0:T(8,128)}), f32[16,16,256]{2,1,0:T(8,128)S(1)}, u32[]{:S(2)}, u32[]{:S(2)}) async-start(f32[16,16,256]{2,1,0:T(8,128)} %bitcast.7), calls=%async_computation.1 | async-start | bytes 524288 | tf_op jit(solution)/shard_map/all_to_all | solution.py:51
  65.0 34.3 %collective-permute-start.1 = (bf16[128,768]{1,0:T(8,128)(2,1)S(1)}, bf16[128,768]{1,0:T(8,128)(2,1)S(1)}, u32[]{:S(2)}, u32[]{:S(2)}) collective-permute-start(bf16[128,768]{1,0:T(8,128)(2,1)S(1)} %dynamic-slice_bitcast_fusion.1), channel_id=1, source_target_pairs={{0,1},{1,0},{2,3},{3,2},{4,5},{5,4},{6,7},{7,6},{8,9},{9,8},{10,11... | collective-permute-start | bytes 589832 | tf_op jit(solution)/shard_map/ppermute | solution.py:57
  76.9 18.4 %all-to-all-start.2 = ((bf16[16,16,256]{2,1,0:T(8,128)(2,1)}), bf16[16,16,256]{2,1,0:T(8,128)(2,1)S(1)}, u32[]{:S(2)}, u32[]{:S(2)}) async-start(bf16[16,16,256]{2,1,0:T(8,128)(2,1)} %broadcast_in_dim.35), calls=%async_computation.2 | async-start | bytes 262144 | tf_op jit(solution)/shard_map/all_to_all | solution.py:51
  95.3 20.7 %all-to-all-start.8 = ((f32[16,24,256]{2,1,0:T(8,128)}), f32[16,24,256]{2,1,0:T(8,128)S(1)}, u32[]{:S(2)}, u32[]{:S(2)}) async-start(f32[16,24,256]{2,1,0:T(8,128)} %bitcast.23), calls=%async_computation.8 | async-start | bytes 786432 | tf_op jit(solution)/shard_map/all_to_all | solution.py:51
  116.0 15.3 %all-to-all-start.3 = ((bf16[32,16,384]{2,1,0:T(8,128)(2,1)}), bf16[32,16,384]{2,1,0:T(8,128)(2,1)S(1)}, u32[]{:S(2)}, u32[]{:S(2)}) async-start(bf16[32,16,384]{2,1,0:T(8,128)(2,1)} %pad_maximum_fusion.4), calls=%async_computation.3 | async-start | bytes 786432 | tf_op jit(solution)/shard_map/all_to_all | solution.py:54
  132.0 19.2 %all-to-all-start.9 = ((bf16[16,24,256]{2,1,0:T(8,128)(2,1)}), bf16[16,24,256]{2,1,0:T(8,128)(2,1)S(1)}, u32[]{:S(2)}, u32[]{:S(2)}) async-start(bf16[16,24,256]{2,1,0:T(8,128)(2,1)} %broadcast_in_dim.41), calls=%async_computation.9 | async-start | bytes 393216 | tf_op jit(solution)/shard_map/all_to_all | solution.py:51
  152.0 16.0 %all-to-all-start.4 = ((bf16[32,16,384]{2,1,0:T(8,128)(2,1)}), bf16[32,16,384]{2,1,0:T(8,128)(2,1)S(1)}, u32[]{:S(2)}, u32[]{:S(2)}) async-start(bf16[32,16,384]{2,1,0:T(8,128)(2,1)} %broadcast_in_dim.36), calls=%async_computation.4 | async-start | bytes 786432 | tf_op jit(solution)/shard_map/all_to_all | solution.py:54
  168.0 23.7 %all-to-all-start.10 = ((bf16[32,24,384]{2,1,0:T(8,128)(2,1)}), bf16[32,24,384]{2,1,0:T(8,128)(2,1)S(1)}, u32[]{:S(2)}, u32[]{:S(2)}) async-start(bf16[32,24,384]{2,1,0:T(8,128)(2,1)} %pad_maximum_fusion), calls=%async_computation.10 | async-start | bytes 1179648 | tf_op jit(solution)/shard_map/all_to_all | solution.py:54
  175.7 1.0 copy-start.4
  191.7 16.0 %all-to-all-start.5 = ((bf16[16,16,256]{2,1,0:T(8,128)(2,1)}), bf16[16,16,256]{2,1,0:T(8,128)(2,1)S(1)}, u32[]{:S(2)}, u32[]{:S(2)}) async-start(bf16[16,16,256]{2,1,0:T(8,128)(2,1)} %bitcast.15), calls=%async_computation.5 | async-start | bytes 262144 | tf_op jit(solution)/shard_map/all_to_all | solution.py:51
  207.8 0.7 copy-start.8
  209.3 11.4 %copy-start.5 = (bf16[16,16,384]{2,1,0:T(8,128)(2,1)S(1)}, bf16[16,16,384]{2,1,0:T(8,128)(2,1)}, u32[]{:S(2)}) copy-start(bf16[16,16,384]{2,1,0:T(8,128)(2,1)} %copy-done.4) | copy-start | bytes 589828
  209.3 22.4 %all-to-all-start.11 = ((bf16[32,24,384]{2,1,0:T(8,128)(2,1)}), bf16[32,24,384]{2,1,0:T(8,128)(2,1)S(1)}, u32[]{:S(2)}, u32[]{:S(2)}) async-start(bf16[32,24,384]{2,1,0:T(8,128)(2,1)} %broadcast_in_dim.42), calls=%async_computation.11 | async-start | bytes 1179648 | tf_op jit(solution)/shard_map/all_to_all | solution.py:54
  215.4 70.9 %collective-permute-start.2 = (bf16[256,768]{1,0:T(8,128)(2,1)}, bf16[256,768]{1,0:T(8,128)(2,1)}, u32[]{:S(2)}, u32[]{:S(2)}) collective-permute-start(bf16[256,768]{1,0:T(8,128)(2,1)} %reshape.214), channel_id=1, source_target_pairs={{0,1},{1,0},{2,3},{3,2},{4,5},{5,4},{6,7},{7,6},{8,9},{9,8},{10,11... | collective-permute-start | bytes 1179656 | tf_op jit(solution)/shard_map/ppermute | solution.py:57
  218.6 66.4 %collective-permute-start.3 = (bf16[384,768]{1,0:T(8,128)(2,1)S(1)}, bf16[384,768]{1,0:T(8,128)(2,1)}, u32[]{:S(2)}, u32[]{:S(2)}) collective-permute-start(bf16[384,768]{1,0:T(8,128)(2,1)S(1)} %reshape.224), channel_id=1, source_target_pairs={{0,1},{1,0},{2,3},{3,2},{4,5},{5,4},{6,7},{7,6},{8,9},{9,8},{10,11... | collective-permute-start | bytes 1769480 | tf_op jit(solution)/shard_map/ppermute | solution.py:57
  220.5 0.9 copy-start.9
  231.8 1.1 copy-start.2
  231.8 1.1 copy-start.3
  232.8 18.7 %all-to-all-start.12 = ((bf16[16,24,256]{2,1,0:T(8,128)(2,1)}), bf16[16,24,256]{2,1,0:T(8,128)(2,1)S(1)}, u32[]{:S(2)}, u32[]{:S(2)}) async-start(bf16[16,24,256]{2,1,0:T(8,128)(2,1)} %bitcast.29), calls=%async_computation.12 | async-start | bytes 393216 | tf_op jit(solution)/shard_map/all_to_all | solution.py:51
  240.3 16.1 %collective-permute-start.4 = (f32[128,768]{1,0:T(8,128)S(1)}, f32[128,768]{1,0:T(8,128)S(1)}, u32[]{:S(2)}, u32[]{:S(2)}) collective-permute-start(f32[128,768]{1,0:T(8,128)S(1)} %dynamic-slice_bitcast_fusion), channel_id=1, source_target_pairs={{0,1},{1,0},{2,3},{3,2},{4,5},{5,4},{6,7},{7,6},{8,9},{9,8},{10,11... | collective-permute-start | bytes 1179656 | tf_op jit(solution)/shard_map/ppermute | solution.py:57
  252.3 14.1 %all-to-all-start.13 = ((bf16[16,24,128]{2,1,0:T(8,128)(2,1)}), bf16[16,24,128]{2,1,0:T(8,128)(2,1)S(1)}, u32[]{:S(2)}, u32[]{:S(2)}) async-start(bf16[16,24,128]{2,1,0:T(8,128)(2,1)} %bitcast.31), calls=%async_computation.13 | async-start | bytes 196608 | tf_op jit(solution)/shard_map/all_to_all | solution.py:51
  256.4 1.1 copy-start.6
  256.4 1.4 copy-start.7
  267.0 16.7 %all-to-all-start.6 = ((bf16[16,16,128]{2,1,0:T(8,128)(2,1)}), bf16[16,16,128]{2,1,0:T(8,128)(2,1)S(1)}, u32[]{:S(2)}, u32[]{:S(2)}) async-start(bf16[16,16,128]{2,1,0:T(8,128)(2,1)} %bitcast.17), calls=%async_computation.6 | async-start | bytes 131072 | tf_op jit(solution)/shard_map/all_to_all | solution.py:51

commit v2 on v0

v2 whole, which is shorter than its diff:
```python
import jax
import jax.numpy as jnp
from jax import lax
from jax.sharding import PartitionSpec as P

sparsity_weight = 1.0
learn_rate = 0.001
beta_first = 0.9
beta_second = 0.999
corr_first = 0.6513215599
corr_second = 0.0099551198
adam_epsilon = 1e-08
norm_epsilon = 1e-06

LANES = 128


def mm(left, right, dims):
    return lax.dot_general(left, right, (dims, ((), ())), preferred_element_type=jnp.float32)


def pick(x, size, index):
    return lax.dynamic_slice_in_dim(x, index * size, size, x.ndim - 1)


def body(activations, enc_weight, enc_bias, dec_weight, dec_bias, dec_first, dec_second):
    snaps = lax.axis_size("snap")
    lats = lax.axis_size("lat")
    rows_dev, width = activations.shape[1:]
    lat_dev = enc_weight.shape[2]
    half = width // 2
    quarter = half // 2
    batch_rows = rows_dev * lats
    block_rows = batch_rows // snaps
    scale_rec = 2.0 / batch_rows
    scale_sparse = sparsity_weight / batch_rows
    lat = lax.axis_index("lat")
    core = lax.bitwise_and(lat, 1)
    chip = lax.shift_right_logical(lat, 1)
    chips = lats // 2
    chip_groups = [[2 * j + k for j in range(chips)] for k in range(2)]
    partner = [(i, i ^ 1) for i in range(lats)]

    def over_snaps(x):
        return lax.all_to_all(x, "snap", 0, 0, tiled=True)

    def over_chips(x):
        return lax.all_to_all(x, "lat", 0, 0, tiled=True, axis_index_groups=chip_groups)

    def exchange(x):
        return lax.ppermute(x, "lat", partner)

    def repeat(x, times):
        return jnp.broadcast_to(x[None], (times,) + x.shape)

    def ordered(axis, own, other):
        low = jnp.where(core == 0, own, other)
        high = jnp.where(core == 0, other, own)
        return jnp.concatenate([low, high], axis=axis)

    rows = activations[0]
    enc_local = enc_weight[0]
    dec_local = dec_weight[:, 0, :]

    part = rows.reshape(rows_dev, 2, half).transpose(1, 0, 2)
    part = part.reshape(2, rows_dev * half // LANES, LANES)
    sent = repeat(part, chips).reshape((lats,) + part.shape[1:])
    acts = lax.all_to_all(sent, "lat", 0, 0, tiled=True).reshape(batch_rows, half)

    enc_split = enc_local.reshape(2, half, lat_dev)
    enc_own = lax.dynamic_index_in_dim(enc_split, core, 0, keepdims=False)
    enc_other = exchange(lax.dynamic_index_in_dim(enc_split, 1 - core, 0, keepdims=False))
    dec_own = pick(dec_local, half, core)
    dec_other = exchange(pick(dec_local, half, 1 - core))
    dec_pair = jnp.concatenate([dec_own, dec_other], axis=0)
    dec_float = dec_local.astype(jnp.float32)
    own_norm = jnp.sqrt(jnp.sum(dec_float * dec_float, axis=1) + norm_epsilon)

    pre_other = exchange(mm(acts, enc_other, ((1,), (0,))))
    pre_own = mm(acts, enc_own, ((1,), (0,)))
    pre = jnp.sum(over_snaps((pre_own + pre_other).reshape(snaps, block_rows, lat_dev)), axis=0) + enc_bias[None, :]

    codes_block = jnp.maximum(pre, 0.0).astype(jnp.bfloat16)
    codes = over_snaps(repeat(codes_block, snaps)).reshape(batch_rows, lat_dev)
    codes_pair = jnp.concatenate([codes, exchange(codes)], axis=1)

    count = batch_rows // (chips // 2)
    place_col = lax.div(chip, chips // 2)
    place_row = lax.rem(chip, chips // 2)
    sent = jnp.stack(
        [
            mm(codes_pair, dec_pair[:, i * quarter : (i + 1) * quarter], ((1,), (0,))).astype(jnp.bfloat16)
            for i in range(2)
        ],
        axis=0,
    ).reshape(chips, count, quarter)
    decoded = jnp.sum(over_chips(sent).astype(jnp.float32), axis=0)
    target = lax.dynamic_slice(acts, (place_row * count, place_col * quarter), (count, quarter))
    bias_block = lax.dynamic_slice_in_dim(dec_bias[0], core * half + place_col * quarter, quarter, 0)
    errors_block = (decoded + bias_block[None, :] - target.astype(jnp.float32)).astype(jnp.bfloat16)
    got = over_chips(repeat(errors_block, chips)).reshape(2, batch_rows, quarter)
    errors = jnp.concatenate([got[0], got[1]], axis=1)

    grad_pair = mm(errors, dec_pair, ((1,), (1,)))
    grad_other = exchange((scale_rec * grad_pair[:, lat_dev:]).astype(jnp.bfloat16))
    grad_own = scale_rec * grad_pair[:, :lat_dev] + grad_other.astype(jnp.float32) + scale_sparse * own_norm[None, :]
    grad_own = grad_own.astype(jnp.bfloat16).reshape(snaps, block_rows, lat_dev)
    grad_own, errors_late = lax.optimization_barrier((grad_own, errors))
    grad = jnp.sum(over_snaps(grad_own).astype(jnp.float32), axis=0)
    grad_block = jnp.where(pre > 0.0, grad, 0.0).astype(jnp.bfloat16)
    grad_pre = over_snaps(repeat(grad_block, snaps)).reshape(batch_rows, lat_dev)

    acc_pair = mm(codes_pair, errors_late, ((0,), (0,)))
    dec_term = ordered(1, acc_pair[:lat_dev], exchange(acc_pair[lat_dev:]))
    code_total = jnp.sum(codes.astype(jnp.float32), axis=0)
    dec_grad = scale_rec * dec_term + scale_sparse * code_total[:, None] * dec_float / own_norm[:, None]
    dec_grad = dec_grad[:, None, :]
    new_first = beta_first * dec_first + (1.0 - beta_first) * dec_grad
    new_second = beta_second * dec_second + (1.0 - beta_second) * dec_grad * dec_grad
    new_decoder = dec_float[:, None, :] - learn_rate * (new_first / corr_first) / (
        jnp.sqrt(new_second / corr_second) + adam_epsilon
    )

    acts_both = lax.optimization_barrier(ordered(0, acts.T, exchange(acts).T))
    enc_grad = mm(acts_both, grad_pre, ((1,), (0,))).astype(jnp.bfloat16)[None]
    return (enc_grad, new_decoder, new_first, new_second)


def solution(mesh):
    in_specs = (
        P("snap", "lat", None),
        P("snap", None, "lat"),
        P("lat"),
        P("lat", "snap", None),
        P("snap", None),
        P("lat", "snap", None),
        P("lat", "snap", None),
    )
    out_specs = (
        P("snap", None, "lat"),
        P("lat", "snap", None),
        P("lat", "snap", None),
        P("lat", "snap", None),
    )
    return jax.shard_map(body, mesh=mesh, in_specs=in_specs, out_specs=out_specs, check_vma=False)
```

time: 1040 us -> 201 us (0.19)
  the two profiles are of different devices: /device:TPU:64 before, /device:TPU:16 now
where the time goes in v2:
time: 201 us; the launch traced here: 200 us
  waiting for transfers between devices  96.4 us (48%)
  starting transfers between devices  51.9 us (26%)
  blocking collectives  22.7 us (11%)
  local copies, waits for them, and re-layouts  14.3 us (7%)
  other arithmetic  7.43 us (4%)
  matrix products  5.8 us (3%)
    all_to_all x2, waiting for transfers between devices, over_chips(): lax.all_to_all(x, 'lat', 0, 0, tiled=True, axis_index_groups=chip_groups)  47.1 us
    all_to_all x1, waiting for transfers between devices, body(): lax.all_to_all(sent, 'lat', 0, 0, tiled=True).reshape(batch_rows, half)  25.7 us
    all_to_all x1, blocking collectives, over_snaps(): return lax.all_to_all(x, 'snap', 0, 0, tiled=True)  22.7 us
    all_to_all x3, waiting for transfers between devices, over_snaps(): return lax.all_to_all(x, 'snap', 0, 0, tiled=True)  19 us
    all_to_all x1, starting transfers between devices, body(): lax.all_to_all(sent, 'lat', 0, 0, tiled=True).reshape(batch_rows, half)  14.3 us
    ppermute x7, starting transfers between devices, exchange(): return lax.ppermute(x, 'lat', partner)  14.3 us
    all_to_all x2, starting transfers between devices, over_chips(): lax.all_to_all(x, 'lat', 0, 0, tiled=True, axis_index_groups=chip_groups)  11.7 us
    all_to_all x3, starting transfers between devices, over_snaps(): return lax.all_to_all(x, 'snap', 0, 0, tiled=True)  11.6 us
  transfers between devices with their start and end apart: 13, of which 10 were waited for; matrix products, arithmetic and copies ran while one was open for 8% of the time, Pallas kernels for 0%

profile of v2, /device:TPU:16, one launch (start us, length us, event | category | flops | bytes accessed | tf_op | source)
XLA Modules:
  0.0 199.6 jit_solution(2731130486954874040)
XLA Ops:
  0.6 0.9 reshape_squeeze.6
  1.6 1.2 broadcast_in_dim.14
  2.8 14.3 %all-to-all-start = ((bf16[64,60,128]{2,1,0:T(8,128)(2,1)}), bf16[64,60,128]{2,1,0:T(8,128)(2,1)S(1)}, u32[]{:S(2)}, u32[]{:S(2)}) async-start(bf16[64,60,128]{2,1,0:T(8,128)(2,1)} %bitcast.1), calls=%async_computation | async-start | bytes 2097152 | tf_op jit(solution)/shard_map/all_to_all | solution.py:68
  17.2 2.0 %collective-permute-start.1 = (bf16[768,128]{1,0:T(8,128)(2,1)S(1)}, bf16[768,128]{1,0:T(8,128)(2,1)S(1)}, u32[]{:S(2)}, u32[]{:S(2)}) collective-permute-start(bf16[768,128]{1,0:T(8,128)(2,1)S(1)} %dynamic-slice_bitcast_fusion.2), channel_id=1, source_target_pairs={{0,1},{1,0},{2,3},{3,2},{4,5},{5,4},{6,7},{7,6},{8,9},{9,8},{10,11... | collective-permute-start | bytes 589832 | tf_op jit(solution)/shard_map/ppermute | solution.py:51
  19.3 25.7 %all-to-all-done = bf16[64,60,128]{2,1,0:T(8,128)(2,1)S(1)} async-done(((bf16[64,60,128]{2,1,0:T(8,128)(2,1)}), bf16[64,60,128]{2,1,0:T(8,128)(2,1)S(1)}, u32[]{:S(2)}, u32[]{:S(2)}) %all-to-all-start) | async-done | bytes 983072 | tf_op jit(solution)/shard_map/all_to_all | solution.py:68
  44.9 0.9 reshape.155
  46.3 2.6 %collective-permute-start.2 = (f32[640,128]{0,1:T(8,128)S(1)}, f32[640,128]{0,1:T(8,128)S(1)}, u32[]{:S(2)}, u32[]{:S(2)}) collective-permute-start(f32[640,128]{0,1:T(8,128)S(1)} %convolution_bitcast_fusion), channel_id=1, source_target_pairs={{0,1},{1,0},{2,3},{3,2},{4,5},{5,4},{6,7},{7,6},{8,9},{9,8},{10,11... | collective-permute-start | bytes 983048 | tf_op jit(solution)/shard_map/ppermute | solution.py:51
  48.9 0.4 convolution_bitcast_fusion.1
  49.4 0.8 collective-permute-done.2
  50.3 22.7 %all_to_all.35 = f32[8,80,128]{2,1,0:T(8,128)S(1)} all-to-all(f32[8,80,128]{2,1,0:T(8,128)S(1)} %bitcast.55), channel_id=1, replica_groups=mesh['snap'=8,'lat'=64] {'snap'}, dimensions={0} | all-to-all | bytes 655360 | tf_op jit(solution)/shard_map/all_to_all | solution.py:45
  73.1 0.7 broadcast_in_dim.16
  73.8 3.4 %all-to-all-start.2 = ((bf16[8,80,128]{2,1,0:T(8,128)(2,1)}), bf16[8,80,128]{2,1,0:T(8,128)(2,1)S(1)}, u32[]{:S(2)}, u32[]{:S(2)}) async-start(bf16[8,80,128]{2,1,0:T(8,128)(2,1)} %broadcast_in_dim.16), calls=%async_computation.2 | async-start | bytes 327680 | tf_op jit(solution)/shard_map/all_to_all | solution.py:45
  77.2 1.9 collective-permute-start.4
  79.2 8.6 %all-to-all-done.2 = bf16[8,80,128]{2,1,0:T(8,128)(2,1)S(1)} async-done(((bf16[8,80,128]{2,1,0:T(8,128)(2,1)}), bf16[8,80,128]{2,1,0:T(8,128)(2,1)S(1)}, u32[]{:S(2)}, u32[]{:S(2)}) %all-to-all-start.2) | async-done | bytes 163872 | tf_op jit(solution)/shard_map/all_to_all | solution.py:45
  87.8 1.9 collective-permute-start.3
  89.7 1.3 collective-permute-done.3
  91.7 1.1 pad_maximum_fusion.1
  92.8 5.7 %all-to-all-start.3 = ((bf16[32,40,384]{2,1,0:T(8,128)(2,1)}), bf16[32,40,384]{2,1,0:T(8,128)(2,1)S(1)}, u32[]{:S(2)}, u32[]{:S(2)}) async-start(bf16[32,40,384]{2,1,0:T(8,128)(2,1)} %bitcast.15), calls=%async_computation.3 | async-start | bytes 1966080 | tf_op jit(solution)/shard_map/all_to_all | solution.py:48
  98.5 0.7 dynamic-slice_reduce_fusion
  99.2 25.6 %all-to-all-done.3 = bf16[32,40,384]{2,1,0:T(8,128)(2,1)S(1)} async-done(((bf16[32,40,384]{2,1,0:T(8,128)(2,1)}), bf16[32,40,384]{2,1,0:T(8,128)(2,1)S(1)}, u32[]{:S(2)}, u32[]{:S(2)}) %all-to-all-start.3) | async-done | bytes 983072 | tf_op jit(solution)/shard_map/all_to_all | solution.py:48
  125.0 1.0 broadcast_in_dim.17
  126.1 6.0 %all-to-all-start.4 = ((bf16[32,40,384]{2,1,0:T(8,128)(2,1)}), bf16[32,40,384]{2,1,0:T(8,128)(2,1)S(1)}, u32[]{:S(2)}, u32[]{:S(2)}) async-start(bf16[32,40,384]{2,1,0:T(8,128)(2,1)} %broadcast_in_dim.17), calls=%async_computation.4 | async-start | bytes 1966080 | tf_op jit(solution)/shard_map/all_to_all | solution.py:48
  132.0 1.9 collective-permute-start
  134.0 1.2 fusion.3
  135.1 1.4 collective-permute-done
  136.8 21.5 %all-to-all-done.4 = bf16[32,40,384]{2,1,0:T(8,128)(2,1)S(1)} async-done(((bf16[32,40,384]{2,1,0:T(8,128)(2,1)}), bf16[32,40,384]{2,1,0:T(8,128)(2,1)S(1)}, u32[]{:S(2)}, u32[]{:S(2)}) %all-to-all-start.4) | async-done | bytes 983072 | tf_op jit(solution)/shard_map/all_to_all | solution.py:48
  158.3 0.8 copy-done.8
  159.3 0.5 fusion.8
  159.8 1.9 collective-permute-start.5
  161.9 1.2 collective-permute-done.5
  163.0 0.7 fusion.12
  163.8 4.0 %all-to-all-start.5 = ((bf16[8,80,128]{2,1,0:T(8,128)(2,1)}), bf16[8,80,128]{2,1,0:T(8,128)(2,1)}, u32[]{:S(2)}, u32[]{:S(2)}) async-start(bf16[8,80,128]{2,1,0:T(8,128)(2,1)} %bitcast.56), calls=%async_computation.5 | async-start | bytes 327680 | tf_op jit(solution)/shard_map/all_to_all | solution.py:45
  167.8 1.4 fusion.19
  169.2 0.9 copy-done.3
  170.1 0.8 slice.43
  170.9 2.0 %collective-permute-start.6 = (f32[128,768]{1,0:T(8,128)}, f32[128,768]{1,0:T(8,128)}, u32[]{:S(2)}, u32[]{:S(2)}) collective-permute-start(f32[128,768]{1,0:T(8,128)} %slice.43), channel_id=1, source_target_pairs={{0,1},{1,0},{2,3},{3,2},{4,5},{5,4},{6,7},{7,6},{8,9},{9,8},{10,11... | collective-permute-start | bytes 1179656 | tf_op jit(solution)/shard_map/ppermute | solution.py:51
  172.9 6.9 %all-to-all-done.5 = bf16[8,80,128]{2,1,0:T(8,128)(2,1)} async-done(((bf16[8,80,128]{2,1,0:T(8,128)(2,1)}), bf16[8,80,128]{2,1,0:T(8,128)(2,1)}, u32[]{:S(2)}, u32[]{:S(2)}) %all-to-all-start.5) | async-done | bytes 163872 | tf_op jit(solution)/shard_map/all_to_all | solution.py:45
  179.8 0.9 convert_reduce_fusion.2
  180.8 0.8 select_convert_fusion
  181.6 0.7 broadcast_in_dim.18
  182.3 4.2 %all-to-all-start.6 = ((bf16[8,80,128]{2,1,0:T(8,128)(2,1)}), bf16[8,80,128]{2,1,0:T(8,128)(2,1)}, u32[]{:S(2)}, u32[]{:S(2)}) async-start(bf16[8,80,128]{2,1,0:T(8,128)(2,1)} %broadcast_in_dim.18), calls=%async_computation.6 | async-start | bytes 327680 | tf_op jit(solution)/shard_map/all_to_all | solution.py:45
  186.5 1.2 select_bitcast_fusion.3
  187.8 0.8 convert_subtract_fusion
  188.6 1.7 copy.27
  190.3 1.7 copy.28
  192.0 1.7 copy.29
  193.7 3.5 %all-to-all-done.6 = bf16[8,80,128]{2,1,0:T(8,128)(2,1)} async-done(((bf16[8,80,128]{2,1,0:T(8,128)(2,1)}), bf16[8,80,128]{2,1,0:T(8,128)(2,1)}, u32[]{:S(2)}, u32[]{:S(2)}) %all-to-all-start.6) | async-done | bytes 163872 | tf_op jit(solution)/shard_map/all_to_all | solution.py:45
  197.2 2.4 %fusion = bf16[1,1536,128]{2,1,0:T(8,128)(2,1)} fusion(bf16[1536,640]{0,1:T(8,128)(2,1)S(1)} %pad_maximum_fusion, bf16[640,128]{1,0:T(8,128)(2,1)} %bitcast.19), kind=kOutput, calls=%fused_computation.1 | convolution fusion | flops 251854848 | bytes 2523136 | tf_op jit(solution)/shard_map/dot_general | solution.py:19
  (48 shorter events, 2.5 us)
Async XLA Ops:
  0.6 16.6 %copy-start = (bf16[1,1536,128]{2,1,0:T(8,128)(2,1)S(1)}, bf16[1,1536,128]{2,1,0:T(8,128)(2,1)}, u32[]{:S(2)}) copy-start(bf16[1,1536,128]{2,1,0:T(8,128)(2,1)} %param.8) | copy-start | bytes 1179652
  2.8 42.1 %all-to-all-start = ((bf16[64,60,128]{2,1,0:T(8,128)(2,1)}), bf16[64,60,128]{2,1,0:T(8,128)(2,1)S(1)}, u32[]{:S(2)}, u32[]{:S(2)}) async-start(bf16[64,60,128]{2,1,0:T(8,128)(2,1)} %bitcast.1), calls=%async_computation | async-start | bytes 2097152 | tf_op jit(solution)/shard_map/all_to_all | solution.py:68
  17.2 28.6 %collective-permute-start.1 = (bf16[768,128]{1,0:T(8,128)(2,1)S(1)}, bf16[768,128]{1,0:T(8,128)(2,1)S(1)}, u32[]{:S(2)}, u32[]{:S(2)}) collective-permute-start(bf16[768,128]{1,0:T(8,128)(2,1)S(1)} %dynamic-slice_bitcast_fusion.2), channel_id=1, source_target_pairs={{0,1},{1,0},{2,3},{3,2},{4,5},{5,4},{6,7},{7,6},{8,9},{9,8},{10,11... | collective-permute-start | bytes 589832 | tf_op jit(solution)/shard_map/ppermute | solution.py:51
  46.3 3.8 %collective-permute-start.2 = (f32[640,128]{0,1:T(8,128)S(1)}, f32[640,128]{0,1:T(8,128)S(1)}, u32[]{:S(2)}, u32[]{:S(2)}) collective-permute-start(f32[640,128]{0,1:T(8,128)S(1)} %convolution_bitcast_fusion), channel_id=1, source_target_pairs={{0,1},{1,0},{2,3},{3,2},{4,5},{5,4},{6,7},{7,6},{8,9},{9,8},{10,11... | collective-permute-start | bytes 983048 | tf_op jit(solution)/shard_map/ppermute | solution.py:51
  48.9 24.2 %copy-start.10 = (f32[128]{0:T(128)S(1)}, f32[128]{0:T(128)}, u32[]{:S(2)}) copy-start(f32[128]{0:T(128)} %param.9) | copy-start | bytes 1540
  49.3 27.8 %copy-start.1 = (bf16[128,1,1536]{2,0,1:T(8,128)(2,1)S(1)}, bf16[128,1,1536]{2,0,1:T(8,128)(2,1)}, u32[]{:S(2)}) copy-start(bf16[128,1,1536]{2,0,1:T(8,128)(2,1)} %param.10) | copy-start | bytes 1179652
  73.1 18.0 %copy-start.6 = (f32[80,128]{1,0:T(8,128)}, f32[80,128]{1,0:T(8,128)S(1)}, u32[]{:S(2)}) copy-start(f32[80,128]{1,0:T(8,128)S(1)} %reduce_sum.45) | copy-start | bytes 122884
  73.8 14.0 %all-to-all-start.2 = ((bf16[8,80,128]{2,1,0:T(8,128)(2,1)}), bf16[8,80,128]{2,1,0:T(8,128)(2,1)S(1)}, u32[]{:S(2)}, u32[]{:S(2)}) async-start(bf16[8,80,128]{2,1,0:T(8,128)(2,1)} %broadcast_in_dim.16), calls=%async_computation.2 | async-start | bytes 327680 | tf_op jit(solution)/shard_map/all_to_all | solution.py:45
  77.2 15.6 %copy-start.7 = (bf16[128,768]{1,0:T(8,128)(2,1)}, bf16[128,768]{1,0:T(8,128)(2,1)S(1)}, u32[]{:S(2)}) copy-start(bf16[128,768]{1,0:T(8,128)(2,1)S(1)} %get-tuple-element.29) | copy-start | bytes 589828
  77.2 12.5 %collective-permute-start.4 = (bf16[128,768]{1,0:T(8,128)(2,1)S(1)}, bf16[128,768]{1,0:T(8,128)(2,1)S(1)}, u32[]{:S(2)}, u32[]{:S(2)}) collective-permute-start(bf16[128,768]{1,0:T(8,128)(2,1)S(1)} %get-tuple-element.30), channel_id=1, source_target_pairs={{0,1},{1,0},{2,3},{3,2},{4,5},{5,4},{6,7},{7,6},{8,9},{9,8},{10,11... | collective-permute-start | bytes 589832 | tf_op jit(solution)/shard_map/ppermute | solution.py:51
  87.8 3.3 %collective-permute-start.3 = (bf16[640,128]{1,0:T(8,128)(2,1)S(1)}, bf16[640,128]{1,0:T(8,128)(2,1)S(1)}, u32[]{:S(2)}, u32[]{:S(2)}) collective-permute-start(bf16[640,128]{1,0:T(8,128)(2,1)S(1)} %bitcast.51), channel_id=1, source_target_pairs={{0,1},{1,0},{2,3},{3,2},{4,5},{5,4},{6,7},{7,6},{8,9},{9,8},{10,11... | collective-permute-start | bytes 491528 | tf_op jit(solution)/shard_map/ppermute | solution.py:51
  89.7 3.1 %copy-start.11 = (bf16[128,768]{1,0:T(8,128)(2,1)}, bf16[128,768]{1,0:T(8,128)(2,1)S(1)}, u32[]{:S(2)}) copy-start(bf16[128,768]{1,0:T(8,128)(2,1)S(1)} %collective-permute-done.4) | copy-start | bytes 589828
  91.1 1.8 copy-start.9
  92.8 32.0 %all-to-all-start.3 = ((bf16[32,40,384]{2,1,0:T(8,128)(2,1)}), bf16[32,40,384]{2,1,0:T(8,128)(2,1)S(1)}, u32[]{:S(2)}, u32[]{:S(2)}) async-start(bf16[32,40,384]{2,1,0:T(8,128)(2,1)} %bitcast.15), calls=%async_computation.3 | async-start | bytes 1966080 | tf_op jit(solution)/shard_map/all_to_all | solution.py:48
  126.1 32.2 %all-to-all-start.4 = ((bf16[32,40,384]{2,1,0:T(8,128)(2,1)}), bf16[32,40,384]{2,1,0:T(8,128)(2,1)S(1)}, u32[]{:S(2)}, u32[]{:S(2)}) async-start(bf16[32,40,384]{2,1,0:T(8,128)(2,1)} %broadcast_in_dim.17), calls=%async_computation.4 | async-start | bytes 1966080 | tf_op jit(solution)/shard_map/all_to_all | solution.py:48
  132.0 4.5 %collective-permute-start = (bf16[640,768]{1,0:T(8,128)(2,1)S(1)}, bf16[640,768]{1,0:T(8,128)(2,1)S(1)}, u32[]{:S(2)}, u32[]{:S(2)}) collective-permute-start(bf16[640,768]{1,0:T(8,128)(2,1)S(1)} %reshape.155), channel_id=1, source_target_pairs={{0,1},{1,0},{2,3},{3,2},{4,5},{5,4},{6,7},{7,6},{8,9},{9,8},{10,11... | collective-permute-start | bytes 2949128 | tf_op jit(solution)/shard_map/ppermute | solution.py:51
  158.2 0.9 copy-start.8
  158.2 1.0 copy-start.12
  159.8 3.3 %collective-permute-start.5 = (bf16[640,128]{1,0:T(8,128)(2,1)S(1)}, bf16[640,128]{1,0:T(8,128)(2,1)S(1)}, u32[]{:S(2)}, u32[]{:S(2)}) collective-permute-start(bf16[640,128]{1,0:T(8,128)(2,1)S(1)} %fusion.9), channel_id=1, source_target_pairs={{0,1},{1,0},{2,3},{3,2},{4,5},{5,4},{6,7},{7,6},{8,9},{9,8},{10,11... | collective-permute-start | bytes 491528 | tf_op jit(solution)/shard_map/ppermute | solution.py:51
  163.8 16.1 %all-to-all-start.5 = ((bf16[8,80,128]{2,1,0:T(8,128)(2,1)}), bf16[8,80,128]{2,1,0:T(8,128)(2,1)}, u32[]{:S(2)}, u32[]{:S(2)}) async-start(bf16[8,80,128]{2,1,0:T(8,128)(2,1)} %bitcast.56), calls=%async_computation.5 | async-start | bytes 327680 | tf_op jit(solution)/shard_map/all_to_all | solution.py:45
  169.2 0.9 copy-start.3
  170.1 17.6 %copy-start.2 = (bf16[128,1,1536]{2,0,1:T(8,128)(2,1)S(1)}, bf16[128,1,1536]{2,0,1:T(8,128)(2,1)}, u32[]{:S(2)}) copy-start(bf16[128,1,1536]{2,0,1:T(8,128)(2,1)} %param.10) | copy-start | bytes 1179652
  170.1 17.6 %copy-start.4 = (f32[128,1,1536]{2,1,0:T(1,128)S(1)}, f32[128,1,1536]{2,1,0:T(1,128)}, u32[]{:S(2)}) copy-start(f32[128,1,1536]{2,1,0:T(1,128)} %param.12) | copy-start | bytes 2359300
  170.9 15.6 %collective-permute-start.6 = (f32[128,768]{1,0:T(8,128)}, f32[128,768]{1,0:T(8,128)}, u32[]{:S(2)}, u32[]{:S(2)}) collective-permute-start(f32[128,768]{1,0:T(8,128)} %slice.43), channel_id=1, source_target_pairs={{0,1},{1,0},{2,3},{3,2},{4,5},{5,4},{6,7},{7,6},{8,9},{9,8},{10,11... | collective-permute-start | bytes 1179656 | tf_op jit(solution)/shard_map/ppermute | solution.py:51
  182.3 14.9 %all-to-all-start.6 = ((bf16[8,80,128]{2,1,0:T(8,128)(2,1)}), bf16[8,80,128]{2,1,0:T(8,128)(2,1)}, u32[]{:S(2)}, u32[]{:S(2)}) async-start(bf16[8,80,128]{2,1,0:T(8,128)(2,1)} %broadcast_in_dim.18), calls=%async_computation.6 | async-start | bytes 327680 | tf_op jit(solution)/shard_map/all_to_all | solution.py:45
  186.5 1.4 copy-start.5

commit v3 on v2

v3 whole, which is shorter than its diff:
```python
import jax
import jax.numpy as jnp
from jax import lax
from jax.experimental import pallas as pl
from jax.experimental.pallas import tpu as pltpu
from jax.sharding import PartitionSpec as P


sparsity_weight = 1.0
learn_rate = 0.001
beta_first = 0.9
beta_second = 0.999
corr_first = 0.6513215599
corr_second = 0.0099551198
adam_epsilon = 1e-08
norm_epsilon = 1e-06

LANES = 128
TEAM = 4


def mm(left, right, dims):
    return lax.dot_general(left, right, (dims, ((), ())), preferred_element_type=jnp.float32)


def encoder_kernel(core_ref, own_ref, other_ref, grad_ref, out_ref):
    grad = grad_ref[...].astype(jnp.float32).T.astype(jnp.bfloat16)
    for mask, half in enumerate((own_ref, other_ref)):
        term = lax.dot_general(grad, half[...], (((1,), (0,)), ((), ())), preferred_element_type=jnp.float32)
        out_ref[core_ref[0] ^ mask] = term.T.astype(jnp.bfloat16)


def encoder_grad(core, own, other, grad):
    half, lat_dev = own.shape[1], grad.shape[1]
    return pl.pallas_call(
        encoder_kernel,
        out_shape=jax.ShapeDtypeStruct((2, half, lat_dev), jnp.bfloat16),
        in_specs=[pl.BlockSpec(memory_space=pltpu.SMEM)] + [pl.BlockSpec(memory_space=pltpu.VMEM)] * 3,
        out_specs=pl.BlockSpec(memory_space=pltpu.VMEM),
        name="encoder_grad",
    )(core, own, other, grad)


def adam_kernel(place_ref, p0, p1, p2, p3, weight_ref, coef_ref, first_ref, second_ref, dec_out, first_out, second_out, term):
    lats, part = p0.shape
    tiles = TEAM * part // LANES
    for mask, piece in enumerate((p0, p1, p2, p3)):
        term[place_ref[0] ^ mask] = piece[...]
    for tile in range(tiles):
        col = tile * LANES % part
        rows = pl.ds(tile, lats, stride=tiles)
        weight = weight_ref[:, tile * LANES : (tile + 1) * LANES].astype(jnp.float32)
        grad = term[tile * LANES // part, :, col : col + LANES] + coef_ref[...] * weight
        first = beta_first * first_ref[rows, :] + (1.0 - beta_first) * grad
        second = beta_second * second_ref[rows, :] + (1.0 - beta_second) * grad * grad
        first_out[rows, :] = first
        second_out[rows, :] = second
        dec_out[rows, :] = weight - learn_rate * (first / corr_first) / (jnp.sqrt(second / corr_second) + adam_epsilon)


def adam(place, pieces, weight, coef, first, second):
    lat_dev, width = weight.shape
    part = width // TEAM
    steps = 4
    lats = lat_dev // steps
    rows = lats * width // LANES
    flat = jax.ShapeDtypeStruct((lat_dev * width // LANES, LANES), jnp.float32)
    by_lat = lambda size: pl.BlockSpec((lats, size), lambda i: (i, 0))
    by_row = pl.BlockSpec((rows, LANES), lambda i: (i, 0))
    outs = pl.pallas_call(
        adam_kernel,
        grid=(steps,),
        out_shape=(flat, flat, flat),
        in_specs=[pl.BlockSpec(memory_space=pltpu.SMEM)]
        + [by_lat(part)] * TEAM
        + [by_lat(width), by_lat(1), by_row, by_row],
        out_specs=(by_row, by_row, by_row),
        scratch_shapes=[pltpu.VMEM((TEAM, lats, part), jnp.float32)],
        name="adam",
    )(place, *pieces, weight, coef, first.reshape(flat.shape), second.reshape(flat.shape))
    return [out.reshape(lat_dev, 1, width) for out in outs]


def body(activations, enc_weight, enc_bias, dec_weight, dec_bias, dec_first, dec_second):
    snaps = lax.axis_size("snap")
    lats = lax.axis_size("lat")
    rows_dev, width = activations.shape[1:]
    lat_dev = enc_weight.shape[2]
    part = width // TEAM
    half = width // 2
    batch_rows = rows_dev * lats
    block_rows = batch_rows // snaps
    teams = lats // TEAM
    team_rows = batch_rows // teams
    scale_rec = 2.0 / batch_rows
    scale_sparse = sparsity_weight / batch_rows
    lat = lax.axis_index("lat")
    team = lax.shift_right_logical(lat, 2)
    core = lax.bitwise_and(lat, 1)
    chip = lax.bitwise_and(lax.shift_right_logical(lat, 1), 1)
    place = 2 * core + chip
    place_groups = [[t * TEAM + p for t in range(teams)] for p in range(TEAM)]
    pair_groups = [
        [c * lats + t * TEAM + 2 * z + k for z in range(2) for c in range(snaps)]
        for t in range(teams)
        for k in range(2)
    ]

    def over_snaps(x):
        return lax.all_to_all(x, "snap", 0, 0, tiled=True)

    def over_pairs(x):
        return lax.all_to_all(x, ("snap", "lat"), 0, 0, tiled=True, axis_index_groups=pair_groups)

    def over_teams(x):
        return lax.all_to_all(x, "lat", 0, 0, tiled=True, axis_index_groups=place_groups)

    def exchange(x, mask):
        return lax.ppermute(x, "lat", [(i, i ^ mask) for i in range(lats)])

    def repeat(x, times):
        return jnp.broadcast_to(x[None], (times,) + x.shape)

    def by_chip(same, other, axis):
        return jnp.concatenate(
            [jnp.where(chip == 0, same, other), jnp.where(chip == 0, other, same)], axis=axis
        )

    def split(x, axis, index):
        size = x.shape[axis] // 2
        return (
            lax.dynamic_slice_in_dim(x, index * size, size, axis),
            lax.dynamic_slice_in_dim(x, (1 - index) * size, size, axis),
        )

    CORE, CHIP = 1, 2
    rows = activations[0]
    enc_local = enc_weight[0]
    dec_local = dec_weight[:, 0, :]

    sent = rows.reshape(rows_dev, 2, half).transpose(1, 0, 2)
    sent = sent.reshape(2, rows_dev * half // LANES, LANES)
    sent = repeat(sent, lats // 2).reshape((lats,) + sent.shape[1:])
    acts = lax.all_to_all(sent, "lat", 0, 0, tiled=True)

    enc_own, give = split(enc_local, 0, core)
    enc_other = exchange(give, CORE)
    acts, enc_own, enc_other = lax.optimization_barrier((acts, enc_own, enc_other))
    acts = acts.reshape(batch_rows, half)

    dec_parts = dec_local.reshape(lat_dev, 2, 2, part)
    keep = lax.dynamic_index_in_dim(dec_parts, chip, 2, keepdims=False).reshape(lat_dev, half)
    give = lax.dynamic_index_in_dim(dec_parts, 1 - chip, 2, keepdims=False).reshape(lat_dev, half)
    dec_chips = lax.optimization_barrier(by_chip(keep, exchange(give, CHIP), 0))
    keep, give = split(dec_chips, 1, core)
    dec_other = exchange(give, CORE)
    dec_team = lax.optimization_barrier(jnp.concatenate([keep, dec_other], axis=0))
    dec_float = dec_local.astype(jnp.float32)
    own_norm = jnp.sqrt(jnp.sum(dec_float * dec_float, axis=1) + norm_epsilon)

    pre_other = exchange(mm(acts, enc_other, ((1,), (0,))), CORE)
    pre_sent = (mm(acts, enc_own, ((1,), (0,))) + pre_other).reshape(snaps, block_rows, lat_dev)
    pre = jnp.sum(over_snaps(pre_sent), axis=0) + enc_bias[None, :]

    codes_block = jnp.maximum(pre, 0.0).astype(jnp.bfloat16)
    codes_chips = over_pairs(repeat(codes_block, 2 * snaps)).reshape(2, batch_rows, lat_dev)
    codes_core = jnp.concatenate([codes_chips[0], codes_chips[1]], axis=1)
    acts_other = exchange(acts, CORE)
    codes = jnp.concatenate([codes_core, exchange(codes_core, CORE)], axis=1)

    sent = mm(codes, dec_team, ((1,), (0,))).astype(jnp.bfloat16).reshape(teams, team_rows, part)
    decoded = jnp.sum(over_teams(sent).astype(jnp.float32), axis=0)
    target = lax.dynamic_slice(acts, (team * team_rows, chip * part), (team_rows, part))
    bias_part = lax.dynamic_slice_in_dim(dec_bias[0], place * part, part, 0)
    errors_block = (decoded + bias_part[None, :] - target.astype(jnp.float32)).astype(jnp.bfloat16)
    errors = over_teams(repeat(errors_block, teams)).reshape(batch_rows, part)

    grad_other = exchange((scale_rec * mm(errors, dec_team[2 * lat_dev :], ((1,), (1,)))).astype(jnp.bfloat16), 1)
    norm_part = scale_sparse * own_norm[None, :]
    grad_sent = jnp.stack(
        [
            scale_rec * mm(errors, dec_team[z * lat_dev : (z + 1) * lat_dev], ((1,), (1,)))
            + grad_other[:, z * lat_dev : (z + 1) * lat_dev].astype(jnp.float32)
            + jnp.where(chip == z, norm_part, 0.0)
            for z in range(2)
        ],
        axis=0,
    ).astype(jnp.bfloat16)
    grad_sent = grad_sent.reshape(2 * snaps, block_rows, lat_dev)
    grad = jnp.sum(over_pairs(grad_sent).astype(jnp.float32), axis=0)
    grad_block = jnp.where(pre > 0.0, grad, 0.0).astype(jnp.bfloat16)
    grad_pre = over_snaps(repeat(grad_block, snaps)).reshape(batch_rows, lat_dev)

    acc_own = scale_rec * mm(codes[:, : 2 * lat_dev], errors, ((0,), (0,)))
    acc_give = scale_rec * mm(codes[:, 2 * lat_dev :], errors, ((0,), (0,)))
    acc_core = exchange(acc_give, CORE)
    keep, give = split(jnp.stack([acc_own, acc_core], axis=0), 1, chip)
    acc_chip = exchange(give, CHIP)
    own_codes = lax.dynamic_index_in_dim(codes_chips, chip, 0, keepdims=False)
    code_total = jnp.sum(own_codes.astype(jnp.float32), axis=0)
    coef = (scale_sparse * code_total / own_norm)[:, None]
    pieces = (keep[0], acc_chip[0], keep[1], acc_chip[1])
    new_decoder, new_first, new_second = adam(place.reshape(1), pieces, dec_local, coef, dec_first, dec_second)

    enc_grad = encoder_grad(core.reshape(1), acts, acts_other, grad_pre).reshape(1, width, lat_dev)
    return (enc_grad, new_decoder, new_first, new_second)


def solution(mesh):
    in_specs = (
        P("snap", "lat", None),
        P("snap", None, "lat"),
        P("lat"),
        P("lat", "snap", None),
        P("snap", None),
        P("lat", "snap", None),
        P("lat", "snap", None),
    )
    out_specs = (
        P("snap", None, "lat"),
        P("lat", "snap", None),
        P("lat", "snap", None),
        P("lat", "snap", None),
    )

    return jax.shard_map(body, mesh=mesh, in_specs=in_specs, out_specs=out_specs, check_vma=False)
```

time: 201 us -> 193 us (0.960)
  blocking collectives: 22.7 us -> 0 us
  starting transfers between devices: 51.9 us -> 67.9 us
  Pallas kernels: 0 us -> 7.3 us
  local copies, waits for them, and re-layouts: 14.3 us -> 8.67 us
  other arithmetic: 7.43 us -> 2.49 us
  waiting for transfers between devices: 96.4 us -> 99.1 us
    all_to_all x1 -> x0, blocking collectives: 22.7 us -> none  [over_snaps(): return lax.all_to_all(x, 'snap', 0, 0, tiled=True)]
    ppermute x7 -> x9, starting transfers between devices: 14.3 us -> 22.9 us  [exchange(): return lax.ppermute(x, 'lat', [(i, i ^ mask) for i in range(lats)])]
    all_to_all x3 -> x5, starting transfers between devices: 26 us -> 34.2 us  [the longest x1 14.5 us: body(): acts = lax.all_to_all(sent, 'lat', 0, 0, tiled=True)]
    pallas_call x0 -> x2, Pallas kernels: none -> 7.3 us  [the longest x1 4.45 us: adam(): pl.pallas_call(adam_kernel, grid=(steps,), out_shape=(flat, flat, flat),...]
    unnamed x29 -> x19, local copies, waits for them, and re-layouts: 6.99 us -> 0.92 us
    ppermute x7 -> x9, waiting for transfers between devices: 4.64 us -> 9.79 us  [exchange(): return lax.ppermute(x, 'lat', [(i, i ^ mask) for i in range(lats)])]
    all_to_all x3 -> x5, waiting for transfers between devices: 72.7 us -> 68.3 us  [the longest x2 33.7 us: over_teams(): lax.all_to_all(x, 'lat', 0, 0, tiled=True, axis_index_groups=place_groups)]
    all_to_all x3 -> x2, waiting for transfers between devices: 19 us -> 21 us  [over_snaps(): return lax.all_to_all(x, 'snap', 0, 0, tiled=True)]
  transfers between devices with their start and end apart: 13 -> 16, of which waited for: 10 -> 12; matrix products, arithmetic and copies ran while one was open for 8% -> 3% of each run, Pallas kernels for 0% -> 2%
where the time goes in v3:
time: 193 us; the launch traced here: 192 us
  waiting for transfers between devices  99.1 us (51%)
  starting transfers between devices  67.9 us (35%)
  local copies, waits for them, and re-layouts  8.67 us (4%)
  Pallas kernels  7.3 us (4%)
  matrix products  5.3 us (3%)
  other arithmetic  2.49 us (1%)
    all_to_all x2, waiting for transfers between devices, over_teams(): lax.all_to_all(x, 'lat', 0, 0, tiled=True, axis_index_groups=place_groups)  33.7 us
    all_to_all x1, waiting for transfers between devices, body(): acts = lax.all_to_all(sent, 'lat', 0, 0, tiled=True)  24.4 us
    ppermute x9, starting transfers between devices, exchange(): return lax.ppermute(x, 'lat', [(i, i ^ mask) for i in range(lats)])  22.9 us
    all_to_all x2, waiting for transfers between devices, over_snaps(): return lax.all_to_all(x, 'snap', 0, 0, tiled=True)  21 us
    all_to_all x1, starting transfers between devices, body(): acts = lax.all_to_all(sent, 'lat', 0, 0, tiled=True)  14.5 us
    all_to_all x2, starting transfers between devices, over_teams(): lax.all_to_all(x, 'lat', 0, 0, tiled=True, axis_index_groups=place_groups)  11 us
    all_to_all x2, starting transfers between devices, over_snaps(): return lax.all_to_all(x, 'snap', 0, 0, tiled=True)  10.9 us
    all_to_all x2, waiting for transfers between devices, over_pairs(): lax.all_to_all(x, ('snap', 'lat'), 0, 0, tiled=True, axis_index_groups=pa...  10.2 us
  transfers between devices with their start and end apart: 16, of which 12 were waited for; matrix products, arithmetic and copies ran while one was open for 3% of the time, Pallas kernels for 2%

profile of v3, /device:TPU:16, one launch (start us, length us, event | category | flops | bytes accessed | tf_op | source)
XLA Modules:
  0.0 191.8 jit_solution(7440621971351534524)
XLA Ops:
  0.6 0.8 reshape_squeeze.6
  1.5 1.2 broadcast_in_dim.18
  2.8 14.5 %all-to-all-start = ((bf16[64,60,128]{2,1,0:T(8,128)(2,1)}), bf16[64,60,128]{2,1,0:T(8,128)(2,1)S(1)}, u32[]{:S(2)}, u32[]{:S(2)}) async-start(bf16[64,60,128]{2,1,0:T(8,128)(2,1)} %bitcast.2), calls=%async_computation | async-start | bytes 2097152 | tf_op jit(solution)/shard_map/all_to_all | solution.py:144
  17.3 2.0 %collective-permute-start = (bf16[768,128]{1,0:T(8,128)(2,1)S(1)}, bf16[768,128]{1,0:T(8,128)(2,1)S(1)}, u32[]{:S(2)}, u32[]{:S(2)}) collective-permute-start(bf16[768,128]{1,0:T(8,128)(2,1)S(1)} %get-tuple-element.44), channel_id=1, source_target_pairs={{0,1},{1,0},{2,3},{3,2},{4,5},{5,4},{6,7},{7,6},{8,9},{9,8},{10,11... | collective-permute-start | bytes 589832 | tf_op jit(solution)/shard_map/ppermute | solution.py:119
  19.4 1.3 collective-permute-done
  20.7 24.4 %all-to-all-done = bf16[64,60,128]{2,1,0:T(8,128)(2,1)S(1)} async-done(((bf16[64,60,128]{2,1,0:T(8,128)(2,1)}), bf16[64,60,128]{2,1,0:T(8,128)(2,1)S(1)}, u32[]{:S(2)}, u32[]{:S(2)}) %all-to-all-start) | async-done | bytes 983072 | tf_op jit(solution)/shard_map/all_to_all | solution.py:144
  45.0 0.9 reshape.155.own_ref
  45.9 0.4 fusion.23
  46.4 2.7 %collective-permute-start.2 = (f32[640,128]{1,0:T(8,128)S(1)}, f32[640,128]{1,0:T(8,128)S(1)}, u32[]{:S(2)}, u32[]{:S(2)}) collective-permute-start(f32[640,128]{1,0:T(8,128)S(1)} %fusion.23), channel_id=1, source_target_pairs={{0,1},{1,0},{2,3},{3,2},{4,5},{5,4},{6,7},{7,6},{8,9},{9,8},{10,11... | collective-permute-start | bytes 983048 | tf_op jit(solution)/shard_map/ppermute | solution.py:119
  49.1 1.2 collective-permute-done.2
  50.3 1.1 convolution_add_fusion
  51.5 7.0 %all-to-all-start.1 = ((f32[8,80,128]{2,1,0:T(8,128)}), f32[8,80,128]{2,1,0:T(8,128)S(1)}, u32[]{:S(2)}, u32[]{:S(2)}) async-start(f32[8,80,128]{2,1,0:T(8,128)} %bitcast.5), calls=%async_computation.1 | async-start | bytes 655360 | tf_op jit(solution)/shard_map/all_to_all | solution.py:110
  58.7 15.3 %all-to-all-done.1 = f32[8,80,128]{2,1,0:T(8,128)S(1)} async-done(((f32[8,80,128]{2,1,0:T(8,128)}), f32[8,80,128]{2,1,0:T(8,128)S(1)}, u32[]{:S(2)}, u32[]{:S(2)}) %all-to-all-start.1) | async-done | bytes 327712 | tf_op jit(solution)/shard_map/all_to_all | solution.py:110
  74.0 0.8 broadcast_in_dim.19
  74.8 3.5 %all-to-all-start.2 = ((bf16[16,80,128]{2,1,0:T(8,128)(2,1)}), bf16[16,80,128]{2,1,0:T(8,128)(2,1)S(1)}, u32[]{:S(2)}, u32[]{:S(2)}) async-start(bf16[16,80,128]{2,1,0:T(8,128)(2,1)} %broadcast_in_dim.19), calls=%async_computation.2 | async-start | bytes 655360 | tf_op jit(solution)/shard_map/all_to_all | solution.py:113
  78.4 3.7 %collective-permute-start.4 = (bf16[128,768]{0,1:T(8,128)(2,1)S(1)}, bf16[128,768]{0,1:T(8,128)(2,1)S(1)}, u32[]{:S(2)}, u32[]{:S(2)}) collective-permute-start(bf16[128,768]{0,1:T(8,128)(2,1)S(1)} %bitcast.78), channel_id=1, source_target_pairs={{0,2},{1,3},{2,0},{3,1},{4,6},{5,7},{6,4},{7,5},{8,10},{9,11},{10,... | collective-permute-start | bytes 589832 | tf_op jit(solution)/shard_map/ppermute | solution.py:119
  82.2 4.9 %collective-permute-done.4 = bf16[128,768]{0,1:T(8,128)(2,1)S(1)} collective-permute-done((bf16[128,768]{0,1:T(8,128)(2,1)S(1)}, bf16[128,768]{0,1:T(8,128)(2,1)S(1)}, u32[]{:S(2)}, u32[]{:S(2)}) %collective-permute-start.4) | collective-permute-done | bytes 196640 | tf_op jit(solution)/shard_map/ppermute | solution.py:119
  87.2 5.0 %all-to-all-done.2 = bf16[16,80,128]{2,1,0:T(8,128)(2,1)S(1)} async-done(((bf16[16,80,128]{2,1,0:T(8,128)(2,1)}), bf16[16,80,128]{2,1,0:T(8,128)(2,1)S(1)}, u32[]{:S(2)}, u32[]{:S(2)}) %all-to-all-start.2) | async-done | bytes 327712 | tf_op jit(solution)/shard_map/all_to_all | solution.py:113
  92.2 1.9 %collective-permute-start.3 = (bf16[640,256]{1,0:T(8,128)(2,1)S(1)}, bf16[640,256]{1,0:T(8,128)(2,1)S(1)}, u32[]{:S(2)}, u32[]{:S(2)}) collective-permute-start(bf16[640,256]{1,0:T(8,128)(2,1)S(1)} %pad_maximum_fusion.2), channel_id=1, source_target_pairs={{0,1},{1,0},{2,3},{3,2},{4,5},{5,4},{6,7},{7,6},{8,9},{9,8},{10,11... | collective-permute-start | bytes 983048 | tf_op jit(solution)/shard_map/ppermute | solution.py:119
  94.2 2.4 %collective-permute-start.5 = (bf16[256,384]{0,1:T(8,128)(2,1)S(1)}, bf16[256,384]{0,1:T(8,128)(2,1)S(1)}, u32[]{:S(2)}, u32[]{:S(2)}) collective-permute-start(bf16[256,384]{0,1:T(8,128)(2,1)S(1)} %get-tuple-element.39), channel_id=1, source_target_pairs={{0,1},{1,0},{2,3},{3,2},{4,5},{5,4},{6,7},{7,6},{8,9},{9,8},{10,11... | collective-permute-start | bytes 589832 | tf_op jit(solution)/shard_map/ppermute | solution.py:119
  96.6 1.0 collective-permute-done.5
  97.7 1.3 convolution_convert_fusion
  99.0 6.2 %all-to-all-start.3 = ((bf16[16,40,384]{2,1,0:T(8,128)(2,1)}), bf16[16,40,384]{2,1,0:T(8,128)(2,1)S(1)}, u32[]{:S(2)}, u32[]{:S(2)}) async-start(bf16[16,40,384]{2,1,0:T(8,128)(2,1)} %bitcast.11), calls=%async_computation.3 | async-start | bytes 983040 | tf_op jit(solution)/shard_map/all_to_all | solution.py:116
  105.3 17.1 %all-to-all-done.3 = bf16[16,40,384]{2,1,0:T(8,128)(2,1)S(1)} async-done(((bf16[16,40,384]{2,1,0:T(8,128)(2,1)}), bf16[16,40,384]{2,1,0:T(8,128)(2,1)S(1)}, u32[]{:S(2)}, u32[]{:S(2)}) %all-to-all-start.3) | async-done | bytes 491552 | tf_op jit(solution)/shard_map/all_to_all | solution.py:116
  122.4 0.8 broadcast_in_dim.20
  123.2 4.8 %all-to-all-start.4 = ((bf16[16,40,384]{2,1,0:T(8,128)(2,1)}), bf16[16,40,384]{2,1,0:T(8,128)(2,1)S(1)}, u32[]{:S(2)}, u32[]{:S(2)}) async-start(bf16[16,40,384]{2,1,0:T(8,128)(2,1)} %broadcast_in_dim.20), calls=%async_computation.4 | async-start | bytes 983040 | tf_op jit(solution)/shard_map/all_to_all | solution.py:116
  128.1 16.7 %all-to-all-done.4 = bf16[16,40,384]{2,1,0:T(8,128)(2,1)S(1)} async-done(((bf16[16,40,384]{2,1,0:T(8,128)(2,1)}), bf16[16,40,384]{2,1,0:T(8,128)(2,1)S(1)}, u32[]{:S(2)}, u32[]{:S(2)}) %all-to-all-start.4) | async-done | bytes 491552 | tf_op jit(solution)/shard_map/all_to_all | solution.py:116
  144.7 0.3 fusion
  145.0 1.9 %collective-permute-start.6 = (bf16[640,256]{1,0:T(8,128)(2,1)S(1)}, bf16[640,256]{1,0:T(8,128)(2,1)S(1)}, u32[]{:S(2)}, u32[]{:S(2)}) collective-permute-start(bf16[640,256]{1,0:T(8,128)(2,1)S(1)} %fusion), channel_id=1, source_target_pairs={{0,1},{1,0},{2,3},{3,2},{4,5},{5,4},{6,7},{7,6},{8,9},{9,8},{10,11... | collective-permute-start | bytes 983048 | tf_op jit(solution)/shard_map/ppermute | solution.py:119
  147.2 1.3 collective-permute-done.6
  149.2 0.8 pad_maximum_fusion.3
  149.9 5.1 %all-to-all-start.5 = ((bf16[16,80,128]{2,1,0:T(8,128)(2,1)}), bf16[16,80,128]{2,1,0:T(8,128)(2,1)S(1)}, u32[]{:S(2)}, u32[]{:S(2)}) async-start(bf16[16,80,128]{2,1,0:T(8,128)(2,1)} %bitcast.16), calls=%async_computation.5 | async-start | bytes 655360 | tf_op jit(solution)/shard_map/all_to_all | solution.py:113
  155.1 1.1 convolution_multiply_fusion.1
  156.2 1.9 collective-permute-start.7
  158.2 2.4 %collective-permute-start.1 = (bf16[640,768]{1,0:T(8,128)(2,1)S(1)}, bf16[640,768]{1,0:T(8,128)(2,1)S(1)}, u32[]{:S(2)}, u32[]{:S(2)}) collective-permute-start(bf16[640,768]{1,0:T(8,128)(2,1)S(1)} %reshape.155.own_ref), channel_id=1, source_target_pairs={{0,1},{1,0},{2,3},{3,2},{4,5},{5,4},{6,7},{7,6},{8,9},{9,8},{10,11... | collective-permute-start | bytes 2949128 | tf_op jit(solution)/shard_map/ppermute | solution.py:119
  160.6 0.7 copy.28.coef_ref
  161.3 0.4 fusion.1
  161.7 1.1 fusion.15
  162.8 3.8 %collective-permute-start.8 = (f32[2,128,384]{2,1,0:T(8,128)S(1)}, f32[2,128,384]{2,1,0:T(8,128)S(1)}, u32[]{:S(2)}, u32[]{:S(2)}) collective-permute-start(f32[2,128,384]{2,1,0:T(8,128)S(1)} %get-tuple-element.32), channel_id=1, source_target_pairs={{0,2},{1,3},{2,0},{3,1},{4,6},{5,7},{6,4},{7,5},{8,10},{9,11},{10,... | collective-permute-start | bytes 1179656 | tf_op jit(solution)/shard_map/ppermute | solution.py:119
  166.7 5.2 %all-to-all-done.5 = bf16[16,80,128]{2,1,0:T(8,128)(2,1)S(1)} async-done(((bf16[16,80,128]{2,1,0:T(8,128)(2,1)}), bf16[16,80,128]{2,1,0:T(8,128)(2,1)S(1)}, u32[]{:S(2)}, u32[]{:S(2)}) %all-to-all-start.5) | async-done | bytes 327712 | tf_op jit(solution)/shard_map/all_to_all | solution.py:113
  171.9 0.7 broadcast_in_dim.22
  172.6 3.9 %all-to-all-start.6 = ((bf16[8,80,128]{2,1,0:T(8,128)(2,1)}), bf16[8,80,128]{2,1,0:T(8,128)(2,1)S(1)}, u32[]{:S(2)}, u32[]{:S(2)}) async-start(bf16[8,80,128]{2,1,0:T(8,128)(2,1)} %broadcast_in_dim.22), calls=%async_computation.6 | async-start | bytes 327680 | tf_op jit(solution)/shard_map/all_to_all | solution.py:110
  176.5 0.8 slice_bitcast_fusion.1
  177.3 0.8 slice_bitcast_fusion
  178.0 4.5 %adam.1 = (f32[1536,128]{1,0:T(8,128)}, f32[1536,128]{1,0:T(8,128)}, f32[1536,128]{1,0:T(8,128)}) custom-call(s32[1]{0:T(128)} %bitcast.19.place_ref, f32[128,384]{1,0:T(8,128)} %get-tuple-element.37.p0, f32[128,384]{1,0:T(8,128)} %get-tuple-element.35.p1, f32[128,384]{1,0:T(8,128)} %get-tuple-element.36.p2, f32[128,384]{1,0:T(8,128)} %get-tuple-element.34.p3, ...), custom_call_target="tpu_custom_call" | custom-call | tf_op jit(solution)/shard_map/adam/pallas_call | solution.py:70
  182.5 5.7 %all-to-all-done.6 = bf16[8,80,128]{2,1,0:T(8,128)(2,1)S(1)} async-done(((bf16[8,80,128]{2,1,0:T(8,128)(2,1)}), bf16[8,80,128]{2,1,0:T(8,128)(2,1)S(1)}, u32[]{:S(2)}, u32[]{:S(2)}) %all-to-all-start.6) | async-done | bytes 163872 | tf_op jit(solution)/shard_map/all_to_all | solution.py:110
  188.3 0.7 copy-done.4
  188.9 2.8 %encoder_grad.1 = bf16[2,768,128]{2,1,0:T(8,128)(2,1)} custom-call(s32[1]{0:T(128)} %bitcast.core_ref, bf16[640,768]{1,0:T(8,128)(2,1)} %copy-done.1, bf16[640,768]{1,0:T(8,128)(2,1)} %copy-done.3, bf16[640,128]{1,0:T(8,128)(2,1)} %bitcast.75), custom_call_target="tpu_custom_call" | custom-call | tf_op jit(solution)/shard_map/encoder_grad/pallas_call | solution.py:35
  (44 shorter events, 1.7 us)
Async XLA Ops:
  0.6 104.6 %copy-start = (f32[1,1536]{1,0:T(1,128)S(1)}, f32[1,1536]{1,0:T(1,128)}, u32[]{:S(2)}) copy-start(f32[1,1536]{1,0:T(1,128)} %param.11) | copy-start | bytes 18436
  2.8 14.5 %copy-start.5 = (bf16[1,1536,128]{2,1,0:T(8,128)(2,1)S(1)}, bf16[1,1536,128]{2,1,0:T(8,128)(2,1)}, u32[]{:S(2)}) copy-start(bf16[1,1536,128]{2,1,0:T(8,128)(2,1)} %param.8) | copy-start | bytes 1179652
  2.8 42.2 %all-to-all-start = ((bf16[64,60,128]{2,1,0:T(8,128)(2,1)}), bf16[64,60,128]{2,1,0:T(8,128)(2,1)S(1)}, u32[]{:S(2)}, u32[]{:S(2)}) async-start(bf16[64,60,128]{2,1,0:T(8,128)(2,1)} %bitcast.2), calls=%async_computation | async-start | bytes 2097152 | tf_op jit(solution)/shard_map/all_to_all | solution.py:144
  17.3 3.3 %collective-permute-start = (bf16[768,128]{1,0:T(8,128)(2,1)S(1)}, bf16[768,128]{1,0:T(8,128)(2,1)S(1)}, u32[]{:S(2)}, u32[]{:S(2)}) collective-permute-start(bf16[768,128]{1,0:T(8,128)(2,1)S(1)} %get-tuple-element.44), channel_id=1, source_target_pairs={{0,1},{1,0},{2,3},{3,2},{4,5},{5,4},{6,7},{7,6},{8,9},{9,8},{10,11... | collective-permute-start | bytes 589832 | tf_op jit(solution)/shard_map/ppermute | solution.py:119
  45.9 112.2 %copy-start.1 = (bf16[640,768]{1,0:T(8,128)(2,1)}, bf16[640,768]{1,0:T(8,128)(2,1)S(1)}, u32[]{:S(2)}) copy-start(bf16[640,768]{1,0:T(8,128)(2,1)S(1)} %reshape.155.own_ref) | copy-start | bytes 2949124
  46.4 12.1 %copy-start.2 = (bf16[128,1,1536]{2,0,1:T(8,128)(2,1)S(1)}, bf16[128,1,1536]{2,0,1:T(8,128)(2,1)}, u32[]{:S(2)}) copy-start(bf16[128,1,1536]{2,0,1:T(8,128)(2,1)} %param.10) | copy-start | bytes 1179652
  46.4 3.9 %collective-permute-start.2 = (f32[640,128]{1,0:T(8,128)S(1)}, f32[640,128]{1,0:T(8,128)S(1)}, u32[]{:S(2)}, u32[]{:S(2)}) collective-permute-start(f32[640,128]{1,0:T(8,128)S(1)} %fusion.23), channel_id=1, source_target_pairs={{0,1},{1,0},{2,3},{3,2},{4,5},{5,4},{6,7},{7,6},{8,9},{9,8},{10,11... | collective-permute-start | bytes 983048 | tf_op jit(solution)/shard_map/ppermute | solution.py:119
  51.5 22.5 %copy-start.8 = (f32[128]{0:T(128)S(1)}, f32[128]{0:T(128)}, u32[]{:S(2)}) copy-start(f32[128]{0:T(128)} %param.9) | copy-start | bytes 1540
  51.5 22.5 %all-to-all-start.1 = ((f32[8,80,128]{2,1,0:T(8,128)}), f32[8,80,128]{2,1,0:T(8,128)S(1)}, u32[]{:S(2)}, u32[]{:S(2)}) async-start(f32[8,80,128]{2,1,0:T(8,128)} %bitcast.5), calls=%async_computation.1 | async-start | bytes 655360 | tf_op jit(solution)/shard_map/all_to_all | solution.py:110
  74.8 17.3 %all-to-all-start.2 = ((bf16[16,80,128]{2,1,0:T(8,128)(2,1)}), bf16[16,80,128]{2,1,0:T(8,128)(2,1)S(1)}, u32[]{:S(2)}, u32[]{:S(2)}) async-start(bf16[16,80,128]{2,1,0:T(8,128)(2,1)} %broadcast_in_dim.19), calls=%async_computation.2 | async-start | bytes 655360 | tf_op jit(solution)/shard_map/all_to_all | solution.py:113
  78.4 8.7 %collective-permute-start.4 = (bf16[128,768]{0,1:T(8,128)(2,1)S(1)}, bf16[128,768]{0,1:T(8,128)(2,1)S(1)}, u32[]{:S(2)}, u32[]{:S(2)}) collective-permute-start(bf16[128,768]{0,1:T(8,128)(2,1)S(1)} %bitcast.78), channel_id=1, source_target_pairs={{0,2},{1,3},{2,0},{3,1},{4,6},{5,7},{6,4},{7,5},{8,10},{9,11},{10,... | collective-permute-start | bytes 589832 | tf_op jit(solution)/shard_map/ppermute | solution.py:119
  92.2 5.5 %collective-permute-start.3 = (bf16[640,256]{1,0:T(8,128)(2,1)S(1)}, bf16[640,256]{1,0:T(8,128)(2,1)S(1)}, u32[]{:S(2)}, u32[]{:S(2)}) collective-permute-start(bf16[640,256]{1,0:T(8,128)(2,1)S(1)} %pad_maximum_fusion.2), channel_id=1, source_target_pairs={{0,1},{1,0},{2,3},{3,2},{4,5},{5,4},{6,7},{7,6},{8,9},{9,8},{10,11... | collective-permute-start | bytes 983048 | tf_op jit(solution)/shard_map/ppermute | solution.py:119
  94.2 3.5 %collective-permute-start.5 = (bf16[256,384]{0,1:T(8,128)(2,1)S(1)}, bf16[256,384]{0,1:T(8,128)(2,1)S(1)}, u32[]{:S(2)}, u32[]{:S(2)}) collective-permute-start(bf16[256,384]{0,1:T(8,128)(2,1)S(1)} %get-tuple-element.39), channel_id=1, source_target_pairs={{0,1},{1,0},{2,3},{3,2},{4,5},{5,4},{6,7},{7,6},{8,9},{9,8},{10,11... | collective-permute-start | bytes 589832 | tf_op jit(solution)/shard_map/ppermute | solution.py:119
  97.7 1.3 copy-start.6
  99.0 23.3 %all-to-all-start.3 = ((bf16[16,40,384]{2,1,0:T(8,128)(2,1)}), bf16[16,40,384]{2,1,0:T(8,128)(2,1)S(1)}, u32[]{:S(2)}, u32[]{:S(2)}) async-start(bf16[16,40,384]{2,1,0:T(8,128)(2,1)} %bitcast.11), calls=%async_computation.3 | async-start | bytes 983040 | tf_op jit(solution)/shard_map/all_to_all | solution.py:116
  123.2 21.5 %all-to-all-start.4 = ((bf16[16,40,384]{2,1,0:T(8,128)(2,1)}), bf16[16,40,384]{2,1,0:T(8,128)(2,1)S(1)}, u32[]{:S(2)}, u32[]{:S(2)}) async-start(bf16[16,40,384]{2,1,0:T(8,128)(2,1)} %broadcast_in_dim.20), calls=%async_computation.4 | async-start | bytes 983040 | tf_op jit(solution)/shard_map/all_to_all | solution.py:116
  145.0 3.5 %collective-permute-start.6 = (bf16[640,256]{1,0:T(8,128)(2,1)S(1)}, bf16[640,256]{1,0:T(8,128)(2,1)S(1)}, u32[]{:S(2)}, u32[]{:S(2)}) collective-permute-start(bf16[640,256]{1,0:T(8,128)(2,1)S(1)} %fusion), channel_id=1, source_target_pairs={{0,1},{1,0},{2,3},{3,2},{4,5},{5,4},{6,7},{7,6},{8,9},{9,8},{10,11... | collective-permute-start | bytes 983048 | tf_op jit(solution)/shard_map/ppermute | solution.py:119
  148.9 6.2 %copy-start.7 = (bf16[640,256]{1,0:T(8,128)(2,1)S(1)}, bf16[640,256]{1,0:T(8,128)(2,1)}, u32[]{:S(2)}) copy-start(bf16[640,256]{1,0:T(8,128)(2,1)} %copy-done.6) | copy-start | bytes 983044
  149.9 21.9 %all-to-all-start.5 = ((bf16[16,80,128]{2,1,0:T(8,128)(2,1)}), bf16[16,80,128]{2,1,0:T(8,128)(2,1)S(1)}, u32[]{:S(2)}, u32[]{:S(2)}) async-start(bf16[16,80,128]{2,1,0:T(8,128)(2,1)} %bitcast.16), calls=%async_computation.5 | async-start | bytes 655360 | tf_op jit(solution)/shard_map/all_to_all | solution.py:113
  156.2 5.5 %collective-permute-start.7 = (f32[256,384]{1,0:T(8,128)}, f32[256,384]{1,0:T(8,128)}, u32[]{:S(2)}, u32[]{:S(2)}) collective-permute-start(f32[256,384]{1,0:T(8,128)} %convolution_multiply_fusion.1), channel_id=1, source_target_pairs={{0,1},{1,0},{2,3},{3,2},{4,5},{5,4},{6,7},{7,6},{8,9},{9,8},{10,11... | collective-permute-start | bytes 1179656 | tf_op jit(solution)/shard_map/ppermute | solution.py:119
  158.2 24.3 %collective-permute-start.1 = (bf16[640,768]{1,0:T(8,128)(2,1)S(1)}, bf16[640,768]{1,0:T(8,128)(2,1)S(1)}, u32[]{:S(2)}, u32[]{:S(2)}) collective-permute-start(bf16[640,768]{1,0:T(8,128)(2,1)S(1)} %reshape.155.own_ref), channel_id=1, source_target_pairs={{0,1},{1,0},{2,3},{3,2},{4,5},{5,4},{6,7},{7,6},{8,9},{9,8},{10,11... | collective-permute-start | bytes 2949128 | tf_op jit(solution)/shard_map/ppermute | solution.py:119
  162.8 14.5 %collective-permute-start.8 = (f32[2,128,384]{2,1,0:T(8,128)S(1)}, f32[2,128,384]{2,1,0:T(8,128)S(1)}, u32[]{:S(2)}, u32[]{:S(2)}) collective-permute-start(f32[2,128,384]{2,1,0:T(8,128)S(1)} %get-tuple-element.32), channel_id=1, source_target_pairs={{0,2},{1,3},{2,0},{3,1},{4,6},{5,7},{6,4},{7,5},{8,10},{9,11},{10,... | collective-permute-start | bytes 1179656 | tf_op jit(solution)/shard_map/ppermute | solution.py:119
  172.6 15.6 %all-to-all-start.6 = ((bf16[8,80,128]{2,1,0:T(8,128)(2,1)}), bf16[8,80,128]{2,1,0:T(8,128)(2,1)S(1)}, u32[]{:S(2)}, u32[]{:S(2)}) async-start(bf16[8,80,128]{2,1,0:T(8,128)(2,1)} %broadcast_in_dim.22), calls=%async_computation.6 | async-start | bytes 327680 | tf_op jit(solution)/shard_map/all_to_all | solution.py:110
  182.5 5.8 %copy-start.3 = (bf16[640,768]{1,0:T(8,128)(2,1)}, bf16[640,768]{1,0:T(8,128)(2,1)S(1)}, u32[]{:S(2)}) copy-start(bf16[640,768]{1,0:T(8,128)(2,1)S(1)} %collective-permute-done.1.other_ref) | copy-start | bytes 2949124
  188.2 0.7 copy-start.4

commit v4 on v3

--- a/solution.py
+++ b/solution.py
@@ -37,6 +37,7 @@
         out_shape=jax.ShapeDtypeStruct((2, half, lat_dev), jnp.bfloat16),
         in_specs=[pl.BlockSpec(memory_space=pltpu.SMEM)] + [pl.BlockSpec(memory_space=pltpu.VMEM)] * 3,
         out_specs=pl.BlockSpec(memory_space=pltpu.VMEM),
+        compiler_params=pltpu.CompilerParams(vmem_limit_bytes=12 << 20),
         name="encoder_grad",
     )(core, own, other, grad)
 
@@ -76,6 +77,7 @@
         + [by_lat(width), by_lat(1), by_row, by_row],
         out_specs=(by_row, by_row, by_row),
         scratch_shapes=[pltpu.VMEM((TEAM, lats, part), jnp.float32)],
+        compiler_params=pltpu.CompilerParams(vmem_limit_bytes=12 << 20),
         name="adam",
     )(place, *pieces, weight, coef, first.reshape(flat.shape), second.reshape(flat.shape))
     return [out.reshape(lat_dev, 1, width) for out in outs]
@@ -95,13 +97,17 @@
     scale_rec = 2.0 / batch_rows
     scale_sparse = sparsity_weight / batch_rows
     lat = lax.axis_index("lat")
-    team = lax.shift_right_logical(lat, 2)
     core = lax.bitwise_and(lat, 1)
-    chip = lax.bitwise_and(lax.shift_right_logical(lat, 1), 1)
+    chip = lax.bitwise_and(lax.shift_right_logical(lat, 4), 1)
+    team = lax.bitwise_and(lax.shift_right_logical(lat, 1), 7) + 8 * lax.shift_right_logical(lat, 5)
     place = 2 * core + chip
-    place_groups = [[t * TEAM + p for t in range(teams)] for p in range(TEAM)]
+
+    def member(team, chip, core):
+        return 32 * (team // 8) + 16 * chip + 2 * (team % 8) + core
+
+    place_groups = [[member(t, z, k) for t in range(teams)] for k in range(2) for z in range(2)]
     pair_groups = [
-        [c * lats + t * TEAM + 2 * z + k for z in range(2) for c in range(snaps)]
+        [c * lats + member(t, z, k) for z in range(2) for c in range(snaps)]
         for t in range(teams)
         for k in range(2)
     ]
@@ -133,7 +139,7 @@
             lax.dynamic_slice_in_dim(x, (1 - index) * size, size, axis),
         )
 
-    CORE, CHIP = 1, 2
+    CORE, CHIP = 1, 16
     rows = activations[0]
     enc_local = enc_weight[0]
     dec_local = dec_weight[:, 0, :]

time: 193 us -> 192 us (level)
  the two profiles are of different devices: /device:TPU:16 before, /device:TPU:8 now
where the time goes in v4:
time: 192 us; the launch traced here: 191 us
  waiting for transfers between devices  93.7 us (49%)
  starting transfers between devices  74.7 us (39%)
  local copies, waits for them, and re-layouts  8.01 us (4%)
  matrix products  6.22 us (3%)
  Pallas kernels  3.69 us (2%)
  other arithmetic  3.35 us (2%)
    all_to_all x2, waiting for transfers between devices, over_teams(): lax.all_to_all(x, 'lat', 0, 0, tiled=True, axis_index_groups=place_groups)  28.5 us
    all_to_all x1, waiting for transfers between devices, body(): acts = lax.all_to_all(sent, 'lat', 0, 0, tiled=True)  23.1 us
    all_to_all x2, waiting for transfers between devices, over_snaps(): return lax.all_to_all(x, 'snap', 0, 0, tiled=True)  22.2 us
    ppermute x9, starting transfers between devices, exchange(): return lax.ppermute(x, 'lat', [(i, i ^ mask) for i in range(lats)])  19.9 us
    all_to_all x1, starting transfers between devices, body(): acts = lax.all_to_all(sent, 'lat', 0, 0, tiled=True)  14.5 us
    all_to_all x2, starting transfers between devices, over_pairs(): lax.all_to_all(x, ('snap', 'lat'), 0, 0, tiled=True, axis_index_groups=pa...  13.8 us
    ppermute x9, waiting for transfers between devices, exchange(): return lax.ppermute(x, 'lat', [(i, i ^ mask) for i in range(lats)])  13.7 us
    all_to_all x2, starting transfers between devices, over_snaps(): return lax.all_to_all(x, 'snap', 0, 0, tiled=True)  13.4 us
  transfers between devices with their start and end apart: 16, of which 12 were waited for; matrix products, arithmetic and copies ran while one was open for 4% of the time, Pallas kernels for 1%

profile of v4, /device:TPU:8, one launch (start us, length us, event | category | flops | bytes accessed | tf_op | source)
XLA Modules:
  0.0 190.7 jit_solution(777747810208197318)
XLA Ops:
  0.6 0.8 reshape_squeeze.6
  1.5 1.2 broadcast_in_dim.18
  2.8 14.5 %all-to-all-start = ((bf16[64,60,128]{2,1,0:T(8,128)(2,1)}), bf16[64,60,128]{2,1,0:T(8,128)(2,1)S(1)}, u32[]{:S(2)}, u32[]{:S(2)}) async-start(bf16[64,60,128]{2,1,0:T(8,128)(2,1)} %bitcast.2), calls=%async_computation | async-start | bytes 2097152 | tf_op jit(solution)/shard_map/all_to_all | solution.py:150
  17.4 2.0 %collective-permute-start = (bf16[768,128]{1,0:T(8,128)(2,1)S(1)}, bf16[768,128]{1,0:T(8,128)(2,1)S(1)}, u32[]{:S(2)}, u32[]{:S(2)}) collective-permute-start(bf16[768,128]{1,0:T(8,128)(2,1)S(1)} %get-tuple-element.44), channel_id=1, source_target_pairs={{0,1},{1,0},{2,3},{3,2},{4,5},{5,4},{6,7},{7,6},{8,9},{9,8},{10,11... | collective-permute-start | bytes 589832 | tf_op jit(solution)/shard_map/ppermute | solution.py:125
  19.4 1.3 collective-permute-done
  20.7 23.1 %all-to-all-done = bf16[64,60,128]{2,1,0:T(8,128)(2,1)S(1)} async-done(((bf16[64,60,128]{2,1,0:T(8,128)(2,1)}), bf16[64,60,128]{2,1,0:T(8,128)(2,1)S(1)}, u32[]{:S(2)}, u32[]{:S(2)}) %all-to-all-start) | async-done | bytes 983072 | tf_op jit(solution)/shard_map/all_to_all | solution.py:150
  43.8 0.9 reshape.155.own_ref
  44.7 0.4 fusion.23
  45.2 3.3 %collective-permute-start.2 = (f32[640,128]{1,0:T(8,128)S(1)}, f32[640,128]{1,0:T(8,128)S(1)}, u32[]{:S(2)}, u32[]{:S(2)}) collective-permute-start(f32[640,128]{1,0:T(8,128)S(1)} %fusion.23), channel_id=1, source_target_pairs={{0,1},{1,0},{2,3},{3,2},{4,5},{5,4},{6,7},{7,6},{8,9},{9,8},{10,11... | collective-permute-start | bytes 983048 | tf_op jit(solution)/shard_map/ppermute | solution.py:125
  48.5 1.2 collective-permute-done.2
  49.7 1.1 convolution_add_fusion
  50.9 7.1 %all-to-all-start.1 = ((f32[8,80,128]{2,1,0:T(8,128)}), f32[8,80,128]{2,1,0:T(8,128)S(1)}, u32[]{:S(2)}, u32[]{:S(2)}) async-start(f32[8,80,128]{2,1,0:T(8,128)} %bitcast.5), calls=%async_computation.1 | async-start | bytes 655360 | tf_op jit(solution)/shard_map/all_to_all | solution.py:116
  58.2 15.0 %all-to-all-done.1 = f32[8,80,128]{2,1,0:T(8,128)S(1)} async-done(((f32[8,80,128]{2,1,0:T(8,128)}), f32[8,80,128]{2,1,0:T(8,128)S(1)}, u32[]{:S(2)}, u32[]{:S(2)}) %all-to-all-start.1) | async-done | bytes 327712 | tf_op jit(solution)/shard_map/all_to_all | solution.py:116
  73.3 0.8 broadcast_in_dim.19
  74.0 3.9 %all-to-all-start.2 = ((bf16[16,80,128]{2,1,0:T(8,128)(2,1)}), bf16[16,80,128]{2,1,0:T(8,128)(2,1)S(1)}, u32[]{:S(2)}, u32[]{:S(2)}) async-start(bf16[16,80,128]{2,1,0:T(8,128)(2,1)} %broadcast_in_dim.19), calls=%async_computation.2 | async-start | bytes 655360 | tf_op jit(solution)/shard_map/all_to_all | solution.py:119
  78.0 2.0 %collective-permute-start.4 = (bf16[128,768]{0,1:T(8,128)(2,1)S(1)}, bf16[128,768]{0,1:T(8,128)(2,1)S(1)}, u32[]{:S(2)}, u32[]{:S(2)}) collective-permute-start(bf16[128,768]{0,1:T(8,128)(2,1)S(1)} %bitcast.78), channel_id=1, source_target_pairs={{0,16},{1,17},{2,18},{3,19},{4,20},{5,21},{6,22},{7,23},{8,24},{9,... | collective-permute-start | bytes 589832 | tf_op jit(solution)/shard_map/ppermute | solution.py:125
  80.0 8.7 %collective-permute-done.4 = bf16[128,768]{0,1:T(8,128)(2,1)S(1)} collective-permute-done((bf16[128,768]{0,1:T(8,128)(2,1)S(1)}, bf16[128,768]{0,1:T(8,128)(2,1)S(1)}, u32[]{:S(2)}, u32[]{:S(2)}) %collective-permute-start.4) | collective-permute-done | bytes 196640 | tf_op jit(solution)/shard_map/ppermute | solution.py:125
  88.8 3.0 %all-to-all-done.2 = bf16[16,80,128]{2,1,0:T(8,128)(2,1)S(1)} async-done(((bf16[16,80,128]{2,1,0:T(8,128)(2,1)}), bf16[16,80,128]{2,1,0:T(8,128)(2,1)S(1)}, u32[]{:S(2)}, u32[]{:S(2)}) %all-to-all-start.2) | async-done | bytes 327712 | tf_op jit(solution)/shard_map/all_to_all | solution.py:119
  91.9 1.9 %collective-permute-start.3 = (bf16[640,256]{1,0:T(8,128)(2,1)S(1)}, bf16[640,256]{1,0:T(8,128)(2,1)S(1)}, u32[]{:S(2)}, u32[]{:S(2)}) collective-permute-start(bf16[640,256]{1,0:T(8,128)(2,1)S(1)} %pad_maximum_fusion.2), channel_id=1, source_target_pairs={{0,1},{1,0},{2,3},{3,2},{4,5},{5,4},{6,7},{7,6},{8,9},{9,8},{10,11... | collective-permute-start | bytes 983048 | tf_op jit(solution)/shard_map/ppermute | solution.py:125
  93.9 2.4 %collective-permute-start.5 = (bf16[256,384]{0,1:T(8,128)(2,1)S(1)}, bf16[256,384]{0,1:T(8,128)(2,1)S(1)}, u32[]{:S(2)}, u32[]{:S(2)}) collective-permute-start(bf16[256,384]{0,1:T(8,128)(2,1)S(1)} %get-tuple-element.39), channel_id=1, source_target_pairs={{0,1},{1,0},{2,3},{3,2},{4,5},{5,4},{6,7},{7,6},{8,9},{9,8},{10,11... | collective-permute-start | bytes 589832 | tf_op jit(solution)/shard_map/ppermute | solution.py:125
  96.3 1.0 collective-permute-done.5
  97.4 1.3 convolution_convert_fusion
  98.7 6.1 %all-to-all-start.3 = ((bf16[16,40,384]{2,1,0:T(8,128)(2,1)}), bf16[16,40,384]{2,1,0:T(8,128)(2,1)S(1)}, u32[]{:S(2)}, u32[]{:S(2)}) async-start(bf16[16,40,384]{2,1,0:T(8,128)(2,1)} %bitcast.11), calls=%async_computation.3 | async-start | bytes 983040 | tf_op jit(solution)/shard_map/all_to_all | solution.py:122
  104.9 14.8 %all-to-all-done.3 = bf16[16,40,384]{2,1,0:T(8,128)(2,1)S(1)} async-done(((bf16[16,40,384]{2,1,0:T(8,128)(2,1)}), bf16[16,40,384]{2,1,0:T(8,128)(2,1)S(1)}, u32[]{:S(2)}, u32[]{:S(2)}) %all-to-all-start.3) | async-done | bytes 491552 | tf_op jit(solution)/shard_map/all_to_all | solution.py:122
  119.8 0.8 broadcast_in_dim.20
  120.6 7.0 %all-to-all-start.4 = ((bf16[16,40,384]{2,1,0:T(8,128)(2,1)}), bf16[16,40,384]{2,1,0:T(8,128)(2,1)S(1)}, u32[]{:S(2)}, u32[]{:S(2)}) async-start(bf16[16,40,384]{2,1,0:T(8,128)(2,1)} %broadcast_in_dim.20), calls=%async_computation.4 | async-start | bytes 983040 | tf_op jit(solution)/shard_map/all_to_all | solution.py:122
  127.7 13.7 %all-to-all-done.4 = bf16[16,40,384]{2,1,0:T(8,128)(2,1)S(1)} async-done(((bf16[16,40,384]{2,1,0:T(8,128)(2,1)}), bf16[16,40,384]{2,1,0:T(8,128)(2,1)S(1)}, u32[]{:S(2)}, u32[]{:S(2)}) %all-to-all-start.4) | async-done | bytes 491552 | tf_op jit(solution)/shard_map/all_to_all | solution.py:122
  141.3 0.3 fusion
  141.7 1.9 %collective-permute-start.6 = (bf16[640,256]{1,0:T(8,128)(2,1)S(1)}, bf16[640,256]{1,0:T(8,128)(2,1)S(1)}, u32[]{:S(2)}, u32[]{:S(2)}) collective-permute-start(bf16[640,256]{1,0:T(8,128)(2,1)S(1)} %fusion), channel_id=1, source_target_pairs={{0,1},{1,0},{2,3},{3,2},{4,5},{5,4},{6,7},{7,6},{8,9},{9,8},{10,11... | collective-permute-start | bytes 983048 | tf_op jit(solution)/shard_map/ppermute | solution.py:125
  143.9 1.3 collective-permute-done.6
  145.2 0.3 fusion.8
  145.5 0.3 fusion.9
  145.8 0.8 pad_maximum_fusion.3
  146.6 9.8 %all-to-all-start.5 = ((bf16[16,80,128]{2,1,0:T(8,128)(2,1)}), bf16[16,80,128]{2,1,0:T(8,128)(2,1)S(1)}, u32[]{:S(2)}, u32[]{:S(2)}) async-start(bf16[16,80,128]{2,1,0:T(8,128)(2,1)} %bitcast.16), calls=%async_computation.5 | async-start | bytes 655360 | tf_op jit(solution)/shard_map/all_to_all | solution.py:119
  156.4 1.1 convolution_multiply_fusion.1
  157.6 1.9 %collective-permute-start.7 = (f32[256,384]{1,0:T(8,128)}, f32[256,384]{1,0:T(8,128)}, u32[]{:S(2)}, u32[]{:S(2)}) collective-permute-start(f32[256,384]{1,0:T(8,128)} %convolution_multiply_fusion.1), channel_id=1, source_target_pairs={{0,1},{1,0},{2,3},{3,2},{4,5},{5,4},{6,7},{7,6},{8,9},{9,8},{10,11... | collective-permute-start | bytes 1179656 | tf_op jit(solution)/shard_map/ppermute | solution.py:125
  159.5 2.4 %collective-permute-start.1 = (bf16[640,768]{1,0:T(8,128)(2,1)S(1)}, bf16[640,768]{1,0:T(8,128)(2,1)S(1)}, u32[]{:S(2)}, u32[]{:S(2)}) collective-permute-start(bf16[640,768]{1,0:T(8,128)(2,1)S(1)} %reshape.155.own_ref), channel_id=1, source_target_pairs={{0,1},{1,0},{2,3},{3,2},{4,5},{5,4},{6,7},{7,6},{8,9},{9,8},{10,11... | collective-permute-start | bytes 2949128 | tf_op jit(solution)/shard_map/ppermute | solution.py:125
  162.0 1.3 fusion.1
  163.3 2.0 %fusion.15 = (f32[2,128,384]{2,1,0:T(8,128)}, f32[2,128,384]{2,1,0:T(8,128)}) fusion(s32[]{:T(128)S(6)} %select_n.98, f32[1,256,384]{2,1,0:T(8,128)S(1)} %fusion.1, f32[1,256,384]{2,1,0:T(8,128)} %bitcast.21, s32[]{:T(128)S(6)} %select_n.97), kind=kLoop, calls=%fused_computation.29 | loop fusion | flops 196608 | bytes 1572872 | tf_op jit(solution)/shard_map/stack | solution.py:203
  165.3 2.0 %collective-permute-start.8 = (f32[2,128,384]{2,1,0:T(8,128)}, f32[2,128,384]{2,1,0:T(8,128)}, u32[]{:S(2)}, u32[]{:S(2)}) collective-permute-start(f32[2,128,384]{2,1,0:T(8,128)} %get-tuple-element.32), channel_id=1, source_target_pairs={{0,16},{1,17},{2,18},{3,19},{4,20},{5,21},{6,22},{7,23},{8,24},{9,... | collective-permute-start | bytes 1179656 | tf_op jit(solution)/shard_map/ppermute | solution.py:125
  167.3 3.2 %all-to-all-done.5 = bf16[16,80,128]{2,1,0:T(8,128)(2,1)S(1)} async-done(((bf16[16,80,128]{2,1,0:T(8,128)(2,1)}), bf16[16,80,128]{2,1,0:T(8,128)(2,1)S(1)}, u32[]{:S(2)}, u32[]{:S(2)}) %all-to-all-start.5) | async-done | bytes 327712 | tf_op jit(solution)/shard_map/all_to_all | solution.py:119
  170.6 0.7 broadcast_in_dim.22
  171.3 6.3 %all-to-all-start.6 = ((bf16[8,80,128]{2,1,0:T(8,128)(2,1)}), bf16[8,80,128]{2,1,0:T(8,128)(2,1)S(1)}, u32[]{:S(2)}, u32[]{:S(2)}) async-start(bf16[8,80,128]{2,1,0:T(8,128)(2,1)} %broadcast_in_dim.22), calls=%async_computation.6 | async-start | bytes 327680 | tf_op jit(solution)/shard_map/all_to_all | solution.py:116
  177.6 1.1 slice_bitcast_fusion.1
  178.8 1.1 slice_bitcast_fusion
  179.8 2.4 %adam.1 = (f32[1536,128]{1,0:T(8,128)}, f32[1536,128]{1,0:T(8,128)}, f32[1536,128]{1,0:T(8,128)}) custom-call(s32[1]{0:T(128)} %bitcast.19.place_ref, f32[128,384]{1,0:T(8,128)S(1)} %get-tuple-element.37.p0, f32[128,384]{1,0:T(8,128)S(1)} %get-tuple-element.35.p1, f32[128,384]{1,0:T(8,128)S(1)} %get-tuple-element.36.p2, ...), custom_call_target="tpu_custom_call" | custom-call | tf_op jit(solution)/shard_map/adam/pallas_call | solution.py:71
  182.2 7.2 %all-to-all-done.6 = bf16[8,80,128]{2,1,0:T(8,128)(2,1)S(1)} async-done(((bf16[8,80,128]{2,1,0:T(8,128)(2,1)}), bf16[8,80,128]{2,1,0:T(8,128)(2,1)S(1)}, u32[]{:S(2)}, u32[]{:S(2)}) %all-to-all-start.6) | async-done | bytes 163872 | tf_op jit(solution)/shard_map/all_to_all | solution.py:116
  189.4 1.3 encoder_grad.1
  (44 shorter events, 1.2 us)
Async XLA Ops:
  0.6 104.2 %copy-start = (f32[1,1536]{1,0:T(1,128)S(1)}, f32[1,1536]{1,0:T(1,128)}, u32[]{:S(2)}) copy-start(f32[1,1536]{1,0:T(1,128)} %param.11) | copy-start | bytes 18436
  2.8 14.5 %copy-start.5 = (bf16[1,1536,128]{2,1,0:T(8,128)(2,1)S(1)}, bf16[1,1536,128]{2,1,0:T(8,128)(2,1)}, u32[]{:S(2)}) copy-start(bf16[1,1536,128]{2,1,0:T(8,128)(2,1)} %param.8) | copy-start | bytes 1179652
  2.8 41.0 %all-to-all-start = ((bf16[64,60,128]{2,1,0:T(8,128)(2,1)}), bf16[64,60,128]{2,1,0:T(8,128)(2,1)S(1)}, u32[]{:S(2)}, u32[]{:S(2)}) async-start(bf16[64,60,128]{2,1,0:T(8,128)(2,1)} %bitcast.2), calls=%async_computation | async-start | bytes 2097152 | tf_op jit(solution)/shard_map/all_to_all | solution.py:150
  17.4 3.3 %collective-permute-start = (bf16[768,128]{1,0:T(8,128)(2,1)S(1)}, bf16[768,128]{1,0:T(8,128)(2,1)S(1)}, u32[]{:S(2)}, u32[]{:S(2)}) collective-permute-start(bf16[768,128]{1,0:T(8,128)(2,1)S(1)} %get-tuple-element.44), channel_id=1, source_target_pairs={{0,1},{1,0},{2,3},{3,2},{4,5},{5,4},{6,7},{7,6},{8,9},{9,8},{10,11... | collective-permute-start | bytes 589832 | tf_op jit(solution)/shard_map/ppermute | solution.py:125
  45.2 12.9 %copy-start.1 = (bf16[128,1,1536]{2,0,1:T(8,128)(2,1)S(1)}, bf16[128,1,1536]{2,0,1:T(8,128)(2,1)}, u32[]{:S(2)}) copy-start(bf16[128,1,1536]{2,0,1:T(8,128)(2,1)} %param.10) | copy-start | bytes 1179652
  45.2 4.6 %collective-permute-start.2 = (f32[640,128]{1,0:T(8,128)S(1)}, f32[640,128]{1,0:T(8,128)S(1)}, u32[]{:S(2)}, u32[]{:S(2)}) collective-permute-start(f32[640,128]{1,0:T(8,128)S(1)} %fusion.23), channel_id=1, source_target_pairs={{0,1},{1,0},{2,3},{3,2},{4,5},{5,4},{6,7},{7,6},{8,9},{9,8},{10,11... | collective-permute-start | bytes 983048 | tf_op jit(solution)/shard_map/ppermute | solution.py:125
  50.9 22.3 %copy-start.8 = (f32[128]{0:T(128)S(1)}, f32[128]{0:T(128)}, u32[]{:S(2)}) copy-start(f32[128]{0:T(128)} %param.9) | copy-start | bytes 1540
  50.9 22.3 %all-to-all-start.1 = ((f32[8,80,128]{2,1,0:T(8,128)}), f32[8,80,128]{2,1,0:T(8,128)S(1)}, u32[]{:S(2)}, u32[]{:S(2)}) async-start(f32[8,80,128]{2,1,0:T(8,128)} %bitcast.5), calls=%async_computation.1 | async-start | bytes 655360 | tf_op jit(solution)/shard_map/all_to_all | solution.py:116
  74.0 17.8 %all-to-all-start.2 = ((bf16[16,80,128]{2,1,0:T(8,128)(2,1)}), bf16[16,80,128]{2,1,0:T(8,128)(2,1)S(1)}, u32[]{:S(2)}, u32[]{:S(2)}) async-start(bf16[16,80,128]{2,1,0:T(8,128)(2,1)} %broadcast_in_dim.19), calls=%async_computation.2 | async-start | bytes 655360 | tf_op jit(solution)/shard_map/all_to_all | solution.py:119
  78.0 10.8 %collective-permute-start.4 = (bf16[128,768]{0,1:T(8,128)(2,1)S(1)}, bf16[128,768]{0,1:T(8,128)(2,1)S(1)}, u32[]{:S(2)}, u32[]{:S(2)}) collective-permute-start(bf16[128,768]{0,1:T(8,128)(2,1)S(1)} %bitcast.78), channel_id=1, source_target_pairs={{0,16},{1,17},{2,18},{3,19},{4,20},{5,21},{6,22},{7,23},{8,24},{9,... | collective-permute-start | bytes 589832 | tf_op jit(solution)/shard_map/ppermute | solution.py:125
  91.9 6.9 %copy-start.4 = (bf16[8,80,128]{2,1,0:T(8,128)(2,1)}, bf16[8,80,128]{2,1,0:T(8,128)(2,1)S(1)}, u32[]{:S(2)}) copy-start(bf16[8,80,128]{2,1,0:T(8,128)(2,1)S(1)} %get-tuple-element.47) | copy-start | bytes 491524
  91.9 5.5 %collective-permute-start.3 = (bf16[640,256]{1,0:T(8,128)(2,1)S(1)}, bf16[640,256]{1,0:T(8,128)(2,1)S(1)}, u32[]{:S(2)}, u32[]{:S(2)}) collective-permute-start(bf16[640,256]{1,0:T(8,128)(2,1)S(1)} %pad_maximum_fusion.2), channel_id=1, source_target_pairs={{0,1},{1,0},{2,3},{3,2},{4,5},{5,4},{6,7},{7,6},{8,9},{9,8},{10,11... | collective-permute-start | bytes 983048 | tf_op jit(solution)/shard_map/ppermute | solution.py:125
  93.9 3.5 %collective-permute-start.5 = (bf16[256,384]{0,1:T(8,128)(2,1)S(1)}, bf16[256,384]{0,1:T(8,128)(2,1)S(1)}, u32[]{:S(2)}, u32[]{:S(2)}) collective-permute-start(bf16[256,384]{0,1:T(8,128)(2,1)S(1)} %get-tuple-element.39), channel_id=1, source_target_pairs={{0,1},{1,0},{2,3},{3,2},{4,5},{5,4},{6,7},{7,6},{8,9},{9,8},{10,11... | collective-permute-start | bytes 589832 | tf_op jit(solution)/shard_map/ppermute | solution.py:125
  97.4 1.3 copy-start.6
  98.7 20.9 %all-to-all-start.3 = ((bf16[16,40,384]{2,1,0:T(8,128)(2,1)}), bf16[16,40,384]{2,1,0:T(8,128)(2,1)S(1)}, u32[]{:S(2)}, u32[]{:S(2)}) async-start(bf16[16,40,384]{2,1,0:T(8,128)(2,1)} %bitcast.11), calls=%async_computation.3 | async-start | bytes 983040 | tf_op jit(solution)/shard_map/all_to_all | solution.py:122
  120.6 20.7 %all-to-all-start.4 = ((bf16[16,40,384]{2,1,0:T(8,128)(2,1)}), bf16[16,40,384]{2,1,0:T(8,128)(2,1)S(1)}, u32[]{:S(2)}, u32[]{:S(2)}) async-start(bf16[16,40,384]{2,1,0:T(8,128)(2,1)} %broadcast_in_dim.20), calls=%async_computation.4 | async-start | bytes 983040 | tf_op jit(solution)/shard_map/all_to_all | solution.py:122
  141.7 3.5 %collective-permute-start.6 = (bf16[640,256]{1,0:T(8,128)(2,1)S(1)}, bf16[640,256]{1,0:T(8,128)(2,1)S(1)}, u32[]{:S(2)}, u32[]{:S(2)}) collective-permute-start(bf16[640,256]{1,0:T(8,128)(2,1)S(1)} %fusion), channel_id=1, source_target_pairs={{0,1},{1,0},{2,3},{3,2},{4,5},{5,4},{6,7},{7,6},{8,9},{9,8},{10,11... | collective-permute-start | bytes 983048 | tf_op jit(solution)/shard_map/ppermute | solution.py:125
  145.5 10.9 %copy-start.7 = (bf16[640,256]{1,0:T(8,128)(2,1)S(1)}, bf16[640,256]{1,0:T(8,128)(2,1)}, u32[]{:S(2)}) copy-start(bf16[640,256]{1,0:T(8,128)(2,1)} %copy-done.6) | copy-start | bytes 983044
  146.6 24.0 %all-to-all-start.5 = ((bf16[16,80,128]{2,1,0:T(8,128)(2,1)}), bf16[16,80,128]{2,1,0:T(8,128)(2,1)S(1)}, u32[]{:S(2)}, u32[]{:S(2)}) async-start(bf16[16,80,128]{2,1,0:T(8,128)(2,1)} %bitcast.16), calls=%async_computation.5 | async-start | bytes 655360 | tf_op jit(solution)/shard_map/all_to_all | solution.py:119
  157.6 5.8 %collective-permute-start.7 = (f32[256,384]{1,0:T(8,128)}, f32[256,384]{1,0:T(8,128)}, u32[]{:S(2)}, u32[]{:S(2)}) collective-permute-start(f32[256,384]{1,0:T(8,128)} %convolution_multiply_fusion.1), channel_id=1, source_target_pairs={{0,1},{1,0},{2,3},{3,2},{4,5},{5,4},{6,7},{7,6},{8,9},{9,8},{10,11... | collective-permute-start | bytes 1179656 | tf_op jit(solution)/shard_map/ppermute | solution.py:125
  159.5 22.7 %collective-permute-start.1 = (bf16[640,768]{1,0:T(8,128)(2,1)S(1)}, bf16[640,768]{1,0:T(8,128)(2,1)S(1)}, u32[]{:S(2)}, u32[]{:S(2)}) collective-permute-start(bf16[640,768]{1,0:T(8,128)(2,1)S(1)} %reshape.155.own_ref), channel_id=1, source_target_pairs={{0,1},{1,0},{2,3},{3,2},{4,5},{5,4},{6,7},{7,6},{8,9},{9,8},{10,11... | collective-permute-start | bytes 2949128 | tf_op jit(solution)/shard_map/ppermute | solution.py:125
  165.3 13.4 %collective-permute-start.8 = (f32[2,128,384]{2,1,0:T(8,128)}, f32[2,128,384]{2,1,0:T(8,128)}, u32[]{:S(2)}, u32[]{:S(2)}) collective-permute-start(f32[2,128,384]{2,1,0:T(8,128)} %get-tuple-element.32), channel_id=1, source_target_pairs={{0,16},{1,17},{2,18},{3,19},{4,20},{5,21},{6,22},{7,23},{8,24},{9,... | collective-permute-start | bytes 1179656 | tf_op jit(solution)/shard_map/ppermute | solution.py:125
  170.6 9.2 %copy-start.2 = (f32[128,1,1536]{2,1,0:T(1,128)S(1)}, f32[128,1,1536]{2,1,0:T(1,128)}, u32[]{:S(2)}) copy-start(f32[128,1,1536]{2,1,0:T(1,128)} %param.12) | copy-start | bytes 2359300
  171.3 18.1 %all-to-all-start.6 = ((bf16[8,80,128]{2,1,0:T(8,128)(2,1)}), bf16[8,80,128]{2,1,0:T(8,128)(2,1)S(1)}, u32[]{:S(2)}, u32[]{:S(2)}) async-start(bf16[8,80,128]{2,1,0:T(8,128)(2,1)} %broadcast_in_dim.22), calls=%async_computation.6 | async-start | bytes 327680 | tf_op jit(solution)/shard_map/all_to_all | solution.py:116
  177.6 2.2 %copy-start.3 = (f32[128,1,1536]{2,1,0:T(1,128)S(1)}, f32[128,1,1536]{2,1,0:T(1,128)}, u32[]{:S(2)}) copy-start(f32[128,1,1536]{2,1,0:T(1,128)} %param.13) | copy-start | bytes 2359300

commit v5 on v3

--- a/solution.py
+++ b/solution.py
@@ -1,3 +1,5 @@
+import functools
+
 import jax
 import jax.numpy as jnp
 from jax import lax
@@ -37,15 +39,93 @@
         out_shape=jax.ShapeDtypeStruct((2, half, lat_dev), jnp.bfloat16),
         in_specs=[pl.BlockSpec(memory_space=pltpu.SMEM)] + [pl.BlockSpec(memory_space=pltpu.VMEM)] * 3,
         out_specs=pl.BlockSpec(memory_space=pltpu.VMEM),
+        compiler_params=pltpu.CompilerParams(vmem_limit_bytes=12 << 20),
         name="encoder_grad",
     )(core, own, other, grad)
+
+
+def small(**more):
+    return dict(compiler_params=pltpu.CompilerParams(vmem_limit_bytes=12 << 20), **more)
+
+
+def whole(count):
+    return [pl.BlockSpec(memory_space=pltpu.VMEM)] * count
+
+
+def decode_kernel(own_ref, other_ref, weight_ref, out_ref):
+    codes = jnp.concatenate([own_ref[0], own_ref[1], other_ref[0], other_ref[1]], axis=1)
+    out_ref[...] = lax.dot_general(
+        codes, weight_ref[...], (((1,), (0,)), ((), ())), preferred_element_type=jnp.float32
+    ).astype(jnp.bfloat16)
+
+
+def decode(own, other, weight):
+    rows, part = own.shape[1], weight.shape[1]
+    steps = 4
+    codes_spec = pl.BlockSpec((2, rows // steps, own.shape[2]), lambda i: (0, i, 0))
+    return pl.pallas_call(
+        decode_kernel,
+        grid=(steps,),
+        out_shape=jax.ShapeDtypeStruct((rows, part), jnp.bfloat16),
+        in_specs=[codes_spec, codes_spec, pl.BlockSpec(weight.shape, lambda i: (0, 0))],
+        out_specs=pl.BlockSpec((rows // steps, part), lambda i: (i, 0)),
+        **small(name="decode"),
+    )(own, other, weight)
+
+
+def grad_kernel(scale, chip_ref, errors_ref, weight_ref, norm_ref, own_ref, other_ref):
+    lats = own_ref.shape[2]
+    for z in range(TEAM):
+        rows = weight_ref[z * lats : (z + 1) * lats, :]
+        term = scale * lax.dot_general(
+            errors_ref[...], rows, (((1,), (1,)), ((), ())), preferred_element_type=jnp.float32
+        )
+        if z < 2:
+            own_ref[z] = term + jnp.where(chip_ref[0] == z, norm_ref[...], 0.0)
+        else:
+            other_ref[z - 2] = term.astype(jnp.bfloat16)
+
+
+def grad_parts(scale, chip, errors, weight, norm):
+    shape = (2, errors.shape[0], weight.shape[0] // TEAM)
+    return pl.pallas_call(
+        functools.partial(grad_kernel, scale),
+        out_shape=(jax.ShapeDtypeStruct(shape, jnp.float32), jax.ShapeDtypeStruct(shape, jnp.bfloat16)),
+        in_specs=[pl.BlockSpec(memory_space=pltpu.SMEM)] + whole(3),
+        out_specs=tuple(whole(2)),
+        **small(name="grad_parts"),
+    )(chip, errors, weight, norm)
+
+
+def acc_kernel(scale, chip_ref, own_ref, other_ref, errors_ref, keep_ref, give_ref, core_ref):
+    for index, ref in ((0, own_ref), (1, own_ref), (0, other_ref), (1, other_ref)):
+        codes = ref[chip_ref[0] ^ index].astype(jnp.float32).T.astype(jnp.bfloat16)
+        term = scale * lax.dot_general(
+            codes, errors_ref[...], (((1,), (0,)), ((), ())), preferred_element_type=jnp.float32
+        )
+        if ref is own_ref:
+            (give_ref if index else keep_ref)[...] = term
+        else:
+            core_ref[index] = term
+
+
+def acc_parts(scale, chip, own, other, errors):
+    shape = (own.shape[2], errors.shape[1])
+    flat = jax.ShapeDtypeStruct(shape, jnp.float32)
+    return pl.pallas_call(
+        functools.partial(acc_kernel, scale),
+        out_shape=(flat, flat, jax.ShapeDtypeStruct((2,) + shape, jnp.float32)),
+        in_specs=[pl.BlockSpec(memory_space=pltpu.SMEM)] + whole(3),
+        out_specs=tuple(whole(3)),
+        **small(name="acc_parts"),
+    )(chip, own, other, errors)
 
 
 def adam_kernel(place_ref, p0, p1, p2, p3, weight_ref, coef_ref, first_ref, second_ref, dec_out, first_out, second_out, term):
     lats, part = p0.shape
     tiles = TEAM * part // LANES
     for mask, piece in enumerate((p0, p1, p2, p3)):
-        term[place_ref[0] ^ mask] = piece[...]
+        term[place_ref[0] ^ mask] = piece[...].reshape(lats, part)
     for tile in range(tiles):
         col = tile * LANES % part
         rows = pl.ds(tile, lats, stride=tiles)
@@ -72,10 +152,11 @@
         grid=(steps,),
         out_shape=(flat, flat, flat),
         in_specs=[pl.BlockSpec(memory_space=pltpu.SMEM)]
-        + [by_lat(part)] * TEAM
+        + [by_lat(part), by_lat(part), pl.BlockSpec((1, lats, part), lambda i: (0, i, 0)), by_lat(part)]
         + [by_lat(width), by_lat(1), by_row, by_row],
         out_specs=(by_row, by_row, by_row),
         scratch_shapes=[pltpu.VMEM((TEAM, lats, part), jnp.float32)],
+        compiler_params=pltpu.CompilerParams(vmem_limit_bytes=12 << 20),
         name="adam",
     )(place, *pieces, weight, coef, first.reshape(flat.shape), second.reshape(flat.shape))
     return [out.reshape(lat_dev, 1, width) for out in outs]
@@ -164,42 +245,31 @@
 
     codes_block = jnp.maximum(pre, 0.0).astype(jnp.bfloat16)
     codes_chips = over_pairs(repeat(codes_block, 2 * snaps)).reshape(2, batch_rows, lat_dev)
-    codes_core = jnp.concatenate([codes_chips[0], codes_chips[1]], axis=1)
+    codes_other = exchange(codes_chips, CORE)
     acts_other = exchange(acts, CORE)
-    codes = jnp.concatenate([codes_core, exchange(codes_core, CORE)], axis=1)
-
-    sent = mm(codes, dec_team, ((1,), (0,))).astype(jnp.bfloat16).reshape(teams, team_rows, part)
+
+    sent = decode(codes_chips, codes_other, dec_team).reshape(teams, team_rows, part)
     decoded = jnp.sum(over_teams(sent).astype(jnp.float32), axis=0)
     target = lax.dynamic_slice(acts, (team * team_rows, chip * part), (team_rows, part))
     bias_part = lax.dynamic_slice_in_dim(dec_bias[0], place * part, part, 0)
     errors_block = (decoded + bias_part[None, :] - target.astype(jnp.float32)).astype(jnp.bfloat16)
     errors = over_teams(repeat(errors_block, teams)).reshape(batch_rows, part)
 
-    grad_other = exchange((scale_rec * mm(errors, dec_team[2 * lat_dev :], ((1,), (1,)))).astype(jnp.bfloat16), 1)
-    norm_part = scale_sparse * own_norm[None, :]
-    grad_sent = jnp.stack(
-        [
-            scale_rec * mm(errors, dec_team[z * lat_dev : (z + 1) * lat_dev], ((1,), (1,)))
-            + grad_other[:, z * lat_dev : (z + 1) * lat_dev].astype(jnp.float32)
-            + jnp.where(chip == z, norm_part, 0.0)
-            for z in range(2)
-        ],
-        axis=0,
-    ).astype(jnp.bfloat16)
+    grad_own, grad_give = grad_parts(scale_rec, chip.reshape(1), errors, dec_team, scale_sparse * own_norm[None, :])
+    grad_sent = (grad_own + exchange(grad_give, CORE).astype(jnp.float32)).astype(jnp.bfloat16)
     grad_sent = grad_sent.reshape(2 * snaps, block_rows, lat_dev)
     grad = jnp.sum(over_pairs(grad_sent).astype(jnp.float32), axis=0)
     grad_block = jnp.where(pre > 0.0, grad, 0.0).astype(jnp.bfloat16)
     grad_pre = over_snaps(repeat(grad_block, snaps)).reshape(batch_rows, lat_dev)
 
-    acc_own = scale_rec * mm(codes[:, : 2 * lat_dev], errors, ((0,), (0,)))
-    acc_give = scale_rec * mm(codes[:, 2 * lat_dev :], errors, ((0,), (0,)))
-    acc_core = exchange(acc_give, CORE)
-    keep, give = split(jnp.stack([acc_own, acc_core], axis=0), 1, chip)
-    acc_chip = exchange(give, CHIP)
+    acc_keep, acc_give, acc_core = acc_parts(scale_rec, chip.reshape(1), codes_chips, codes_other, errors)
+    acc_core = exchange(acc_core, CORE)
+    acc_chip = exchange(acc_give, CHIP)
+    acc_both = exchange(acc_core[1], CHIP)
     own_codes = lax.dynamic_index_in_dim(codes_chips, chip, 0, keepdims=False)
     code_total = jnp.sum(own_codes.astype(jnp.float32), axis=0)
     coef = (scale_sparse * code_total / own_norm)[:, None]
-    pieces = (keep[0], acc_chip[0], keep[1], acc_chip[1])
+    pieces = (acc_keep, acc_chip, acc_core, acc_both)
     new_decoder, new_first, new_second = adam(place.reshape(1), pieces, dec_local, coef, dec_first, dec_second)
 
     enc_grad = encoder_grad(core.reshape(1), acts, acts_other, grad_pre).reshape(1, width, lat_dev)

time: 193 us -> 196 us (1.016)
  the two profiles are of different devices: /device:TPU:16 before, /device:TPU:48 now
where the time goes in v5:
time: 196 us; the launch traced here: 195 us
  starting transfers between devices  88.3 us (45%)
  waiting for transfers between devices  83.5 us (43%)
  local copies, waits for them, and re-layouts  10.2 us (5%)
  Pallas kernels  9.03 us (5%)
    all_to_all x2, waiting for transfers between devices, over_teams(): lax.all_to_all(x, 'lat', 0, 0, tiled=True, axis_index_groups=place_groups)  32.7 us
    ppermute x10, starting transfers between devices, exchange(): return lax.ppermute(x, 'lat', [(i, i ^ mask) for i in range(lats)])  24.5 us
    all_to_all x1, waiting for transfers between devices, body(): acts = lax.all_to_all(sent, 'lat', 0, 0, tiled=True)  24.4 us
    all_to_all x2, starting transfers between devices, over_pairs(): lax.all_to_all(x, ('snap', 'lat'), 0, 0, tiled=True, axis_index_groups=pa...  19.8 us
    all_to_all x2, starting transfers between devices, over_snaps(): return lax.all_to_all(x, 'snap', 0, 0, tiled=True)  19.2 us
    ppermute x10, waiting for transfers between devices, exchange(): return lax.ppermute(x, 'lat', [(i, i ^ mask) for i in range(lats)])  14.8 us
    all_to_all x1, starting transfers between devices, body(): acts = lax.all_to_all(sent, 'lat', 0, 0, tiled=True)  13.6 us
    all_to_all x2, starting transfers between devices, over_teams(): lax.all_to_all(x, 'lat', 0, 0, tiled=True, axis_index_groups=place_groups)  11.2 us
  transfers between devices with their start and end apart: 17, of which 11 were waited for; matrix products, arithmetic and copies ran while one was open for 2% of the time, Pallas kernels for 2%

profile of v5, /device:TPU:48, one launch (start us, length us, event | category | flops | bytes accessed | tf_op | source)
XLA Modules:
  0.0 194.8 jit_solution(13540330662356219952)
XLA Ops:
  0.6 0.8 reshape_squeeze.6
  1.5 1.2 broadcast_in_dim.12
  2.8 13.6 %all-to-all-start = ((bf16[64,60,128]{2,1,0:T(8,128)(2,1)}), bf16[64,60,128]{2,1,0:T(8,128)(2,1)S(1)}, u32[]{:S(2)}, u32[]{:S(2)}) async-start(bf16[64,60,128]{2,1,0:T(8,128)(2,1)} %bitcast.2), calls=%async_computation | async-start | bytes 2097152 | tf_op jit(solution)/shard_map/all_to_all | solution.py:225
  16.4 2.0 %collective-permute-start = (bf16[768,128]{1,0:T(8,128)(2,1)S(1)}, bf16[768,128]{1,0:T(8,128)(2,1)S(1)}, u32[]{:S(2)}, u32[]{:S(2)}) collective-permute-start(bf16[768,128]{1,0:T(8,128)(2,1)S(1)} %get-tuple-element.40), channel_id=1, source_target_pairs={{0,1},{1,0},{2,3},{3,2},{4,5},{5,4},{6,7},{7,6},{8,9},{9,8},{10,11... | collective-permute-start | bytes 589832 | tf_op jit(solution)/shard_map/ppermute | solution.py:200
  18.5 1.3 collective-permute-done
  19.8 24.4 %all-to-all-done = bf16[64,60,128]{2,1,0:T(8,128)(2,1)S(1)} async-done(((bf16[64,60,128]{2,1,0:T(8,128)(2,1)}), bf16[64,60,128]{2,1,0:T(8,128)(2,1)S(1)}, u32[]{:S(2)}, u32[]{:S(2)}) %all-to-all-start) | async-done | bytes 983072 | tf_op jit(solution)/shard_map/all_to_all | solution.py:225
  44.2 0.9 reshape.162.own_ref
  45.1 0.4 fusion.1
  45.5 2.5 %collective-permute-start.2 = (f32[640,128]{1,0:T(8,128)S(1)}, f32[640,128]{1,0:T(8,128)S(1)}, u32[]{:S(2)}, u32[]{:S(2)}) collective-permute-start(f32[640,128]{1,0:T(8,128)S(1)} %fusion.1), channel_id=1, source_target_pairs={{0,1},{1,0},{2,3},{3,2},{4,5},{5,4},{6,7},{7,6},{8,9},{9,8},{10,11... | collective-permute-start | bytes 983048 | tf_op jit(solution)/shard_map/ppermute | solution.py:200
  48.0 1.2 collective-permute-done.2
  49.3 1.2 convolution_add_fusion
  50.4 9.8 %all-to-all-start.1 = ((f32[8,80,128]{2,1,0:T(8,128)}), f32[8,80,128]{2,1,0:T(8,128)S(1)}, u32[]{:S(2)}, u32[]{:S(2)}) async-start(f32[8,80,128]{2,1,0:T(8,128)} %bitcast.5), calls=%async_computation.1 | async-start | bytes 655360 | tf_op jit(solution)/shard_map/all_to_all | solution.py:191
  60.3 10.0 %all-to-all-done.1 = f32[8,80,128]{2,1,0:T(8,128)S(1)} async-done(((f32[8,80,128]{2,1,0:T(8,128)}), f32[8,80,128]{2,1,0:T(8,128)S(1)}, u32[]{:S(2)}, u32[]{:S(2)}) %all-to-all-start.1) | async-done | bytes 327712 | tf_op jit(solution)/shard_map/all_to_all | solution.py:191
  70.4 0.8 broadcast_in_dim.13
  71.2 8.7 %all-to-all-start.2 = ((bf16[16,80,128]{2,1,0:T(8,128)(2,1)}), bf16[16,80,128]{2,1,0:T(8,128)(2,1)S(1)}, u32[]{:S(2)}, u32[]{:S(2)}) async-start(bf16[16,80,128]{2,1,0:T(8,128)(2,1)} %broadcast_in_dim.13), calls=%async_computation.2 | async-start | bytes 655360 | tf_op jit(solution)/shard_map/all_to_all | solution.py:194
  79.9 2.7 %dynamic-slice_reduce_fusion.1 = (bf16[128,2,384]{2,1,0:T(2,128)(2,1)S(1)}, bf16[128,2,384]{2,1,0:T(2,128)(2,1)S(1)}) fusion(bf16[128,2,2,384]{3,2,1,0:T(2,128)(2,1)S(1)} %reshape_squeeze.7, s32[]{:T(128)S(6)} %select_n.53, s32[]{:T(128)S(6)} %select_n.54), kind=kLoop, calls=%fused_computation.8 | loop fusion | bytes 786440 | tf_op jit(solution)/shard_map/jit(dynamic_index_in_dim)/dynamic_slice | solution.py:233
  82.6 3.4 %collective-permute-start.4 = (bf16[128,768]{1,0:T(8,128)(2,1)S(1)}, bf16[128,768]{1,0:T(8,128)(2,1)S(1)}, u32[]{:S(2)}, u32[]{:S(2)}) collective-permute-start(bf16[128,768]{1,0:T(8,128)(2,1)S(1)} %bitcast.55), channel_id=1, source_target_pairs={{0,2},{1,3},{2,0},{3,1},{4,6},{5,7},{6,4},{7,5},{8,10},{9,11},{10,... | collective-permute-start | bytes 589832 | tf_op jit(solution)/shard_map/ppermute | solution.py:200
  86.1 4.1 %collective-permute-done.4 = bf16[128,768]{1,0:T(8,128)(2,1)S(1)} collective-permute-done((bf16[128,768]{1,0:T(8,128)(2,1)S(1)}, bf16[128,768]{1,0:T(8,128)(2,1)S(1)}, u32[]{:S(2)}, u32[]{:S(2)}) %collective-permute-start.4) | collective-permute-done | bytes 196640 | tf_op jit(solution)/shard_map/ppermute | solution.py:200
  90.3 1.9 collective-permute-start.3
  92.3 2.4 %collective-permute-start.5 = (bf16[256,384]{1,0:T(8,128)(2,1)S(1)}, bf16[256,384]{1,0:T(8,128)(2,1)S(1)}, u32[]{:S(2)}, u32[]{:S(2)}) collective-permute-start(bf16[256,384]{1,0:T(8,128)(2,1)S(1)} %get-tuple-element.37), channel_id=1, source_target_pairs={{0,1},{1,0},{2,3},{3,2},{4,5},{5,4},{6,7},{7,6},{8,9},{9,8},{10,11... | collective-permute-start | bytes 589832 | tf_op jit(solution)/shard_map/ppermute | solution.py:200
  94.7 1.0 collective-permute-done.5
  95.8 2.1 %decode.1 = bf16[640,384]{1,0:T(8,128)(2,1)} custom-call(bf16[2,640,128]{2,1,0:T(8,128)(2,1)S(1)} %bitcast.44, bf16[2,640,128]{2,1,0:T(8,128)(2,1)S(1)} %collective-permute-done.3.other_ref, bf16[512,384]{1,0:T(8,128)(2,1)S(1)} %pad_maximum_fusion.1.weight_ref), custom_call_target="tpu_custom_call" | custom-call | tf_op jit(solution)/shard_map/decode/pallas_call | solution.py:66
  97.9 6.4 %all-to-all-start.3 = ((bf16[16,40,384]{2,1,0:T(8,128)(2,1)}), bf16[16,40,384]{2,1,0:T(8,128)(2,1)S(1)}, u32[]{:S(2)}, u32[]{:S(2)}) async-start(bf16[16,40,384]{2,1,0:T(8,128)(2,1)} %bitcast.8), calls=%async_computation.3 | async-start | bytes 983040 | tf_op jit(solution)/shard_map/all_to_all | solution.py:197
  104.3 17.0 %all-to-all-done.3 = bf16[16,40,384]{2,1,0:T(8,128)(2,1)S(1)} async-done(((bf16[16,40,384]{2,1,0:T(8,128)(2,1)}), bf16[16,40,384]{2,1,0:T(8,128)(2,1)S(1)}, u32[]{:S(2)}, u32[]{:S(2)}) %all-to-all-start.3) | async-done | bytes 491552 | tf_op jit(solution)/shard_map/all_to_all | solution.py:197
  121.4 0.8 broadcast_in_dim.14
  122.3 4.9 %all-to-all-start.4 = ((bf16[16,40,384]{2,1,0:T(8,128)(2,1)}), bf16[16,40,384]{2,1,0:T(8,128)(2,1)S(1)}, u32[]{:S(2)}, u32[]{:S(2)}) async-start(bf16[16,40,384]{2,1,0:T(8,128)(2,1)} %broadcast_in_dim.14), calls=%async_computation.4 | async-start | bytes 983040 | tf_op jit(solution)/shard_map/all_to_all | solution.py:197
  127.1 0.2 multiply_reduce_fusion
  127.3 0.1 convert_reduce_fusion.2
  127.4 15.7 %all-to-all-done.4 = bf16[16,40,384]{2,1,0:T(8,128)(2,1)S(1)} async-done(((bf16[16,40,384]{2,1,0:T(8,128)(2,1)}), bf16[16,40,384]{2,1,0:T(8,128)(2,1)S(1)}, u32[]{:S(2)}, u32[]{:S(2)}) %all-to-all-start.4) | async-done | bytes 491552 | tf_op jit(solution)/shard_map/all_to_all | solution.py:197
  143.0 0.7 grad_parts.1
  143.7 1.9 collective-permute-start.6
  145.6 1.6 collective-permute-done.6
  147.2 0.8 add_convert_fusion
  148.0 11.1 %all-to-all-start.5 = ((bf16[16,80,128]{2,1,0:T(8,128)(2,1)}), bf16[16,80,128]{2,1,0:T(8,128)(2,1)S(1)}, u32[]{:S(2)}, u32[]{:S(2)}) async-start(bf16[16,80,128]{2,1,0:T(8,128)(2,1)} %bitcast.12), calls=%async_computation.5 | async-start | bytes 655360 | tf_op jit(solution)/shard_map/all_to_all | solution.py:194
  159.1 1.9 collective-permute-start.1
  161.0 1.4 acc_parts.1
  162.4 2.5 %collective-permute-start.8 = (f32[2,128,384]{2,1,0:T(8,128)}, f32[2,128,384]{2,1,0:T(8,128)S(1)}, u32[]{:S(2)}, u32[]{:S(2)}) collective-permute-start(f32[2,128,384]{2,1,0:T(8,128)} %get-tuple-element.22), channel_id=1, source_target_pairs={{0,1},{1,0},{2,3},{3,2},{4,5},{5,4},{6,7},{7,6},{8,9},{9,8},{10,11... | collective-permute-start | bytes 1179656 | tf_op jit(solution)/shard_map/ppermute | solution.py:200
  164.9 3.4 %collective-permute-start.7 = (f32[128,384]{1,0:T(8,128)}, f32[128,384]{1,0:T(8,128)S(1)}, u32[]{:S(2)}, u32[]{:S(2)}) collective-permute-start(f32[128,384]{1,0:T(8,128)} %get-tuple-element.21), channel_id=1, source_target_pairs={{0,2},{1,3},{2,0},{3,1},{4,6},{5,7},{6,4},{7,5},{8,10},{9,11},{10,... | collective-permute-start | bytes 589832 | tf_op jit(solution)/shard_map/ppermute | solution.py:200
  168.3 1.6 all-to-all-done.5
  169.9 0.7 broadcast_in_dim.16
  170.6 9.4 %all-to-all-start.6 = ((bf16[8,80,128]{2,1,0:T(8,128)(2,1)}), bf16[8,80,128]{2,1,0:T(8,128)(2,1)S(1)}, u32[]{:S(2)}, u32[]{:S(2)}) async-start(bf16[8,80,128]{2,1,0:T(8,128)(2,1)} %broadcast_in_dim.16), calls=%async_computation.6 | async-start | bytes 327680 | tf_op jit(solution)/shard_map/all_to_all | solution.py:191
  180.0 0.7 slice_bitcast_fusion
  180.7 2.5 %collective-permute-start.9 = (f32[128,384]{1,0:T(8,128)}, f32[128,384]{1,0:T(8,128)S(1)}, u32[]{:S(2)}, u32[]{:S(2)}) collective-permute-start(f32[128,384]{1,0:T(8,128)} %slice_bitcast_fusion), channel_id=1, source_target_pairs={{0,2},{1,3},{2,0},{3,1},{4,6},{5,7},{6,4},{7,5},{8,10},{9,11},{10,... | collective-permute-start | bytes 589832 | tf_op jit(solution)/shard_map/ppermute | solution.py:200
  183.2 0.1 copy.20.coef_ref
  183.3 5.5 %collective-permute-done.9.p3 = f32[128,384]{1,0:T(8,128)S(1)} collective-permute-done((f32[128,384]{1,0:T(8,128)}, f32[128,384]{1,0:T(8,128)S(1)}, u32[]{:S(2)}, u32[]{:S(2)}) %collective-permute-start.9) | collective-permute-done | bytes 196640 | tf_op jit(solution)/shard_map/ppermute | solution.py:200
  188.8 1.1 copy-done.3
  190.0 2.3 %adam.1 = (f32[1536,128]{1,0:T(8,128)}, f32[1536,128]{1,0:T(8,128)}, f32[1536,128]{1,0:T(8,128)}) custom-call(s32[1]{0:T(128)} %bitcast.15.place_ref, f32[128,384]{1,0:T(8,128)S(1)} %get-tuple-element.20.p0, f32[128,384]{1,0:T(8,128)S(1)} %collective-permute-done.7.p1, f32[2,128,384]{2,1,0:T(8,128)S(1)} %collective-permute-done.8.p2, ...), custom_call_target="tpu_custom_call" | custom-call | tf_op jit(solution)/shard_map/adam/pallas_call | solution.py:150
  192.3 2.5 %encoder_grad.1 = bf16[2,768,128]{2,1,0:T(8,128)(2,1)} custom-call(s32[1]{0:T(128)} %bitcast.core_ref, bf16[640,768]{1,0:T(8,128)(2,1)S(1)} %reshape.162.own_ref, bf16[640,768]{1,0:T(8,128)(2,1)} %collective-permute-done.1.other_ref, bf16[640,128]{1,0:T(8,128)(2,1)S(1)} %bitcast.50), custom_call_target="tpu_custom_call" | custom-call | tf_op jit(solution)/shard_map/encoder_grad/pallas_call | solution.py:37
  (35 shorter events, 0.6 us)
Async XLA Ops:
  0.6 103.6 %copy-start = (f32[1,1536]{1,0:T(1,128)S(1)}, f32[1,1536]{1,0:T(1,128)}, u32[]{:S(2)}) copy-start(f32[1,1536]{1,0:T(1,128)} %param.11) | copy-start | bytes 18436
  2.8 13.6 %copy-start.4 = (bf16[1,1536,128]{2,1,0:T(8,128)(2,1)S(1)}, bf16[1,1536,128]{2,1,0:T(8,128)(2,1)}, u32[]{:S(2)}) copy-start(bf16[1,1536,128]{2,1,0:T(8,128)(2,1)} %param.8) | copy-start | bytes 1179652
  2.8 41.4 %all-to-all-start = ((bf16[64,60,128]{2,1,0:T(8,128)(2,1)}), bf16[64,60,128]{2,1,0:T(8,128)(2,1)S(1)}, u32[]{:S(2)}, u32[]{:S(2)}) async-start(bf16[64,60,128]{2,1,0:T(8,128)(2,1)} %bitcast.2), calls=%async_computation | async-start | bytes 2097152 | tf_op jit(solution)/shard_map/all_to_all | solution.py:225
  16.4 3.3 %collective-permute-start = (bf16[768,128]{1,0:T(8,128)(2,1)S(1)}, bf16[768,128]{1,0:T(8,128)(2,1)S(1)}, u32[]{:S(2)}, u32[]{:S(2)}) collective-permute-start(bf16[768,128]{1,0:T(8,128)(2,1)S(1)} %get-tuple-element.40), channel_id=1, source_target_pairs={{0,1},{1,0},{2,3},{3,2},{4,5},{5,4},{6,7},{7,6},{8,9},{9,8},{10,11... | collective-permute-start | bytes 589832 | tf_op jit(solution)/shard_map/ppermute | solution.py:200
  45.5 3.7 %collective-permute-start.2 = (f32[640,128]{1,0:T(8,128)S(1)}, f32[640,128]{1,0:T(8,128)S(1)}, u32[]{:S(2)}, u32[]{:S(2)}) collective-permute-start(f32[640,128]{1,0:T(8,128)S(1)} %fusion.1), channel_id=1, source_target_pairs={{0,1},{1,0},{2,3},{3,2},{4,5},{5,4},{6,7},{7,6},{8,9},{9,8},{10,11... | collective-permute-start | bytes 983048 | tf_op jit(solution)/shard_map/ppermute | solution.py:200
  50.4 9.8 %copy-start.1 = (bf16[128,1,1536]{2,0,1:T(8,128)(2,1)S(1)}, bf16[128,1,1536]{2,0,1:T(8,128)(2,1)}, u32[]{:S(2)}) copy-start(bf16[128,1,1536]{2,0,1:T(8,128)(2,1)} %param.10) | copy-start | bytes 1179652
  50.4 19.9 %all-to-all-start.1 = ((f32[8,80,128]{2,1,0:T(8,128)}), f32[8,80,128]{2,1,0:T(8,128)S(1)}, u32[]{:S(2)}, u32[]{:S(2)}) async-start(f32[8,80,128]{2,1,0:T(8,128)} %bitcast.5), calls=%async_computation.1 | async-start | bytes 655360 | tf_op jit(solution)/shard_map/all_to_all | solution.py:191
  60.3 10.1 %copy-start.5 = (f32[128]{0:T(128)S(1)}, f32[128]{0:T(128)}, u32[]{:S(2)}) copy-start(f32[128]{0:T(128)} %param.9) | copy-start | bytes 1540
  71.2 19.1 %all-to-all-start.2 = ((bf16[16,80,128]{2,1,0:T(8,128)(2,1)}), bf16[16,80,128]{2,1,0:T(8,128)(2,1)S(1)}, u32[]{:S(2)}, u32[]{:S(2)}) async-start(bf16[16,80,128]{2,1,0:T(8,128)(2,1)} %broadcast_in_dim.13), calls=%async_computation.2 | async-start | bytes 655360 | tf_op jit(solution)/shard_map/all_to_all | solution.py:194
  82.6 7.6 %collective-permute-start.4 = (bf16[128,768]{1,0:T(8,128)(2,1)S(1)}, bf16[128,768]{1,0:T(8,128)(2,1)S(1)}, u32[]{:S(2)}, u32[]{:S(2)}) collective-permute-start(bf16[128,768]{1,0:T(8,128)(2,1)S(1)} %bitcast.55), channel_id=1, source_target_pairs={{0,2},{1,3},{2,0},{3,1},{4,6},{5,7},{6,4},{7,5},{8,10},{9,11},{10,... | collective-permute-start | bytes 589832 | tf_op jit(solution)/shard_map/ppermute | solution.py:200
  90.3 5.5 %collective-permute-start.3 = (bf16[2,640,128]{2,1,0:T(8,128)(2,1)S(1)}, bf16[2,640,128]{2,1,0:T(8,128)(2,1)S(1)}, u32[]{:S(2)}, u32[]{:S(2)}) collective-permute-start(bf16[2,640,128]{2,1,0:T(8,128)(2,1)S(1)} %bitcast.43), channel_id=1, source_target_pairs={{0,1},{1,0},{2,3},{3,2},{4,5},{5,4},{6,7},{7,6},{8,9},{9,8},{10,11... | collective-permute-start | bytes 983048 | tf_op jit(solution)/shard_map/ppermute | solution.py:200
  92.3 3.5 %collective-permute-start.5 = (bf16[256,384]{1,0:T(8,128)(2,1)S(1)}, bf16[256,384]{1,0:T(8,128)(2,1)S(1)}, u32[]{:S(2)}, u32[]{:S(2)}) collective-permute-start(bf16[256,384]{1,0:T(8,128)(2,1)S(1)} %get-tuple-element.37), channel_id=1, source_target_pairs={{0,1},{1,0},{2,3},{3,2},{4,5},{5,4},{6,7},{7,6},{8,9},{9,8},{10,11... | collective-permute-start | bytes 589832 | tf_op jit(solution)/shard_map/ppermute | solution.py:200
  97.9 23.4 %all-to-all-start.3 = ((bf16[16,40,384]{2,1,0:T(8,128)(2,1)}), bf16[16,40,384]{2,1,0:T(8,128)(2,1)S(1)}, u32[]{:S(2)}, u32[]{:S(2)}) async-start(bf16[16,40,384]{2,1,0:T(8,128)(2,1)} %bitcast.8), calls=%async_computation.3 | async-start | bytes 983040 | tf_op jit(solution)/shard_map/all_to_all | solution.py:197
  122.3 20.8 %all-to-all-start.4 = ((bf16[16,40,384]{2,1,0:T(8,128)(2,1)}), bf16[16,40,384]{2,1,0:T(8,128)(2,1)S(1)}, u32[]{:S(2)}, u32[]{:S(2)}) async-start(bf16[16,40,384]{2,1,0:T(8,128)(2,1)} %broadcast_in_dim.14), calls=%async_computation.4 | async-start | bytes 983040 | tf_op jit(solution)/shard_map/all_to_all | solution.py:197
  143.7 3.5 %collective-permute-start.6 = (bf16[2,640,128]{2,1,0:T(8,128)(2,1)S(1)}, bf16[2,640,128]{2,1,0:T(8,128)(2,1)S(1)}, u32[]{:S(2)}, u32[]{:S(2)}) collective-permute-start(bf16[2,640,128]{2,1,0:T(8,128)(2,1)S(1)} %get-tuple-element.19), channel_id=1, source_target_pairs={{0,1},{1,0},{2,3},{3,2},{4,5},{5,4},{6,7},{7,6},{8,9},{9,8},{10,11... | collective-permute-start | bytes 983048 | tf_op jit(solution)/shard_map/ppermute | solution.py:200
  148.0 21.8 %all-to-all-start.5 = ((bf16[16,80,128]{2,1,0:T(8,128)(2,1)}), bf16[16,80,128]{2,1,0:T(8,128)(2,1)S(1)}, u32[]{:S(2)}, u32[]{:S(2)}) async-start(bf16[16,80,128]{2,1,0:T(8,128)(2,1)} %bitcast.12), calls=%async_computation.5 | async-start | bytes 655360 | tf_op jit(solution)/shard_map/all_to_all | solution.py:194
  159.1 33.2 %collective-permute-start.1 = (bf16[640,768]{1,0:T(8,128)(2,1)S(1)}, bf16[640,768]{1,0:T(8,128)(2,1)}, u32[]{:S(2)}, u32[]{:S(2)}) collective-permute-start(bf16[640,768]{1,0:T(8,128)(2,1)S(1)} %reshape.162.own_ref), channel_id=1, source_target_pairs={{0,1},{1,0},{2,3},{3,2},{4,5},{5,4},{6,7},{7,6},{8,9},{9,8},{10,11... | collective-permute-start | bytes 2949128 | tf_op jit(solution)/shard_map/ppermute | solution.py:200
  162.4 26.4 %copy-start.2 = (f32[128,1,1536]{2,1,0:T(1,128)S(1)}, f32[128,1,1536]{2,1,0:T(1,128)}, u32[]{:S(2)}) copy-start(f32[128,1,1536]{2,1,0:T(1,128)} %param.12) | copy-start | bytes 2359300
  162.4 17.7 %collective-permute-start.8 = (f32[2,128,384]{2,1,0:T(8,128)}, f32[2,128,384]{2,1,0:T(8,128)S(1)}, u32[]{:S(2)}, u32[]{:S(2)}) collective-permute-start(f32[2,128,384]{2,1,0:T(8,128)} %get-tuple-element.22), channel_id=1, source_target_pairs={{0,1},{1,0},{2,3},{3,2},{4,5},{5,4},{6,7},{7,6},{8,9},{9,8},{10,11... | collective-permute-start | bytes 1179656 | tf_op jit(solution)/shard_map/ppermute | solution.py:200
  164.9 18.4 %collective-permute-start.7 = (f32[128,384]{1,0:T(8,128)}, f32[128,384]{1,0:T(8,128)S(1)}, u32[]{:S(2)}, u32[]{:S(2)}) collective-permute-start(f32[128,384]{1,0:T(8,128)} %get-tuple-element.21), channel_id=1, source_target_pairs={{0,2},{1,3},{2,0},{3,1},{4,6},{5,7},{6,4},{7,5},{8,10},{9,11},{10,... | collective-permute-start | bytes 589832 | tf_op jit(solution)/shard_map/ppermute | solution.py:200
  170.6 21.7 %all-to-all-start.6 = ((bf16[8,80,128]{2,1,0:T(8,128)(2,1)}), bf16[8,80,128]{2,1,0:T(8,128)(2,1)S(1)}, u32[]{:S(2)}, u32[]{:S(2)}) async-start(bf16[8,80,128]{2,1,0:T(8,128)(2,1)} %broadcast_in_dim.16), calls=%async_computation.6 | async-start | bytes 327680 | tf_op jit(solution)/shard_map/all_to_all | solution.py:191
  180.7 8.1 %collective-permute-start.9 = (f32[128,384]{1,0:T(8,128)}, f32[128,384]{1,0:T(8,128)S(1)}, u32[]{:S(2)}, u32[]{:S(2)}) collective-permute-start(f32[128,384]{1,0:T(8,128)} %slice_bitcast_fusion), channel_id=1, source_target_pairs={{0,2},{1,3},{2,0},{3,1},{4,6},{5,7},{6,4},{7,5},{8,10},{9,11},{10,... | collective-permute-start | bytes 589832 | tf_op jit(solution)/shard_map/ppermute | solution.py:200
  188.8 1.1 copy-start.3

commit v6 on v5

--- a/solution.py
+++ b/solution.py
@@ -50,27 +50,6 @@
 
 def whole(count):
     return [pl.BlockSpec(memory_space=pltpu.VMEM)] * count
-
-
-def decode_kernel(own_ref, other_ref, weight_ref, out_ref):
-    codes = jnp.concatenate([own_ref[0], own_ref[1], other_ref[0], other_ref[1]], axis=1)
-    out_ref[...] = lax.dot_general(
-        codes, weight_ref[...], (((1,), (0,)), ((), ())), preferred_element_type=jnp.float32
-    ).astype(jnp.bfloat16)
-
-
-def decode(own, other, weight):
-    rows, part = own.shape[1], weight.shape[1]
-    steps = 4
-    codes_spec = pl.BlockSpec((2, rows // steps, own.shape[2]), lambda i: (0, i, 0))
-    return pl.pallas_call(
-        decode_kernel,
-        grid=(steps,),
-        out_shape=jax.ShapeDtypeStruct((rows, part), jnp.bfloat16),
-        in_specs=[codes_spec, codes_spec, pl.BlockSpec(weight.shape, lambda i: (0, 0))],
-        out_specs=pl.BlockSpec((rows // steps, part), lambda i: (i, 0)),
-        **small(name="decode"),
-    )(own, other, weight)
 
 
 def grad_kernel(scale, chip_ref, errors_ref, weight_ref, norm_ref, own_ref, other_ref):
@@ -147,12 +126,14 @@
     flat = jax.ShapeDtypeStruct((lat_dev * width // LANES, LANES), jnp.float32)
     by_lat = lambda size: pl.BlockSpec((lats, size), lambda i: (i, 0))
     by_row = pl.BlockSpec((rows, LANES), lambda i: (i, 0))
+    first_of = pl.BlockSpec((1, lats, part), lambda i: (0, i, 0))
+    second_of = pl.BlockSpec((1, lats, part), lambda i: (1, i, 0))
     outs = pl.pallas_call(
         adam_kernel,
         grid=(steps,),
         out_shape=(flat, flat, flat),
         in_specs=[pl.BlockSpec(memory_space=pltpu.SMEM)]
-        + [by_lat(part), by_lat(part), pl.BlockSpec((1, lats, part), lambda i: (0, i, 0)), by_lat(part)]
+        + [by_lat(part), first_of, first_of, second_of]
         + [by_lat(width), by_lat(1), by_row, by_row],
         out_specs=(by_row, by_row, by_row),
         scratch_shapes=[pltpu.VMEM((TEAM, lats, part), jnp.float32)],
@@ -229,9 +210,12 @@
     acts, enc_own, enc_other = lax.optimization_barrier((acts, enc_own, enc_other))
     acts = acts.reshape(batch_rows, half)
 
-    dec_parts = dec_local.reshape(lat_dev, 2, 2, part)
-    keep = lax.dynamic_index_in_dim(dec_parts, chip, 2, keepdims=False).reshape(lat_dev, half)
-    give = lax.dynamic_index_in_dim(dec_parts, 1 - chip, 2, keepdims=False).reshape(lat_dev, half)
+    def chip_parts(index):
+        return jnp.concatenate(
+            [lax.dynamic_slice_in_dim(dec_local, k * half + index * part, part, 1) for k in range(2)], axis=1
+        )
+
+    keep, give = chip_parts(chip), chip_parts(1 - chip)
     dec_chips = lax.optimization_barrier(by_chip(keep, exchange(give, CHIP), 0))
     keep, give = split(dec_chips, 1, core)
     dec_other = exchange(give, CORE)
@@ -240,7 +224,8 @@
     own_norm = jnp.sqrt(jnp.sum(dec_float * dec_float, axis=1) + norm_epsilon)
 
     pre_other = exchange(mm(acts, enc_other, ((1,), (0,))), CORE)
-    pre_sent = (mm(acts, enc_own, ((1,), (0,))) + pre_other).reshape(snaps, block_rows, lat_dev)
+    pre_own = lax.optimization_barrier(mm(acts, enc_own, ((1,), (0,))))
+    pre_sent = (pre_own + pre_other).reshape(snaps, block_rows, lat_dev)
     pre = jnp.sum(over_snaps(pre_sent), axis=0) + enc_bias[None, :]
 
     codes_block = jnp.maximum(pre, 0.0).astype(jnp.bfloat16)
@@ -248,7 +233,8 @@
     codes_other = exchange(codes_chips, CORE)
     acts_other = exchange(acts, CORE)
 
-    sent = decode(codes_chips, codes_other, dec_team).reshape(teams, team_rows, part)
+    codes = jnp.concatenate([codes_chips[0], codes_chips[1], codes_other[0], codes_other[1]], axis=1)
+    sent = mm(codes, dec_team, ((1,), (0,))).astype(jnp.bfloat16).reshape(teams, team_rows, part)
     decoded = jnp.sum(over_teams(sent).astype(jnp.float32), axis=0)
     target = lax.dynamic_slice(acts, (team * team_rows, chip * part), (team_rows, part))
     bias_part = lax.dynamic_slice_in_dim(dec_bias[0], place * part, part, 0)
@@ -264,12 +250,12 @@
 
     acc_keep, acc_give, acc_core = acc_parts(scale_rec, chip.reshape(1), codes_chips, codes_other, errors)
     acc_core = exchange(acc_core, CORE)
+    acc_give = lax.optimization_barrier(jnp.stack([acc_give, acc_core[1]], axis=0))
     acc_chip = exchange(acc_give, CHIP)
-    acc_both = exchange(acc_core[1], CHIP)
     own_codes = lax.dynamic_index_in_dim(codes_chips, chip, 0, keepdims=False)
     code_total = jnp.sum(own_codes.astype(jnp.float32), axis=0)
     coef = (scale_sparse * code_total / own_norm)[:, None]
-    pieces = (acc_keep, acc_chip, acc_core, acc_both)
+    pieces = (acc_keep, acc_chip, acc_core, acc_chip)
     new_decoder, new_first, new_second = adam(place.reshape(1), pieces, dec_local, coef, dec_first, dec_second)
 
     enc_grad = encoder_grad(core.reshape(1), acts, acts_other, grad_pre).reshape(1, width, lat_dev)

time: 196 us -> 185 us (0.944)
  the two profiles are of different devices: /device:TPU:48 before, /device:TPU:16 now
where the time goes in v6:
time: 185 us; the launch traced here: 184 us
  waiting for transfers between devices  99 us (54%)
  starting transfers between devices  63.8 us (34%)
  local copies, waits for them, and re-layouts  9.54 us (5%)
  Pallas kernels  4.96 us (3%)
  other arithmetic  3.45 us (2%)
  matrix products  2.12 us (1%)
    all_to_all x2, waiting for transfers between devices, over_teams(): lax.all_to_all(x, 'lat', 0, 0, tiled=True, axis_index_groups=place_groups)  32.7 us
    all_to_all x1, waiting for transfers between devices, body(): acts = lax.all_to_all(sent, 'lat', 0, 0, tiled=True)  24.4 us
    ppermute x9, starting transfers between devices, exchange(): return lax.ppermute(x, 'lat', [(i, i ^ mask) for i in range(lats)])  20.8 us
    all_to_all x2, waiting for transfers between devices, over_snaps(): return lax.all_to_all(x, 'snap', 0, 0, tiled=True)  18.4 us
    all_to_all x2, waiting for transfers between devices, over_pairs(): lax.all_to_all(x, ('snap', 'lat'), 0, 0, tiled=True, axis_index_groups=pa...  18.4 us
    all_to_all x1, starting transfers between devices, body(): acts = lax.all_to_all(sent, 'lat', 0, 0, tiled=True)  14.5 us
    all_to_all x2, starting transfers between devices, over_teams(): lax.all_to_all(x, 'lat', 0, 0, tiled=True, axis_index_groups=place_groups)  11 us
    all_to_all x2, starting transfers between devices, over_snaps(): return lax.all_to_all(x, 'snap', 0, 0, tiled=True)  10.4 us
  transfers between devices with their start and end apart: 16, of which 11 were waited for; matrix products, arithmetic and copies ran while one was open for 2% of the time, Pallas kernels for 2%

profile of v6, /device:TPU:16, one launch (start us, length us, event | category | flops | bytes accessed | tf_op | source)
XLA Modules:
  0.0 183.9 jit_solution(15364471037368814298)
XLA Ops:
  0.6 0.8 reshape_squeeze.3
  1.5 1.3 broadcast_in_dim.12
  2.8 14.5 %all-to-all-start = ((bf16[64,60,128]{2,1,0:T(8,128)(2,1)}), bf16[64,60,128]{2,1,0:T(8,128)(2,1)S(1)}, u32[]{:S(2)}, u32[]{:S(2)}) async-start(bf16[64,60,128]{2,1,0:T(8,128)(2,1)} %bitcast.2), calls=%async_computation | async-start | bytes 2097152 | tf_op jit(solution)/shard_map/all_to_all | solution.py:206
  17.3 2.0 %collective-permute-start = (bf16[768,128]{1,0:T(8,128)(2,1)S(1)}, bf16[768,128]{1,0:T(8,128)(2,1)S(1)}, u32[]{:S(2)}, u32[]{:S(2)}) collective-permute-start(bf16[768,128]{1,0:T(8,128)(2,1)S(1)} %get-tuple-element.42), channel_id=1, source_target_pairs={{0,1},{1,0},{2,3},{3,2},{4,5},{5,4},{6,7},{7,6},{8,9},{9,8},{10,11... | collective-permute-start | bytes 589832 | tf_op jit(solution)/shard_map/ppermute | solution.py:181
  19.4 1.3 collective-permute-done
  20.7 24.4 %all-to-all-done = bf16[64,60,128]{2,1,0:T(8,128)(2,1)S(1)} async-done(((bf16[64,60,128]{2,1,0:T(8,128)(2,1)}), bf16[64,60,128]{2,1,0:T(8,128)(2,1)S(1)}, u32[]{:S(2)}, u32[]{:S(2)}) %all-to-all-start) | async-done | bytes 983072 | tf_op jit(solution)/shard_map/all_to_all | solution.py:206
  45.0 0.9 reshape.162.own_ref
  46.0 0.4 fusion.11
  46.4 2.6 %collective-permute-start.2 = (f32[640,128]{1,0:T(8,128)S(1)}, f32[640,128]{1,0:T(8,128)S(1)}, u32[]{:S(2)}, u32[]{:S(2)}) collective-permute-start(f32[640,128]{1,0:T(8,128)S(1)} %fusion.11), channel_id=1, source_target_pairs={{0,1},{1,0},{2,3},{3,2},{4,5},{5,4},{6,7},{7,6},{8,9},{9,8},{10,11... | collective-permute-start | bytes 983048 | tf_op jit(solution)/shard_map/ppermute | solution.py:181
  49.0 0.4 fusion.10
  49.4 0.8 collective-permute-done.2
  50.2 0.8 add.103
  50.9 7.0 %all-to-all-start.1 = ((f32[8,80,128]{2,1,0:T(8,128)}), f32[8,80,128]{2,1,0:T(8,128)S(1)}, u32[]{:S(2)}, u32[]{:S(2)}) async-start(f32[8,80,128]{2,1,0:T(8,128)} %bitcast.5), calls=%async_computation.1 | async-start | bytes 655360 | tf_op jit(solution)/shard_map/all_to_all | solution.py:172
  58.0 2.3 %collective-permute-start.4 = (bf16[128,768]{1,0:T(8,128)(2,1)S(1)}, bf16[128,768]{1,0:T(8,128)(2,1)S(1)}, u32[]{:S(2)}, u32[]{:S(2)}) collective-permute-start(bf16[128,768]{1,0:T(8,128)(2,1)S(1)} %pad_maximum_fusion.4), channel_id=1, source_target_pairs={{0,2},{1,3},{2,0},{3,1},{4,6},{5,7},{6,4},{7,5},{8,10},{9,11},{10,... | collective-permute-start | bytes 589832 | tf_op jit(solution)/shard_map/ppermute | solution.py:181
  60.3 13.1 %all-to-all-done.1 = f32[8,80,128]{2,1,0:T(8,128)S(1)} async-done(((f32[8,80,128]{2,1,0:T(8,128)}), f32[8,80,128]{2,1,0:T(8,128)S(1)}, u32[]{:S(2)}, u32[]{:S(2)}) %all-to-all-start.1) | async-done | bytes 327712 | tf_op jit(solution)/shard_map/all_to_all | solution.py:172
  73.5 0.8 broadcast_in_dim.13
  74.3 3.5 %all-to-all-start.2 = ((bf16[16,80,128]{2,1,0:T(8,128)(2,1)}), bf16[16,80,128]{2,1,0:T(8,128)(2,1)S(1)}, u32[]{:S(2)}, u32[]{:S(2)}) async-start(bf16[16,80,128]{2,1,0:T(8,128)(2,1)} %broadcast_in_dim.13), calls=%async_computation.2 | async-start | bytes 655360 | tf_op jit(solution)/shard_map/all_to_all | solution.py:175
  78.0 1.9 %collective-permute-start.5 = (bf16[256,384]{1,0:T(8,128)(2,1)S(1)}, bf16[256,384]{1,0:T(8,128)(2,1)S(1)}, u32[]{:S(2)}, u32[]{:S(2)}) collective-permute-start(bf16[256,384]{1,0:T(8,128)(2,1)S(1)} %get-tuple-element.35), channel_id=1, source_target_pairs={{0,1},{1,0},{2,3},{3,2},{4,5},{5,4},{6,7},{7,6},{8,9},{9,8},{10,11... | collective-permute-start | bytes 589832 | tf_op jit(solution)/shard_map/ppermute | solution.py:181
  79.9 11.7 %all-to-all-done.2 = bf16[16,80,128]{2,1,0:T(8,128)(2,1)S(1)} async-done(((bf16[16,80,128]{2,1,0:T(8,128)(2,1)}), bf16[16,80,128]{2,1,0:T(8,128)(2,1)S(1)}, u32[]{:S(2)}, u32[]{:S(2)}) %all-to-all-start.2) | async-done | bytes 327712 | tf_op jit(solution)/shard_map/all_to_all | solution.py:175
  91.6 1.9 %collective-permute-start.3 = (bf16[2,640,128]{2,1,0:T(8,128)(2,1)S(1)}, bf16[2,640,128]{2,1,0:T(8,128)(2,1)S(1)}, u32[]{:S(2)}, u32[]{:S(2)}) collective-permute-start(bf16[2,640,128]{2,1,0:T(8,128)(2,1)S(1)} %bitcast.51), channel_id=1, source_target_pairs={{0,1},{1,0},{2,3},{3,2},{4,5},{5,4},{6,7},{7,6},{8,9},{9,8},{10,11... | collective-permute-start | bytes 983048 | tf_op jit(solution)/shard_map/ppermute | solution.py:181
  93.6 1.5 collective-permute-done.3.other_ref
  95.1 1.3 convolution_convert_fusion
  96.4 6.3 %all-to-all-start.3 = ((bf16[16,40,384]{2,1,0:T(8,128)(2,1)}), bf16[16,40,384]{2,1,0:T(8,128)(2,1)S(1)}, u32[]{:S(2)}, u32[]{:S(2)}) async-start(bf16[16,40,384]{2,1,0:T(8,128)(2,1)} %bitcast.16), calls=%async_computation.3 | async-start | bytes 983040 | tf_op jit(solution)/shard_map/all_to_all | solution.py:178
  102.7 16.8 %all-to-all-done.3 = bf16[16,40,384]{2,1,0:T(8,128)(2,1)S(1)} async-done(((bf16[16,40,384]{2,1,0:T(8,128)(2,1)}), bf16[16,40,384]{2,1,0:T(8,128)(2,1)S(1)}, u32[]{:S(2)}, u32[]{:S(2)}) %all-to-all-start.3) | async-done | bytes 491552 | tf_op jit(solution)/shard_map/all_to_all | solution.py:178
  119.6 0.8 broadcast_in_dim.14
  120.4 4.8 %all-to-all-start.4 = ((bf16[16,40,384]{2,1,0:T(8,128)(2,1)}), bf16[16,40,384]{2,1,0:T(8,128)(2,1)S(1)}, u32[]{:S(2)}, u32[]{:S(2)}) async-start(bf16[16,40,384]{2,1,0:T(8,128)(2,1)} %broadcast_in_dim.14), calls=%async_computation.4 | async-start | bytes 983040 | tf_op jit(solution)/shard_map/all_to_all | solution.py:178
  125.5 0.5 multiply_bitcast_fusion
  126.0 15.9 %all-to-all-done.4 = bf16[16,40,384]{2,1,0:T(8,128)(2,1)S(1)} async-done(((bf16[16,40,384]{2,1,0:T(8,128)(2,1)}), bf16[16,40,384]{2,1,0:T(8,128)(2,1)S(1)}, u32[]{:S(2)}, u32[]{:S(2)}) %all-to-all-start.4) | async-done | bytes 491552 | tf_op jit(solution)/shard_map/all_to_all | solution.py:178
  141.9 0.7 grad_parts.1
  142.6 1.9 %collective-permute-start.6 = (bf16[2,640,128]{2,1,0:T(8,128)(2,1)S(1)}, bf16[2,640,128]{2,1,0:T(8,128)(2,1)S(1)}, u32[]{:S(2)}, u32[]{:S(2)}) collective-permute-start(bf16[2,640,128]{2,1,0:T(8,128)(2,1)S(1)} %get-tuple-element.19), channel_id=1, source_target_pairs={{0,1},{1,0},{2,3},{3,2},{4,5},{5,4},{6,7},{7,6},{8,9},{9,8},{10,11... | collective-permute-start | bytes 983048 | tf_op jit(solution)/shard_map/ppermute | solution.py:181
  144.5 1.6 collective-permute-done.6
  146.1 0.8 add_convert_fusion
  146.9 3.5 %all-to-all-start.5 = ((bf16[16,80,128]{2,1,0:T(8,128)(2,1)}), bf16[16,80,128]{2,1,0:T(8,128)(2,1)S(1)}, u32[]{:S(2)}, u32[]{:S(2)}) async-start(bf16[16,80,128]{2,1,0:T(8,128)(2,1)} %bitcast.20), calls=%async_computation.5 | async-start | bytes 655360 | tf_op jit(solution)/shard_map/all_to_all | solution.py:175
  150.4 0.6 acc_parts.1
  151.1 0.7 copy-done.4
  151.8 2.2 %collective-permute-start.7 = (f32[2,128,384]{2,1,0:T(8,128)S(1)}, f32[2,128,384]{2,1,0:T(8,128)S(1)}, u32[]{:S(2)}, u32[]{:S(2)}) collective-permute-start(f32[2,128,384]{2,1,0:T(8,128)S(1)} %get-tuple-element.22), channel_id=1, source_target_pairs={{0,1},{1,0},{2,3},{3,2},{4,5},{5,4},{6,7},{7,6},{8,9},{9,8},{10,11... | collective-permute-start | bytes 1179656 | tf_op jit(solution)/shard_map/ppermute | solution.py:181
  153.9 2.3 %collective-permute-start.1 = (bf16[640,768]{1,0:T(8,128)(2,1)S(1)}, bf16[640,768]{1,0:T(8,128)(2,1)S(1)}, u32[]{:S(2)}, u32[]{:S(2)}) collective-permute-start(bf16[640,768]{1,0:T(8,128)(2,1)S(1)} %reshape.162.own_ref), channel_id=1, source_target_pairs={{0,1},{1,0},{2,3},{3,2},{4,5},{5,4},{6,7},{7,6},{8,9},{9,8},{10,11... | collective-permute-start | bytes 2949128 | tf_op jit(solution)/shard_map/ppermute | solution.py:181
  156.3 0.8 pad_maximum_fusion.2
  157.0 3.7 %collective-permute-start.8 = (f32[2,128,384]{2,1,0:T(8,128)}, f32[2,128,384]{2,1,0:T(8,128)S(1)}, u32[]{:S(2)}, u32[]{:S(2)}) collective-permute-start(f32[2,128,384]{2,1,0:T(8,128)} %pad_maximum_fusion.2), channel_id=1, source_target_pairs={{0,2},{1,3},{2,0},{3,1},{4,6},{5,7},{6,4},{7,5},{8,10},{9,11},{10,... | collective-permute-start | bytes 1179656 | tf_op jit(solution)/shard_map/ppermute | solution.py:181
  160.8 6.7 %all-to-all-done.5 = bf16[16,80,128]{2,1,0:T(8,128)(2,1)S(1)} async-done(((bf16[16,80,128]{2,1,0:T(8,128)(2,1)}), bf16[16,80,128]{2,1,0:T(8,128)(2,1)S(1)}, u32[]{:S(2)}, u32[]{:S(2)}) %all-to-all-start.5) | async-done | bytes 327712 | tf_op jit(solution)/shard_map/all_to_all | solution.py:175
  167.6 0.7 broadcast_in_dim.16
  168.2 3.4 %all-to-all-start.6 = ((bf16[8,80,128]{2,1,0:T(8,128)(2,1)}), bf16[8,80,128]{2,1,0:T(8,128)(2,1)S(1)}, u32[]{:S(2)}, u32[]{:S(2)}) async-start(bf16[8,80,128]{2,1,0:T(8,128)(2,1)} %broadcast_in_dim.16), calls=%async_computation.6 | async-start | bytes 327680 | tf_op jit(solution)/shard_map/all_to_all | solution.py:172
  171.8 1.1 copy-done.2
  172.9 1.1 copy-done.3
  174.0 0.9 copy-done.5
  175.0 2.3 %adam.1 = (f32[1536,128]{1,0:T(8,128)}, f32[1536,128]{1,0:T(8,128)}, f32[1536,128]{1,0:T(8,128)}) custom-call(s32[1]{0:T(128)} %bitcast.23.place_ref, f32[128,384]{1,0:T(8,128)S(1)} %copy-done.5, f32[2,128,384]{2,1,0:T(8,128)S(1)} %collective-permute-done.8.p1.p3, f32[2,128,384]{2,1,0:T(8,128)S(1)} %collective-permute-done.7.p2, ...), custom_call_target="tpu_custom_call" | custom-call | tf_op jit(solution)/shard_map/adam/pallas_call | solution.py:131
  177.3 5.3 %all-to-all-done.6 = bf16[8,80,128]{2,1,0:T(8,128)(2,1)S(1)} async-done(((bf16[8,80,128]{2,1,0:T(8,128)(2,1)}), bf16[8,80,128]{2,1,0:T(8,128)(2,1)S(1)}, u32[]{:S(2)}, u32[]{:S(2)}) %all-to-all-start.6) | async-done | bytes 163872 | tf_op jit(solution)/shard_map/all_to_all | solution.py:172
  182.6 1.3 encoder_grad.1
  (43 shorter events, 1.1 us)
Async XLA Ops:
  0.6 102.0 %copy-start = (f32[1,1536]{1,0:T(1,128)S(1)}, f32[1,1536]{1,0:T(1,128)}, u32[]{:S(2)}) copy-start(f32[1,1536]{1,0:T(1,128)} %param.11) | copy-start | bytes 18436
  2.8 14.5 %copy-start.6 = (bf16[1,1536,128]{2,1,0:T(8,128)(2,1)S(1)}, bf16[1,1536,128]{2,1,0:T(8,128)(2,1)}, u32[]{:S(2)}) copy-start(bf16[1,1536,128]{2,1,0:T(8,128)(2,1)} %param.8) | copy-start | bytes 1179652
  2.8 42.2 %all-to-all-start = ((bf16[64,60,128]{2,1,0:T(8,128)(2,1)}), bf16[64,60,128]{2,1,0:T(8,128)(2,1)S(1)}, u32[]{:S(2)}, u32[]{:S(2)}) async-start(bf16[64,60,128]{2,1,0:T(8,128)(2,1)} %bitcast.2), calls=%async_computation | async-start | bytes 2097152 | tf_op jit(solution)/shard_map/all_to_all | solution.py:206
  17.3 3.3 %collective-permute-start = (bf16[768,128]{1,0:T(8,128)(2,1)S(1)}, bf16[768,128]{1,0:T(8,128)(2,1)S(1)}, u32[]{:S(2)}, u32[]{:S(2)}) collective-permute-start(bf16[768,128]{1,0:T(8,128)(2,1)S(1)} %get-tuple-element.42), channel_id=1, source_target_pairs={{0,1},{1,0},{2,3},{3,2},{4,5},{5,4},{6,7},{7,6},{8,9},{9,8},{10,11... | collective-permute-start | bytes 589832 | tf_op jit(solution)/shard_map/ppermute | solution.py:181
  46.4 3.8 %collective-permute-start.2 = (f32[640,128]{1,0:T(8,128)S(1)}, f32[640,128]{1,0:T(8,128)S(1)}, u32[]{:S(2)}, u32[]{:S(2)}) collective-permute-start(f32[640,128]{1,0:T(8,128)S(1)} %fusion.11), channel_id=1, source_target_pairs={{0,1},{1,0},{2,3},{3,2},{4,5},{5,4},{6,7},{7,6},{8,9},{9,8},{10,11... | collective-permute-start | bytes 983048 | tf_op jit(solution)/shard_map/ppermute | solution.py:181
  49.4 8.6 %copy-start.1 = (bf16[128,1,1536]{2,0,1:T(8,128)(2,1)S(1)}, bf16[128,1,1536]{2,0,1:T(8,128)(2,1)}, u32[]{:S(2)}) copy-start(bf16[128,1,1536]{2,0,1:T(8,128)(2,1)} %param.10) | copy-start | bytes 1179652
  50.9 22.5 %copy-start.7 = (f32[128]{0:T(128)S(1)}, f32[128]{0:T(128)}, u32[]{:S(2)}) copy-start(f32[128]{0:T(128)} %param.9) | copy-start | bytes 1540
  50.9 22.5 %all-to-all-start.1 = ((f32[8,80,128]{2,1,0:T(8,128)}), f32[8,80,128]{2,1,0:T(8,128)S(1)}, u32[]{:S(2)}, u32[]{:S(2)}) async-start(f32[8,80,128]{2,1,0:T(8,128)} %bitcast.5), calls=%async_computation.1 | async-start | bytes 655360 | tf_op jit(solution)/shard_map/all_to_all | solution.py:172
  58.0 19.8 %collective-permute-start.4 = (bf16[128,768]{1,0:T(8,128)(2,1)S(1)}, bf16[128,768]{1,0:T(8,128)(2,1)S(1)}, u32[]{:S(2)}, u32[]{:S(2)}) collective-permute-start(bf16[128,768]{1,0:T(8,128)(2,1)S(1)} %pad_maximum_fusion.4), channel_id=1, source_target_pairs={{0,2},{1,3},{2,0},{3,1},{4,6},{5,7},{6,4},{7,5},{8,10},{9,11},{10,... | collective-permute-start | bytes 589832 | tf_op jit(solution)/shard_map/ppermute | solution.py:181
  74.3 17.3 %all-to-all-start.2 = ((bf16[16,80,128]{2,1,0:T(8,128)(2,1)}), bf16[16,80,128]{2,1,0:T(8,128)(2,1)S(1)}, u32[]{:S(2)}, u32[]{:S(2)}) async-start(bf16[16,80,128]{2,1,0:T(8,128)(2,1)} %broadcast_in_dim.13), calls=%async_computation.2 | async-start | bytes 655360 | tf_op jit(solution)/shard_map/all_to_all | solution.py:175
  78.0 15.5 %collective-permute-start.5 = (bf16[256,384]{1,0:T(8,128)(2,1)S(1)}, bf16[256,384]{1,0:T(8,128)(2,1)S(1)}, u32[]{:S(2)}, u32[]{:S(2)}) collective-permute-start(bf16[256,384]{1,0:T(8,128)(2,1)S(1)} %get-tuple-element.35), channel_id=1, source_target_pairs={{0,1},{1,0},{2,3},{3,2},{4,5},{5,4},{6,7},{7,6},{8,9},{9,8},{10,11... | collective-permute-start | bytes 589832 | tf_op jit(solution)/shard_map/ppermute | solution.py:181
  91.6 3.5 %collective-permute-start.3 = (bf16[2,640,128]{2,1,0:T(8,128)(2,1)S(1)}, bf16[2,640,128]{2,1,0:T(8,128)(2,1)S(1)}, u32[]{:S(2)}, u32[]{:S(2)}) collective-permute-start(bf16[2,640,128]{2,1,0:T(8,128)(2,1)S(1)} %bitcast.51), channel_id=1, source_target_pairs={{0,1},{1,0},{2,3},{3,2},{4,5},{5,4},{6,7},{7,6},{8,9},{9,8},{10,11... | collective-permute-start | bytes 983048 | tf_op jit(solution)/shard_map/ppermute | solution.py:181
  96.4 23.1 %all-to-all-start.3 = ((bf16[16,40,384]{2,1,0:T(8,128)(2,1)}), bf16[16,40,384]{2,1,0:T(8,128)(2,1)S(1)}, u32[]{:S(2)}, u32[]{:S(2)}) async-start(bf16[16,40,384]{2,1,0:T(8,128)(2,1)} %bitcast.16), calls=%async_computation.3 | async-start | bytes 983040 | tf_op jit(solution)/shard_map/all_to_all | solution.py:178
  120.4 21.5 %all-to-all-start.4 = ((bf16[16,40,384]{2,1,0:T(8,128)(2,1)}), bf16[16,40,384]{2,1,0:T(8,128)(2,1)S(1)}, u32[]{:S(2)}, u32[]{:S(2)}) async-start(bf16[16,40,384]{2,1,0:T(8,128)(2,1)} %broadcast_in_dim.14), calls=%async_computation.4 | async-start | bytes 983040 | tf_op jit(solution)/shard_map/all_to_all | solution.py:178
  142.6 3.5 %collective-permute-start.6 = (bf16[2,640,128]{2,1,0:T(8,128)(2,1)S(1)}, bf16[2,640,128]{2,1,0:T(8,128)(2,1)S(1)}, u32[]{:S(2)}, u32[]{:S(2)}) collective-permute-start(bf16[2,640,128]{2,1,0:T(8,128)(2,1)S(1)} %get-tuple-element.19), channel_id=1, source_target_pairs={{0,1},{1,0},{2,3},{3,2},{4,5},{5,4},{6,7},{7,6},{8,9},{9,8},{10,11... | collective-permute-start | bytes 983048 | tf_op jit(solution)/shard_map/ppermute | solution.py:181
  146.9 20.6 %all-to-all-start.5 = ((bf16[16,80,128]{2,1,0:T(8,128)(2,1)}), bf16[16,80,128]{2,1,0:T(8,128)(2,1)S(1)}, u32[]{:S(2)}, u32[]{:S(2)}) async-start(bf16[16,80,128]{2,1,0:T(8,128)(2,1)} %bitcast.20), calls=%async_computation.5 | async-start | bytes 655360 | tf_op jit(solution)/shard_map/all_to_all | solution.py:175
  151.1 0.7 copy-start.4
  151.8 15.8 %copy-start.8 = (f32[128]{0:T(128)S(1)}, f32[128]{0:T(128)}, u32[]{:S(2)}) copy-start(f32[128]{0:T(128)} %param.9) | copy-start | bytes 1540
  151.8 19.9 %copy-start.9 = (f32[128,1]{0,1:T(1,128)S(1)}, f32[128,1]{0,1:T(1,128)}, u32[]{:S(2)}) copy-start(f32[128,1]{0,1:T(1,128)} %get-tuple-element.48) | copy-start | bytes 1540
  151.8 4.5 %collective-permute-start.7 = (f32[2,128,384]{2,1,0:T(8,128)S(1)}, f32[2,128,384]{2,1,0:T(8,128)S(1)}, u32[]{:S(2)}, u32[]{:S(2)}) collective-permute-start(f32[2,128,384]{2,1,0:T(8,128)S(1)} %get-tuple-element.22), channel_id=1, source_target_pairs={{0,1},{1,0},{2,3},{3,2},{4,5},{5,4},{6,7},{7,6},{8,9},{9,8},{10,11... | collective-permute-start | bytes 1179656 | tf_op jit(solution)/shard_map/ppermute | solution.py:181
  153.9 23.4 %collective-permute-start.1 = (bf16[640,768]{1,0:T(8,128)(2,1)S(1)}, bf16[640,768]{1,0:T(8,128)(2,1)S(1)}, u32[]{:S(2)}, u32[]{:S(2)}) collective-permute-start(bf16[640,768]{1,0:T(8,128)(2,1)S(1)} %reshape.162.own_ref), channel_id=1, source_target_pairs={{0,1},{1,0},{2,3},{3,2},{4,5},{5,4},{6,7},{7,6},{8,9},{9,8},{10,11... | collective-permute-start | bytes 2949128 | tf_op jit(solution)/shard_map/ppermute | solution.py:181
  157.0 14.7 %collective-permute-start.8 = (f32[2,128,384]{2,1,0:T(8,128)}, f32[2,128,384]{2,1,0:T(8,128)S(1)}, u32[]{:S(2)}, u32[]{:S(2)}) collective-permute-start(f32[2,128,384]{2,1,0:T(8,128)} %pad_maximum_fusion.2), channel_id=1, source_target_pairs={{0,2},{1,3},{2,0},{3,1},{4,6},{5,7},{6,4},{7,5},{8,10},{9,11},{10,... | collective-permute-start | bytes 1179656 | tf_op jit(solution)/shard_map/ppermute | solution.py:181
  168.2 14.3 %all-to-all-start.6 = ((bf16[8,80,128]{2,1,0:T(8,128)(2,1)}), bf16[8,80,128]{2,1,0:T(8,128)(2,1)S(1)}, u32[]{:S(2)}, u32[]{:S(2)}) async-start(bf16[8,80,128]{2,1,0:T(8,128)(2,1)} %broadcast_in_dim.16), calls=%async_computation.6 | async-start | bytes 327680 | tf_op jit(solution)/shard_map/all_to_all | solution.py:172
  171.8 1.1 copy-start.2
  172.9 1.1 copy-start.3
  174.0 0.9 copy-start.5

commit v7 on v6

--- a/solution.py
+++ b/solution.py
@@ -162,14 +162,15 @@
     chip = lax.bitwise_and(lax.shift_right_logical(lat, 1), 1)
     place = 2 * core + chip
     place_groups = [[t * TEAM + p for t in range(teams)] for p in range(TEAM)]
+    snap_order = [h * (snaps // 2) + x for x in range(snaps // 2) for h in range(2)]
     pair_groups = [
-        [c * lats + t * TEAM + 2 * z + k for z in range(2) for c in range(snaps)]
+        [c * lats + t * TEAM + 2 * z + k for z in range(2) for c in snap_order]
         for t in range(teams)
         for k in range(2)
     ]
 
     def over_snaps(x):
-        return lax.all_to_all(x, "snap", 0, 0, tiled=True)
+        return lax.all_to_all(x, "snap", 0, 0, tiled=True, axis_index_groups=[snap_order])
 
     def over_pairs(x):
         return lax.all_to_all(x, ("snap", "lat"), 0, 0, tiled=True, axis_index_groups=pair_groups)
@@ -200,8 +201,7 @@
     enc_local = enc_weight[0]
     dec_local = dec_weight[:, 0, :]
 
-    sent = rows.reshape(rows_dev, 2, half).transpose(1, 0, 2)
-    sent = sent.reshape(2, rows_dev * half // LANES, LANES)
+    sent = jnp.stack([rows[:, k * half : (k + 1) * half].reshape(rows_dev * half // LANES, LANES) for k in range(2)])
     sent = repeat(sent, lats // 2).reshape((lats,) + sent.shape[1:])
     acts = lax.all_to_all(sent, "lat", 0, 0, tiled=True)
 

time: 185 us -> 184 us (level)
  waiting for transfers between devices: 99 us -> 95.6 us
  starting transfers between devices: 63.8 us -> 66.1 us
    all_to_all x2, waiting for transfers between devices: 18.4 us -> 14.9 us  [over_pairs(): lax.all_to_all(x, ('snap', 'lat'), 0, 0, tiled=True, axis_index_groups=pa...]
  transfers between devices with their start and end apart: 16 -> 16, of which waited for: 11 -> 12; matrix products, arithmetic and copies ran while one was open for 2% -> 2% of each run, Pallas kernels for 2% -> 2%
where the time goes in v7:
time: 184 us; the launch traced here: 183 us
  waiting for transfers between devices  95.6 us (52%)
  starting transfers between devices  66.1 us (36%)
  local copies, waits for them, and re-layouts  9.52 us (5%)
  Pallas kernels  4.96 us (3%)
  other arithmetic  3.46 us (2%)
  matrix products  2.12 us (1%)
    all_to_all x2, waiting for transfers between devices, over_teams(): lax.all_to_all(x, 'lat', 0, 0, tiled=True, axis_index_groups=place_groups)  31.5 us
    all_to_all x1, waiting for transfers between devices, body(): acts = lax.all_to_all(sent, 'lat', 0, 0, tiled=True)  24.4 us
    ppermute x9, starting transfers between devices, exchange(): return lax.ppermute(x, 'lat', [(i, i ^ mask) for i in range(lats)])  20.9 us
    all_to_all x2, waiting for transfers between devices, over_snaps(): lax.all_to_all(x, 'snap', 0, 0, tiled=True, axis_index_groups=[snap_order])  18.5 us
    all_to_all x2, waiting for transfers between devices, over_pairs(): lax.all_to_all(x, ('snap', 'lat'), 0, 0, tiled=True, axis_index_groups=pa...  14.9 us
    all_to_all x1, starting transfers between devices, body(): acts = lax.all_to_all(sent, 'lat', 0, 0, tiled=True)  14.5 us
    all_to_all x2, starting transfers between devices, over_teams(): lax.all_to_all(x, 'lat', 0, 0, tiled=True, axis_index_groups=place_groups)  11.5 us
    all_to_all x2, starting transfers between devices, over_snaps(): lax.all_to_all(x, 'snap', 0, 0, tiled=True, axis_index_groups=[snap_order])  11.1 us
  transfers between devices with their start and end apart: 16, of which 12 were waited for; matrix products, arithmetic and copies ran while one was open for 2% of the time, Pallas kernels for 2%

profile of v7, /device:TPU:16, one launch (start us, length us, event | category | flops | bytes accessed | tf_op | source)
XLA Modules:
  0.0 182.8 jit_solution(17714872233979345895)
XLA Ops:
  0.6 0.8 fusion.10
  1.5 1.3 broadcast_in_dim.9
  2.8 14.5 %all-to-all-start = ((bf16[64,60,128]{2,1,0:T(8,128)(2,1)}), bf16[64,60,128]{2,1,0:T(8,128)(2,1)S(1)}, u32[]{:S(2)}, u32[]{:S(2)}) async-start(bf16[64,60,128]{2,1,0:T(8,128)(2,1)} %bitcast.2), calls=%async_computation | async-start | bytes 2097152 | tf_op jit(solution)/shard_map/all_to_all | solution.py:206
  17.3 2.0 %collective-permute-start = (bf16[768,128]{1,0:T(8,128)(2,1)S(1)}, bf16[768,128]{1,0:T(8,128)(2,1)S(1)}, u32[]{:S(2)}, u32[]{:S(2)}) collective-permute-start(bf16[768,128]{1,0:T(8,128)(2,1)S(1)} %get-tuple-element.42), channel_id=1, source_target_pairs={{0,1},{1,0},{2,3},{3,2},{4,5},{5,4},{6,7},{7,6},{8,9},{9,8},{10,11... | collective-permute-start | bytes 589832 | tf_op jit(solution)/shard_map/ppermute | solution.py:182
  19.4 1.3 collective-permute-done
  20.7 24.4 %all-to-all-done = bf16[64,60,128]{2,1,0:T(8,128)(2,1)S(1)} async-done(((bf16[64,60,128]{2,1,0:T(8,128)(2,1)}), bf16[64,60,128]{2,1,0:T(8,128)(2,1)S(1)}, u32[]{:S(2)}, u32[]{:S(2)}) %all-to-all-start) | async-done | bytes 983072 | tf_op jit(solution)/shard_map/all_to_all | solution.py:206
  45.0 0.9 reshape.162.own_ref
  45.9 0.4 fusion.12
  46.4 2.6 %collective-permute-start.2 = (f32[640,128]{1,0:T(8,128)S(1)}, f32[640,128]{1,0:T(8,128)S(1)}, u32[]{:S(2)}, u32[]{:S(2)}) collective-permute-start(f32[640,128]{1,0:T(8,128)S(1)} %fusion.12), channel_id=1, source_target_pairs={{0,1},{1,0},{2,3},{3,2},{4,5},{5,4},{6,7},{7,6},{8,9},{9,8},{10,11... | collective-permute-start | bytes 983048 | tf_op jit(solution)/shard_map/ppermute | solution.py:182
  49.4 0.8 collective-permute-done.2
  50.2 0.8 add.103
  50.9 7.0 %all-to-all-start.1 = ((f32[8,80,128]{2,1,0:T(8,128)}), f32[8,80,128]{2,1,0:T(8,128)S(1)}, u32[]{:S(2)}, u32[]{:S(2)}) async-start(f32[8,80,128]{2,1,0:T(8,128)} %bitcast.5), calls=%async_computation.1 | async-start | bytes 655360 | tf_op jit(solution)/shard_map/all_to_all | solution.py:173
  58.0 2.3 %collective-permute-start.4 = (bf16[128,768]{1,0:T(8,128)(2,1)S(1)}, bf16[128,768]{1,0:T(8,128)(2,1)S(1)}, u32[]{:S(2)}, u32[]{:S(2)}) collective-permute-start(bf16[128,768]{1,0:T(8,128)(2,1)S(1)} %pad_maximum_fusion.4), channel_id=1, source_target_pairs={{0,2},{1,3},{2,0},{3,1},{4,6},{5,7},{6,4},{7,5},{8,10},{9,11},{10,... | collective-permute-start | bytes 589832 | tf_op jit(solution)/shard_map/ppermute | solution.py:182
  60.3 13.5 %all-to-all-done.1 = f32[8,80,128]{2,1,0:T(8,128)S(1)} async-done(((f32[8,80,128]{2,1,0:T(8,128)}), f32[8,80,128]{2,1,0:T(8,128)S(1)}, u32[]{:S(2)}, u32[]{:S(2)}) %all-to-all-start.1) | async-done | bytes 327712 | tf_op jit(solution)/shard_map/all_to_all | solution.py:173
  73.9 0.8 broadcast_in_dim.10
  74.7 3.5 %all-to-all-start.2 = ((bf16[16,80,128]{2,1,0:T(8,128)(2,1)}), bf16[16,80,128]{2,1,0:T(8,128)(2,1)S(1)}, u32[]{:S(2)}, u32[]{:S(2)}) async-start(bf16[16,80,128]{2,1,0:T(8,128)(2,1)} %broadcast_in_dim.10), calls=%async_computation.2 | async-start | bytes 655360 | tf_op jit(solution)/shard_map/all_to_all | solution.py:176
  78.4 1.9 %collective-permute-start.5 = (bf16[256,384]{1,0:T(8,128)(2,1)S(1)}, bf16[256,384]{1,0:T(8,128)(2,1)S(1)}, u32[]{:S(2)}, u32[]{:S(2)}) collective-permute-start(bf16[256,384]{1,0:T(8,128)(2,1)S(1)} %get-tuple-element.35), channel_id=1, source_target_pairs={{0,1},{1,0},{2,3},{3,2},{4,5},{5,4},{6,7},{7,6},{8,9},{9,8},{10,11... | collective-permute-start | bytes 589832 | tf_op jit(solution)/shard_map/ppermute | solution.py:182
  80.3 9.9 %all-to-all-done.2 = bf16[16,80,128]{2,1,0:T(8,128)(2,1)S(1)} async-done(((bf16[16,80,128]{2,1,0:T(8,128)(2,1)}), bf16[16,80,128]{2,1,0:T(8,128)(2,1)S(1)}, u32[]{:S(2)}, u32[]{:S(2)}) %all-to-all-start.2) | async-done | bytes 327712 | tf_op jit(solution)/shard_map/all_to_all | solution.py:176
  90.2 1.9 %collective-permute-start.3 = (bf16[2,640,128]{2,1,0:T(8,128)(2,1)S(1)}, bf16[2,640,128]{2,1,0:T(8,128)(2,1)S(1)}, u32[]{:S(2)}, u32[]{:S(2)}) collective-permute-start(bf16[2,640,128]{2,1,0:T(8,128)(2,1)S(1)} %bitcast.49), channel_id=1, source_target_pairs={{0,1},{1,0},{2,3},{3,2},{4,5},{5,4},{6,7},{7,6},{8,9},{9,8},{10,11... | collective-permute-start | bytes 983048 | tf_op jit(solution)/shard_map/ppermute | solution.py:182
  92.2 1.5 collective-permute-done.3.other_ref
  93.8 1.3 convolution_convert_fusion
  95.0 6.3 %all-to-all-start.3 = ((bf16[16,40,384]{2,1,0:T(8,128)(2,1)}), bf16[16,40,384]{2,1,0:T(8,128)(2,1)S(1)}, u32[]{:S(2)}, u32[]{:S(2)}) async-start(bf16[16,40,384]{2,1,0:T(8,128)(2,1)} %bitcast.16), calls=%async_computation.3 | async-start | bytes 983040 | tf_op jit(solution)/shard_map/all_to_all | solution.py:179
  101.4 16.8 %all-to-all-done.3 = bf16[16,40,384]{2,1,0:T(8,128)(2,1)S(1)} async-done(((bf16[16,40,384]{2,1,0:T(8,128)(2,1)}), bf16[16,40,384]{2,1,0:T(8,128)(2,1)S(1)}, u32[]{:S(2)}, u32[]{:S(2)}) %all-to-all-start.3) | async-done | bytes 491552 | tf_op jit(solution)/shard_map/all_to_all | solution.py:179
  118.3 0.8 broadcast_in_dim.11
  119.1 5.2 %all-to-all-start.4 = ((bf16[16,40,384]{2,1,0:T(8,128)(2,1)}), bf16[16,40,384]{2,1,0:T(8,128)(2,1)S(1)}, u32[]{:S(2)}, u32[]{:S(2)}) async-start(bf16[16,40,384]{2,1,0:T(8,128)(2,1)} %broadcast_in_dim.11), calls=%async_computation.4 | async-start | bytes 983040 | tf_op jit(solution)/shard_map/all_to_all | solution.py:179
  124.5 0.5 multiply_bitcast_fusion
  125.1 14.7 %all-to-all-done.4 = bf16[16,40,384]{2,1,0:T(8,128)(2,1)S(1)} async-done(((bf16[16,40,384]{2,1,0:T(8,128)(2,1)}), bf16[16,40,384]{2,1,0:T(8,128)(2,1)S(1)}, u32[]{:S(2)}, u32[]{:S(2)}) %all-to-all-start.4) | async-done | bytes 491552 | tf_op jit(solution)/shard_map/all_to_all | solution.py:179
  139.7 0.7 grad_parts.1
  140.4 1.9 %collective-permute-start.6 = (bf16[2,640,128]{2,1,0:T(8,128)(2,1)S(1)}, bf16[2,640,128]{2,1,0:T(8,128)(2,1)S(1)}, u32[]{:S(2)}, u32[]{:S(2)}) collective-permute-start(bf16[2,640,128]{2,1,0:T(8,128)(2,1)S(1)} %get-tuple-element.19), channel_id=1, source_target_pairs={{0,1},{1,0},{2,3},{3,2},{4,5},{5,4},{6,7},{7,6},{8,9},{9,8},{10,11... | collective-permute-start | bytes 983048 | tf_op jit(solution)/shard_map/ppermute | solution.py:182
  142.3 1.6 collective-permute-done.6
  143.9 0.8 add_convert_fusion
  144.7 4.6 %all-to-all-start.5 = ((bf16[16,80,128]{2,1,0:T(8,128)(2,1)}), bf16[16,80,128]{2,1,0:T(8,128)(2,1)S(1)}, u32[]{:S(2)}, u32[]{:S(2)}) async-start(bf16[16,80,128]{2,1,0:T(8,128)(2,1)} %bitcast.20), calls=%async_computation.5 | async-start | bytes 655360 | tf_op jit(solution)/shard_map/all_to_all | solution.py:176
  149.4 0.6 acc_parts.1
  150.0 0.7 copy-done.4
  150.7 2.0 %collective-permute-start.7 = (f32[2,128,384]{2,1,0:T(8,128)S(1)}, f32[2,128,384]{2,1,0:T(8,128)S(1)}, u32[]{:S(2)}, u32[]{:S(2)}) collective-permute-start(f32[2,128,384]{2,1,0:T(8,128)S(1)} %get-tuple-element.22), channel_id=1, source_target_pairs={{0,1},{1,0},{2,3},{3,2},{4,5},{5,4},{6,7},{7,6},{8,9},{9,8},{10,11... | collective-permute-start | bytes 1179656 | tf_op jit(solution)/shard_map/ppermute | solution.py:182
  152.7 2.4 %collective-permute-start.1 = (bf16[640,768]{1,0:T(8,128)(2,1)S(1)}, bf16[640,768]{1,0:T(8,128)(2,1)S(1)}, u32[]{:S(2)}, u32[]{:S(2)}) collective-permute-start(bf16[640,768]{1,0:T(8,128)(2,1)S(1)} %reshape.162.own_ref), channel_id=1, source_target_pairs={{0,1},{1,0},{2,3},{3,2},{4,5},{5,4},{6,7},{7,6},{8,9},{9,8},{10,11... | collective-permute-start | bytes 2949128 | tf_op jit(solution)/shard_map/ppermute | solution.py:182
  155.2 0.8 pad_maximum_fusion.2
  155.9 3.8 %collective-permute-start.8 = (f32[2,128,384]{2,1,0:T(8,128)}, f32[2,128,384]{2,1,0:T(8,128)S(1)}, u32[]{:S(2)}, u32[]{:S(2)}) collective-permute-start(f32[2,128,384]{2,1,0:T(8,128)} %pad_maximum_fusion.2), channel_id=1, source_target_pairs={{0,2},{1,3},{2,0},{3,1},{4,6},{5,7},{6,4},{7,5},{8,10},{9,11},{10,... | collective-permute-start | bytes 1179656 | tf_op jit(solution)/shard_map/ppermute | solution.py:182
  159.8 5.0 %all-to-all-done.5 = bf16[16,80,128]{2,1,0:T(8,128)(2,1)S(1)} async-done(((bf16[16,80,128]{2,1,0:T(8,128)(2,1)}), bf16[16,80,128]{2,1,0:T(8,128)(2,1)S(1)}, u32[]{:S(2)}, u32[]{:S(2)}) %all-to-all-start.5) | async-done | bytes 327712 | tf_op jit(solution)/shard_map/all_to_all | solution.py:176
  164.8 0.7 broadcast_in_dim.12
  165.5 4.1 %all-to-all-start.6 = ((bf16[8,80,128]{2,1,0:T(8,128)(2,1)}), bf16[8,80,128]{2,1,0:T(8,128)(2,1)S(1)}, u32[]{:S(2)}, u32[]{:S(2)}) async-start(bf16[8,80,128]{2,1,0:T(8,128)(2,1)} %broadcast_in_dim.12), calls=%async_computation.6 | async-start | bytes 327680 | tf_op jit(solution)/shard_map/all_to_all | solution.py:173
  169.7 1.3 collective-permute-done.8.p1.p3
  171.0 1.1 copy-done.2
  172.1 1.1 copy-done.3
  173.3 0.9 copy-done.5
  174.2 2.3 %adam.1 = (f32[1536,128]{1,0:T(8,128)}, f32[1536,128]{1,0:T(8,128)}, f32[1536,128]{1,0:T(8,128)}) custom-call(s32[1]{0:T(128)} %bitcast.23.place_ref, f32[128,384]{1,0:T(8,128)S(1)} %copy-done.5, f32[2,128,384]{2,1,0:T(8,128)S(1)} %collective-permute-done.8.p1.p3, f32[2,128,384]{2,1,0:T(8,128)S(1)} %collective-permute-done.7.p2, ...), custom_call_target="tpu_custom_call" | custom-call | tf_op jit(solution)/shard_map/adam/pallas_call | solution.py:131
  176.5 4.9 %all-to-all-done.6 = bf16[8,80,128]{2,1,0:T(8,128)(2,1)S(1)} async-done(((bf16[8,80,128]{2,1,0:T(8,128)(2,1)}), bf16[8,80,128]{2,1,0:T(8,128)(2,1)S(1)}, u32[]{:S(2)}, u32[]{:S(2)}) %all-to-all-start.6) | async-done | bytes 163872 | tf_op jit(solution)/shard_map/all_to_all | solution.py:173
  181.5 1.3 encoder_grad.1
  (44 shorter events, 1.5 us)
Async XLA Ops:
  0.6 100.7 %copy-start = (f32[1,1536]{1,0:T(1,128)S(1)}, f32[1,1536]{1,0:T(1,128)}, u32[]{:S(2)}) copy-start(f32[1,1536]{1,0:T(1,128)} %param.11) | copy-start | bytes 18436
  2.8 14.5 %copy-start.6 = (bf16[1,1536,128]{2,1,0:T(8,128)(2,1)S(1)}, bf16[1,1536,128]{2,1,0:T(8,128)(2,1)}, u32[]{:S(2)}) copy-start(bf16[1,1536,128]{2,1,0:T(8,128)(2,1)} %param.8) | copy-start | bytes 1179652
  2.8 42.2 %all-to-all-start = ((bf16[64,60,128]{2,1,0:T(8,128)(2,1)}), bf16[64,60,128]{2,1,0:T(8,128)(2,1)S(1)}, u32[]{:S(2)}, u32[]{:S(2)}) async-start(bf16[64,60,128]{2,1,0:T(8,128)(2,1)} %bitcast.2), calls=%async_computation | async-start | bytes 2097152 | tf_op jit(solution)/shard_map/all_to_all | solution.py:206
  17.3 3.3 %collective-permute-start = (bf16[768,128]{1,0:T(8,128)(2,1)S(1)}, bf16[768,128]{1,0:T(8,128)(2,1)S(1)}, u32[]{:S(2)}, u32[]{:S(2)}) collective-permute-start(bf16[768,128]{1,0:T(8,128)(2,1)S(1)} %get-tuple-element.42), channel_id=1, source_target_pairs={{0,1},{1,0},{2,3},{3,2},{4,5},{5,4},{6,7},{7,6},{8,9},{9,8},{10,11... | collective-permute-start | bytes 589832 | tf_op jit(solution)/shard_map/ppermute | solution.py:182
  46.4 3.8 %collective-permute-start.2 = (f32[640,128]{1,0:T(8,128)S(1)}, f32[640,128]{1,0:T(8,128)S(1)}, u32[]{:S(2)}, u32[]{:S(2)}) collective-permute-start(f32[640,128]{1,0:T(8,128)S(1)} %fusion.12), channel_id=1, source_target_pairs={{0,1},{1,0},{2,3},{3,2},{4,5},{5,4},{6,7},{7,6},{8,9},{9,8},{10,11... | collective-permute-start | bytes 983048 | tf_op jit(solution)/shard_map/ppermute | solution.py:182
  49.4 8.6 %copy-start.1 = (bf16[128,1,1536]{2,0,1:T(8,128)(2,1)S(1)}, bf16[128,1,1536]{2,0,1:T(8,128)(2,1)}, u32[]{:S(2)}) copy-start(bf16[128,1,1536]{2,0,1:T(8,128)(2,1)} %param.10) | copy-start | bytes 1179652
  50.9 23.0 %copy-start.7 = (f32[128]{0:T(128)S(1)}, f32[128]{0:T(128)}, u32[]{:S(2)}) copy-start(f32[128]{0:T(128)} %param.9) | copy-start | bytes 1540
  50.9 22.9 %all-to-all-start.1 = ((f32[8,80,128]{2,1,0:T(8,128)}), f32[8,80,128]{2,1,0:T(8,128)S(1)}, u32[]{:S(2)}, u32[]{:S(2)}) async-start(f32[8,80,128]{2,1,0:T(8,128)} %bitcast.5), calls=%async_computation.1 | async-start | bytes 655360 | tf_op jit(solution)/shard_map/all_to_all | solution.py:173
  58.0 20.2 %collective-permute-start.4 = (bf16[128,768]{1,0:T(8,128)(2,1)S(1)}, bf16[128,768]{1,0:T(8,128)(2,1)S(1)}, u32[]{:S(2)}, u32[]{:S(2)}) collective-permute-start(bf16[128,768]{1,0:T(8,128)(2,1)S(1)} %pad_maximum_fusion.4), channel_id=1, source_target_pairs={{0,2},{1,3},{2,0},{3,1},{4,6},{5,7},{6,4},{7,5},{8,10},{9,11},{10,... | collective-permute-start | bytes 589832 | tf_op jit(solution)/shard_map/ppermute | solution.py:182
  74.7 15.5 %all-to-all-start.2 = ((bf16[16,80,128]{2,1,0:T(8,128)(2,1)}), bf16[16,80,128]{2,1,0:T(8,128)(2,1)S(1)}, u32[]{:S(2)}, u32[]{:S(2)}) async-start(bf16[16,80,128]{2,1,0:T(8,128)(2,1)} %broadcast_in_dim.10), calls=%async_computation.2 | async-start | bytes 655360 | tf_op jit(solution)/shard_map/all_to_all | solution.py:176
  78.4 13.7 %collective-permute-start.5 = (bf16[256,384]{1,0:T(8,128)(2,1)S(1)}, bf16[256,384]{1,0:T(8,128)(2,1)S(1)}, u32[]{:S(2)}, u32[]{:S(2)}) collective-permute-start(bf16[256,384]{1,0:T(8,128)(2,1)S(1)} %get-tuple-element.35), channel_id=1, source_target_pairs={{0,1},{1,0},{2,3},{3,2},{4,5},{5,4},{6,7},{7,6},{8,9},{9,8},{10,11... | collective-permute-start | bytes 589832 | tf_op jit(solution)/shard_map/ppermute | solution.py:182
  90.2 3.5 %collective-permute-start.3 = (bf16[2,640,128]{2,1,0:T(8,128)(2,1)S(1)}, bf16[2,640,128]{2,1,0:T(8,128)(2,1)S(1)}, u32[]{:S(2)}, u32[]{:S(2)}) collective-permute-start(bf16[2,640,128]{2,1,0:T(8,128)(2,1)S(1)} %bitcast.49), channel_id=1, source_target_pairs={{0,1},{1,0},{2,3},{3,2},{4,5},{5,4},{6,7},{7,6},{8,9},{9,8},{10,11... | collective-permute-start | bytes 983048 | tf_op jit(solution)/shard_map/ppermute | solution.py:182
  95.0 23.1 %all-to-all-start.3 = ((bf16[16,40,384]{2,1,0:T(8,128)(2,1)}), bf16[16,40,384]{2,1,0:T(8,128)(2,1)S(1)}, u32[]{:S(2)}, u32[]{:S(2)}) async-start(bf16[16,40,384]{2,1,0:T(8,128)(2,1)} %bitcast.16), calls=%async_computation.3 | async-start | bytes 983040 | tf_op jit(solution)/shard_map/all_to_all | solution.py:179
  119.1 20.6 %all-to-all-start.4 = ((bf16[16,40,384]{2,1,0:T(8,128)(2,1)}), bf16[16,40,384]{2,1,0:T(8,128)(2,1)S(1)}, u32[]{:S(2)}, u32[]{:S(2)}) async-start(bf16[16,40,384]{2,1,0:T(8,128)(2,1)} %broadcast_in_dim.11), calls=%async_computation.4 | async-start | bytes 983040 | tf_op jit(solution)/shard_map/all_to_all | solution.py:179
  140.4 3.5 %collective-permute-start.6 = (bf16[2,640,128]{2,1,0:T(8,128)(2,1)S(1)}, bf16[2,640,128]{2,1,0:T(8,128)(2,1)S(1)}, u32[]{:S(2)}, u32[]{:S(2)}) collective-permute-start(bf16[2,640,128]{2,1,0:T(8,128)(2,1)S(1)} %get-tuple-element.19), channel_id=1, source_target_pairs={{0,1},{1,0},{2,3},{3,2},{4,5},{5,4},{6,7},{7,6},{8,9},{9,8},{10,11... | collective-permute-start | bytes 983048 | tf_op jit(solution)/shard_map/ppermute | solution.py:182
  144.7 20.0 %all-to-all-start.5 = ((bf16[16,80,128]{2,1,0:T(8,128)(2,1)}), bf16[16,80,128]{2,1,0:T(8,128)(2,1)S(1)}, u32[]{:S(2)}, u32[]{:S(2)}) async-start(bf16[16,80,128]{2,1,0:T(8,128)(2,1)} %bitcast.20), calls=%async_computation.5 | async-start | bytes 655360 | tf_op jit(solution)/shard_map/all_to_all | solution.py:176
  150.0 0.7 copy-start.4
  150.7 14.1 %copy-start.8 = (f32[128]{0:T(128)S(1)}, f32[128]{0:T(128)}, u32[]{:S(2)}) copy-start(f32[128]{0:T(128)} %param.9) | copy-start | bytes 1540
  150.7 18.9 %copy-start.9 = (f32[128,1]{0,1:T(1,128)S(1)}, f32[128,1]{0,1:T(1,128)}, u32[]{:S(2)}) copy-start(f32[128,1]{0,1:T(1,128)} %get-tuple-element.50) | copy-start | bytes 1540
  150.7 4.5 %collective-permute-start.7 = (f32[2,128,384]{2,1,0:T(8,128)S(1)}, f32[2,128,384]{2,1,0:T(8,128)S(1)}, u32[]{:S(2)}, u32[]{:S(2)}) collective-permute-start(f32[2,128,384]{2,1,0:T(8,128)S(1)} %get-tuple-element.22), channel_id=1, source_target_pairs={{0,1},{1,0},{2,3},{3,2},{4,5},{5,4},{6,7},{7,6},{8,9},{9,8},{10,11... | collective-permute-start | bytes 1179656 | tf_op jit(solution)/shard_map/ppermute | solution.py:182
  152.7 23.8 %collective-permute-start.1 = (bf16[640,768]{1,0:T(8,128)(2,1)S(1)}, bf16[640,768]{1,0:T(8,128)(2,1)S(1)}, u32[]{:S(2)}, u32[]{:S(2)}) collective-permute-start(bf16[640,768]{1,0:T(8,128)(2,1)S(1)} %reshape.162.own_ref), channel_id=1, source_target_pairs={{0,1},{1,0},{2,3},{3,2},{4,5},{5,4},{6,7},{7,6},{8,9},{9,8},{10,11... | collective-permute-start | bytes 2949128 | tf_op jit(solution)/shard_map/ppermute | solution.py:182
  155.9 15.1 %collective-permute-start.8 = (f32[2,128,384]{2,1,0:T(8,128)}, f32[2,128,384]{2,1,0:T(8,128)S(1)}, u32[]{:S(2)}, u32[]{:S(2)}) collective-permute-start(f32[2,128,384]{2,1,0:T(8,128)} %pad_maximum_fusion.2), channel_id=1, source_target_pairs={{0,2},{1,3},{2,0},{3,1},{4,6},{5,7},{6,4},{7,5},{8,10},{9,11},{10,... | collective-permute-start | bytes 1179656 | tf_op jit(solution)/shard_map/ppermute | solution.py:182
  165.5 16.0 %all-to-all-start.6 = ((bf16[8,80,128]{2,1,0:T(8,128)(2,1)}), bf16[8,80,128]{2,1,0:T(8,128)(2,1)S(1)}, u32[]{:S(2)}, u32[]{:S(2)}) async-start(bf16[8,80,128]{2,1,0:T(8,128)(2,1)} %broadcast_in_dim.12), calls=%async_computation.6 | async-start | bytes 327680 | tf_op jit(solution)/shard_map/all_to_all | solution.py:173
  171.0 1.1 copy-start.2
  172.1 1.1 copy-start.3
  173.3 0.9 copy-start.5
